TPU v7x, 128 devices: a whole 4x4x4 slice. The times are simulated.
128 devices in a mesh: dp: 32 (over x, z, core), mp: 4 (over y).
Axes of the slice: x: 4, y: 4, z: 4, core: 2. Of those that a mesh axis runs over, the one named last changes fastest.
Arguments:
- tokens: bfloat16 [32, 768, 1536], P('dp'), may hold values from -6 to 6
- lengths: int32 [32], P('dp'), may hold values from 1 to 768, as said below
- buckets: int32 [32], P('dp'), may hold values from 0 to 3, as said below
- out_cotangent: bfloat16 [32, 768, 1536], P('dp'), may hold values from -6 to 6
- gain_attn: bfloat16 [1536], replicated, may hold values from 0.5 to 1.5
- w_query: bfloat16 [1536, 1536], P(None, 'mp'), may hold values from -0.15625 to 0.15625
- w_key: bfloat16 [1536, 1536], P(None, 'mp'), may hold values from -0.15625 to 0.15625
- w_value: bfloat16 [1536, 1536], P(None, 'mp'), may hold values from -0.15625 to 0.15625
- w_outgate: bfloat16 [1536, 1536], P(None, 'mp'), may hold values from -0.15625 to 0.15625
- w_forget: bfloat16 [1536, 24], P(None, 'mp'), may hold values from -0.15625 to 0.15625
- b_forget: bfloat16 [24], P('mp'), may hold values from 1 to 7
- w_out: bfloat16 [1536, 1536], P('mp'), may hold values from -1.5 to 1.5
- gain_mlp: bfloat16 [1536], replicated, may hold values from 0.5 to 1.5
- w_gate: bfloat16 [1536, 4096], P(None, 'mp'), may hold values from -0.15625 to 0.15625
- w_up: bfloat16 [1536, 4096], P(None, 'mp'), may hold values from -0.15625 to 0.15625
- w_down: bfloat16 [4096, 1536], P('mp'), may hold values from -0.09375 to 0.09375
Outputs:
- output: bfloat16 [32, 768, 1536], P('dp')
- input_grad: float32 [32, 768, 1536], P('dp')
- grad_gain_attn: float32 [1536], P('dp')
- grad_query: float32 [1536, 1536], P('dp', 'mp')
- grad_key: float32 [1536, 1536], P('dp', 'mp')
- grad_value: float32 [1536, 1536], P('dp', 'mp')
- grad_outgate: float32 [1536, 1536], P('dp', 'mp')
- grad_forget: float32 [1536, 24], P('dp', 'mp')
- grad_bias: float32 [24], P('mp')
- grad_out: float32 [1536, 1536], P('mp', 'dp')
- grad_gain_mlp: float32 [1536], P('dp')
- grad_gate: float32 [1536, 4096], P('dp', 'mp')
- grad_up: float32 [1536, 4096], P('dp', 'mp')
- grad_down: float32 [4096, 1536], P('mp', 'dp')
- rms: float32 [3, 4], replicated
Inputs may be any that keep to these rules, and one draw needn't show every extreme that they name: `lengths`: A sequence with bucket id b has a length between b * 192 + 1 and (b + 1) * 192; some sequence has length 768. `buckets`: every bucket id occurs in every draw.
All inputs are finite; a program needn't handle non-finite values.
Results may differ from a plain program's by a relative error of at most 0.014.
Values sent between devices are 32-bit elements; how exact they have to be, the bound alone decides.
A program may use at most 256 MiB of HBM per device.

v0:
```python
import math

import jax
import jax.numpy as jnp
from jax import lax
from jax.sharding import PartitionSpec as P

NBUCKET = 4


EPSILON = 1e-06


def sent_together(arrays, axis, dim, along):
    widths = [math.prod(a.shape[along:]) for a in arrays]
    both = jnp.concatenate(
        [a.reshape(*a.shape[:along], w) for a, w in zip(arrays, widths)], axis=along
    )
    filled = lax.psum_scatter(both, axis, scatter_dimension=dim, tiled=True)
    tiles = jnp.split(filled, [sum(widths[:k]) for k in range(1, len(widths))], axis=along)
    return tuple(
        (b.reshape(*filled.shape[:along], *a.shape[along:]) for a, b in zip(arrays, tiles))
    )


def side_by_side(arrays, axis, dim, along):
    both = jnp.concatenate(arrays, axis=along)
    filled, at, done = (lax.psum_scatter(both, axis, scatter_dimension=dim, tiled=True), 0, [])
    for a in arrays:
        done.append(lax.slice_in_dim(filled, at, at + a.shape[along], axis=along))
        at += a.shape[along]
    return tuple(done)


def sent_to_all(array, axis):
    devices = lax.axis_size(axis)
    return lax.all_to_all(
        jnp.broadcast_to(array[None], (devices, *array.shape)), axis, 0, 0, tiled=True
    )


def over_copies(array, axis):
    return sent_to_all(array, axis).sum(axis=0)


def in_one(arrays, axis):
    ends = [0]
    for a in arrays:
        ends.append(ends[-1] + a.size)
    subtotal = over_copies(jnp.concatenate([a.ravel() for a in arrays]), axis)
    return tuple((subtotal[b:e].reshape(a.shape) for a, b, e in zip(arrays, ends, ends[1:])))


def norm_rows(values):
    return values * lax.rsqrt(jnp.mean(values * values, axis=-1, keepdims=True) + EPSILON)


def gain_norm(values, gain_row):
    return norm_rows(values) * gain_row


def swiglu(gate_pre, up_pre):
    return jax.nn.silu(gate_pre) * up_pre


def low_dot(left, right):
    return jnp.dot(left, right, preferred_element_type=jnp.float32)


def back_dot(left, right):
    return lax.dot_general(
        left, right, (((0,), (0,)), ((), ())), preferred_element_type=jnp.float32
    )


def trans_dot(left, right):
    return lax.dot_general(
        left, right, (((1,), (1,)), ((), ())), preferred_element_type=jnp.float32
    )


def per_device(
    tokens,
    lengths,
    buckets,
    out_cotangent,
    gain_attn,
    w_query,
    w_key,
    w_value,
    w_outgate,
    w_forget,
    b_forget,
    w_out,
    gain_mlp,
    w_gate,
    w_up,
    w_down,
):
    inputs = tokens[0].astype(jnp.float32)
    seq_len, model_width = inputs.shape
    head_count = w_forget.shape[1]
    head_dim = w_query.shape[1] // head_count
    score_scale = head_dim ** (-0.5)
    valid_len = lengths[0]
    positions = jnp.arange(seq_len)
    valid_rows = (positions < valid_len).astype(jnp.float32)[:, None]
    allowed = (positions[None, :] <= positions[:, None]) & (positions[None, :] < valid_len)
    normed_in, norm_back_in = jax.vjp(gain_norm, inputs, gain_attn.astype(jnp.float32))
    in_low = normed_in.astype(jnp.bfloat16)
    query_pre = low_dot(in_low, w_query)
    key_pre = low_dot(in_low, w_key)
    value_pre = low_dot(in_low, w_value)
    outgate_pre = low_dot(in_low, w_outgate)
    forget_pre = low_dot(in_low, w_forget) + b_forget.astype(jnp.float32)
    query_norm, query_back = jax.vjp(norm_rows, query_pre.reshape(seq_len, head_count, head_dim))
    key_norm, key_back = jax.vjp(norm_rows, key_pre.reshape(seq_len, head_count, head_dim))
    query_low = query_norm.astype(jnp.bfloat16)
    key_low = key_norm.astype(jnp.bfloat16)
    value_low = value_pre.astype(jnp.bfloat16).reshape(seq_len, head_count, head_dim)
    log_decay = jnp.cumsum(jax.nn.log_sigmoid(forget_pre), axis=0).T

    def masked_scores():
        base_scores = (
            jnp.einsum("ihd,jhd->hij", query_low, key_low, preferred_element_type=jnp.float32)
            * score_scale
        )
        base_scores = base_scores + log_decay[:, :, None] - log_decay[:, None, :]
        return jnp.where(allowed[None], base_scores, -1e30)

    masked = masked_scores()
    row_top = jnp.max(masked, axis=-1, keepdims=True)
    exponent = jnp.exp(masked - row_top)
    row_total = jnp.sum(exponent, axis=-1, keepdims=True)
    attn_probs = exponent / row_total
    log_total = row_top + jnp.log(row_total)
    attended = jnp.einsum(
        "hij,jhd->ihd",
        attn_probs.astype(jnp.bfloat16),
        value_low,
        preferred_element_type=jnp.float32,
    ).reshape(seq_len, head_count * head_dim)
    gate_sig = jax.nn.sigmoid(outgate_pre)
    gated_low = (attended * gate_sig).astype(jnp.bfloat16)
    branch_attn = lax.psum(low_dot(gated_low, w_out), "mp")
    middle = inputs + branch_attn
    normed_mid, norm_back_mid = jax.vjp(gain_norm, middle, gain_mlp.astype(jnp.float32))
    mid_low = normed_mid.astype(jnp.bfloat16)
    gate_pre = low_dot(mid_low, w_gate)
    up_pre = low_dot(mid_low, w_up)
    hidden_f, swiglu_back = jax.vjp(swiglu, gate_pre, up_pre)
    hidden_low = hidden_f.astype(jnp.bfloat16)
    branch_mlp = lax.psum(low_dot(hidden_low, w_down), "mp")
    layer_out = (middle + branch_mlp).astype(jnp.bfloat16)
    bucket_hot = (buckets[0] == jnp.arange(NBUCKET)).astype(jnp.float32)
    square_sums = jnp.stack(
        [
            jnp.sum(valid_rows * inputs * inputs),
            jnp.sum(valid_rows * branch_attn * branch_attn),
            jnp.sum(valid_rows * branch_mlp * branch_mlp),
        ]
    )
    bucket_sums = square_sums[:, None] * bucket_hot[None, :]
    bucket_count = valid_len.astype(jnp.float32) * bucket_hot
    grad_rows = out_cotangent[0].astype(jnp.float32) * valid_rows
    grad_rows_low = grad_rows.astype(jnp.bfloat16)
    grad_w_down = back_dot(hidden_low, grad_rows_low)
    grad_hidden = trans_dot(grad_rows_low, w_down)
    grad_gate_f, grad_up_f = swiglu_back(grad_hidden)
    gate_grad_low = grad_gate_f.astype(jnp.bfloat16)
    up_grad_low = grad_up_f.astype(jnp.bfloat16)
    grad_w_gate = back_dot(mid_low, gate_grad_low)
    grad_w_up = back_dot(mid_low, up_grad_low)
    grad_mid_norm = lax.psum(trans_dot(gate_grad_low, w_gate) + trans_dot(up_grad_low, w_up), "mp")
    grad_middle_part, grad_gain_mlp = norm_back_mid(grad_mid_norm)
    grad_middle = grad_rows + grad_middle_part
    middle_low = grad_middle.astype(jnp.bfloat16)
    grad_w_out = back_dot(gated_low, middle_low)
    grad_gated = trans_dot(middle_low, w_out)
    attended_grad_low = (grad_gated * gate_sig).astype(jnp.bfloat16)
    outgate_grad_low = (grad_gated * attended * gate_sig * (1.0 - gate_sig)).astype(jnp.bfloat16)
    attended_heads = attended_grad_low.reshape(seq_len, head_count, head_dim)
    again_probs = jnp.exp(masked_scores() - log_total)
    grad_probs = jnp.einsum(
        "ihd,jhd->hij", attended_heads, value_low, preferred_element_type=jnp.float32
    )
    row_delta = jnp.sum(again_probs * grad_probs, axis=-1, keepdims=True)
    scores_grad_low = (again_probs * (grad_probs - row_delta)).astype(jnp.bfloat16)
    value_grad_low = (
        jnp.einsum(
            "hij,ihd->jhd",
            again_probs.astype(jnp.bfloat16),
            attended_heads,
            preferred_element_type=jnp.float32,
        )
        .reshape(seq_len, head_count * head_dim)
        .astype(jnp.bfloat16)
    )
    grad_query_norm = (
        jnp.einsum("hij,jhd->ihd", scores_grad_low, key_low, preferred_element_type=jnp.float32)
        * score_scale
    )
    grad_key_norm = (
        jnp.einsum("hij,ihd->jhd", scores_grad_low, query_low, preferred_element_type=jnp.float32)
        * score_scale
    )
    score_grad = scores_grad_low.astype(jnp.float32)
    grad_decay = jnp.sum(score_grad, axis=2) - jnp.sum(score_grad, axis=1)
    grad_log_forget = jnp.flip(jnp.cumsum(jnp.flip(grad_decay, 1), axis=1), 1).T
    forget_grad_low = (grad_log_forget * jax.nn.sigmoid(-forget_pre)).astype(jnp.bfloat16)
    query_grad_low = (
        query_back(grad_query_norm)[0].reshape(seq_len, head_count * head_dim).astype(jnp.bfloat16)
    )
    key_grad_low = (
        key_back(grad_key_norm)[0].reshape(seq_len, head_count * head_dim).astype(jnp.bfloat16)
    )
    grad_w_query = back_dot(in_low, query_grad_low)
    grad_w_key = back_dot(in_low, key_grad_low)
    grad_w_value = back_dot(in_low, value_grad_low)
    grad_w_outgate = back_dot(in_low, outgate_grad_low)
    grad_w_forget = back_dot(in_low, forget_grad_low)
    grad_b_forget = jnp.sum(forget_grad_low.astype(jnp.float32), axis=0)
    grad_in_local = (
        trans_dot(query_grad_low, w_query)
        + trans_dot(key_grad_low, w_key)
        + trans_dot(value_grad_low, w_value)
    )
    grad_in_local = (
        grad_in_local
        + trans_dot(outgate_grad_low, w_outgate)
        + trans_dot(forget_grad_low, w_forget)
    )
    grad_in_norm = lax.psum(grad_in_local, "mp")
    grad_in_part, grad_gain_attn = norm_back_in(grad_in_norm)
    input_grad = grad_middle + grad_in_part
    all_shares = (
        *sent_together(
            (grad_gain_attn, grad_w_query, grad_w_key, grad_w_value, grad_w_outgate, grad_w_forget),
            "dp",
            0,
            1,
        ),
        lax.psum_scatter(grad_w_out, "dp", scatter_dimension=1, tiled=True),
        *side_by_side((grad_w_gate, grad_w_up), "dp", 0, 1),
        lax.psum_scatter(grad_w_down, "dp", scatter_dimension=1, tiled=True),
        lax.psum_scatter(grad_gain_mlp, "dp", scatter_dimension=0, tiled=True),
    )
    attn_shares = all_shares[:7]
    mlp_shares = all_shares[7:]
    bucket_total, bucket_rows, bias_sum = in_one((bucket_sums, bucket_count, grad_b_forget), "dp")
    rms = jnp.sqrt(bucket_total / (bucket_rows[None, :] * model_width))
    return (
        layer_out[None],
        input_grad[None],
        attn_shares[0],
        attn_shares[1],
        attn_shares[2],
        attn_shares[3],
        attn_shares[4],
        attn_shares[5],
        bias_sum,
        attn_shares[6],
        mlp_shares[3],
        mlp_shares[0],
        mlp_shares[1],
        mlp_shares[2],
        rms,
    )


def solution(mesh):
    placed = (
        P("dp", None, None),
        P("dp"),
        P("dp"),
        P("dp", None, None),
        P(),
        P(None, "mp"),
        P(None, "mp"),
        P(None, "mp"),
        P(None, "mp"),
        P(None, "mp"),
        P("mp"),
        P("mp", None),
        P(),
        P(None, "mp"),
        P(None, "mp"),
        P("mp", None),
    )
    return jax.shard_map(
        per_device,
        mesh=mesh,
        in_specs=placed,
        out_specs=(
            P("dp", None, None),
            P("dp", None, None),
            P("dp"),
            P("dp", "mp"),
            P("dp", "mp"),
            P("dp", "mp"),
            P("dp", "mp"),
            P("dp", "mp"),
            P("mp"),
            P("mp", "dp"),
            P("dp"),
            P("dp", "mp"),
            P("dp", "mp"),
            P("mp", "dp"),
            P(),
        ),
        check_vma=False,
    )
```

profile of v0, /device:TPU:0, one launch (start us, length us, event | category | flops | bytes accessed | tf_op | source)
XLA Modules:
  0.0 918.8 jit_solution(12748875508411315006)
XLA Ops:
  18.3 4.2 multiply_reduce_fusion.7
  30.5 7.2 fusion.82
  37.6 6.9 fusion
  44.6 6.5 fusion.5
  58.5 103.3 %all-reduce.6.cloned.1.call-done = f32[768,1536]{1,0:T(8,128)} async-done(((f32[768,1536]{1,0:T(8,128)}), f32[768,1536]{1,0:T(8,128)}) %all-reduce.6.cloned.1.call-update) | async-done | bytes 4718608 | tf_op jit(solution)/shard_map/psum | solution.py:145
  161.8 3.8 multiply_reduce_fusion.3
  174.6 4.9 multiply_convert_fusion.2
  182.2 4.4 convolution_add_fusion
  187.1 5.6 fusion.86
  192.7 95.3 %all-reduce.8.cloned.1.call-done = f32[768,1536]{1,0:T(8,128)} async-done(((f32[768,1536]{1,0:T(8,128)}), f32[768,1536]{1,0:T(8,128)}) %all-reduce.8.cloned.1.call-update) | async-done | bytes 4718608 | tf_op jit(solution)/shard_map/psum | solution.py:174
  288.0 5.0 multiply_reduce_fusion.1
  293.9 3.7 fusion.19
  303.5 6.5 multiply_reduce_fusion
  310.1 9.8 %convert_reduce_fusion = (f32[6,768]{1,0:T(8,128)S(1)}, f32[6,768]{1,0:T(8,128)S(1)}, bf16[6,768,768]{1,2,0:T(8,128)(2,1)}) fusion(f32[6,768,768]{1,2,0:T(8,128)} %get-tuple-element.151, f32[6,768]{1,0:T(8,128)S(1)} %get-tuple-element.150, f32[6,768,768]{1,2,0:T(8,128)S(1)} %bitcast.193, f32[6,768]{1,0:T(8,128)S(1)} %log_add_fusion), kind=kLoop, calls=%fused_computation | loop fusion | flops 24763392 | bytes 35463168 | tf_op jit(solution)/shard_map/reduce_sum | solution.py:208
  319.9 6.3 multiply_reduce_fusion.4
  326.1 5.3 multiply_reduce_fusion.5
  353.4 6.2 fusion.93
  359.6 4.6 fusion.94
  364.2 10.5 %pad_maximum_fusion = f32[1536,2048]{0,1:T(8,128)} fusion(f32[1536,1024]{0,1:T(8,128)} %fusion.94, f32[1536,1024]{0,1:T(8,128)} %fusion.93), kind=kLoop, calls=%fused_computation.8 | loop fusion | flops 3145728 | bytes 25165824 | tf_op jit(solution)/shard_map/concatenate | solution.py:27
  374.7 12.7 %copy.111 = f32[1536,2048]{1,0:T(8,128)} copy(f32[1536,2048]{0,1:T(8,128)} %pad_maximum_fusion) | data formatting | bytes 25165824
  401.1 128.1 %all-reduce.10.cloned.1.call-done = (f32[768,1536]{1,0:T(8,128)}, f32[768,1536]{1,0:T(8,128)}) async-done(((f32[768,1536]{1,0:T(8,128)}, f32[768,1536]{1,0:T(8,128)}), (f32[768,1536]{1,0:T(8,128)}, f32[768,1536]{1,0:T(8,128)})) %all-reduce.10.cloned.1.call-update) | async-done | bytes 9437200 | tf_op jit(solution)/shard_map/psum | solution.py:153
  529.3 10.4 %fusion.23 = (f32[]{:T(128)}, f32[]{:T(128)}, bf16[1,768,1536]{2,1,0:T(8,128)(2,1)}, f32[]{:T(128)}, f32[768]{0:T(1024)S(1)}, /*index=5*/f32[1536]{0:T(1024)S(1)}) fusion(f32[768,1536]{1,0:T(8,128)} %all-reduce.6.cloned.1.call-done, f32[768]{0:T(1024)S(1)} %fusion.72, f32[768,1536]{1,0:T(8,128)} %get-tuple-element.114, f32[768,1536]{1,0:T(8,128)} %copy-done.2, ...), kind=kLoop, calls=%fused_computation.39 | loop fusion | flops 21231356 | bytes 23614476 | tf_op jit(solution)/shard_map/reduce_sum | solution.py:159
  539.7 34.5 %concatenate.9 = f32[1536,1543]{0,1:T(8,128)} concatenate(f32[1536,1]{0,1:T(1,128)S(1)} %reshape.318, f32[1536,384]{0,1:T(8,128)} %fusion.37, f32[1536,384]{0,1:T(8,128)} %fusion.39, f32[1536,384]{0,1:T(8,128)} %fusion.35, f32[1536,384]{0,1:T(8,128)} %fusion.95, f32[1536,6]{0,1:T(8,128)S(1)} %fusion.92), dimensions={1} | concatenate | bytes 18960384 | tf_op jit(solution)/shard_map/concatenate | solution.py:16
  574.2 10.6 %copy.109 = f32[1536,1543]{1,0:T(8,128)} copy(f32[1536,1543]{0,1:T(8,128)} %concatenate.9) | data formatting | bytes 18960384
  586.0 5.3 fusion.54
  591.4 6.2 fusion.58
  599.5 69.3 %all-reduce = f32[1536]{0:T(1024)S(1)} all-reduce(f32[1536]{0:T(1024)S(1)} %get-tuple-element.105), channel_id=4, replica_groups=mesh['dp'=32,'mp'=4] {'dp'}, use_global_device_ids=true, to_apply=%region_30.31.clone | all-reduce | flops 1536 | bytes 12288
  672.3 3.8 all-to-all-start
  676.2 8.4 fusion.21
  687.8 50.7 %reduce-scatter.13.cloned.1.call-done = f32[48,1543]{1,0:T(8,128)} async-done(((f32[1536,1543]{1,0:T(8,128)}), f32[48,1543]{1,0:T(8,128)}) %reduce-scatter.13.cloned.1.call-update) | async-done | bytes 296272
  743.2 78.4 %reduce-scatter.9.cloned.1.call-done = f32[384,48]{0,1:T(8,128)} async-done(((f32[384,1536]{0,1:T(8,128)}), f32[384,48]{0,1:T(8,128)}) %reduce-scatter.9.cloned.1.call-update) | async-done | bytes 73744 | tf_op jit(solution)/shard_map/reduce_scatter | solution.py:243
  821.5 90.0 %reduce-scatter.11.cloned.1.call-done = f32[1024,48]{0,1:T(8,128)} async-done(((f32[1024,1536]{0,1:T(8,128)}), f32[1024,48]{0,1:T(8,128)}) %reduce-scatter.11.cloned.1.call-update) | async-done | bytes 196624 | tf_op jit(solution)/shard_map/reduce_scatter | solution.py:245
  (215 shorter events, 93.2 us)
Async XLA Ops:
  7.2 167.4 %copy-start = (bf16[1024,1536]{1,0:T(8,128)(2,1)S(1)}, bf16[1024,1536]{1,0:T(8,128)(2,1)}, u32[]{:S(2)}) copy-start(bf16[1024,1536]{1,0:T(8,128)(2,1)} %param.31) | copy-start | bytes 9437188
  7.2 5.9 copy-start.44
  7.2 154.6 %all-reduce.6.cloned.1.call-start = ((), (), s32[]{:S(2)}) async-start(), calls=%async_computation.5 | async-start | bytes 9437184 | tf_op jit(solution)/shard_map/psum | solution.py:145
  7.3 3.8 copy-start.4
  9.6 15.2 %copy-start.45 = (f32[768]{0:T(1024)}, f32[768]{0:T(1024)S(1)}, u32[]{:S(2)}) copy-start(f32[768]{0:T(1024)S(1)} %fusion.70) | copy-start | bytes 9220
  10.3 14.5 %copy-start.42 = (f32[1536]{0:T(1024)}, f32[1536]{0:T(1024)S(1)}, u32[]{:S(2)}) copy-start(f32[1536]{0:T(1024)S(1)} %convert_element_type.141) | copy-start | bytes 18436
  24.9 4.3 copy-start.7
  24.9 4.3 copy-start.36
  30.3 14.2 %copy-start.40 = (bf16[768,384]{0,1:T(8,128)(2,1)}, bf16[768,384]{0,1:T(8,128)(2,1)S(1)}, u32[]{:S(2)}) copy-start(bf16[768,384]{0,1:T(8,128)(2,1)S(1)} %convolution_convert_fusion) | copy-start | bytes 1769476
  44.6 6.5 copy-start.38
  57.9 230.1 %all-reduce.8.cloned.1.call-start = ((), (), s32[]{:S(2)}) async-start(), calls=%async_computation.6 | async-start | bytes 9437184 | tf_op jit(solution)/shard_map/psum | solution.py:174
  186.6 342.6 %all-reduce.10.cloned.1.call-start = ((), (), s32[]{:S(2)}) async-start(), calls=%async_computation.11 | async-start | bytes 18874368 | tf_op jit(solution)/shard_map/psum | solution.py:153
  288.0 5.1 copy-start.10
  288.0 5.9 copy-start.29
  293.8 3.7 copy-start.34
  293.9 3.7 copy-start.35
  293.9 6.4 slice-start
  293.9 7.8 slice-start.1
  293.9 9.0 slice-start.2
  297.6 5.9 slice-start.3
  297.6 5.9 copy-start.41
  310.1 9.8 %copy-start.12 = (f32[768,6,64]{0,2,1:T(8,128)S(1)}, f32[768,6,64]{0,2,1:T(8,128)}, u32[]{:S(2)}) copy-start(f32[768,6,64]{0,2,1:T(8,128)} %get-tuple-element.143) | copy-start | bytes 3538948
  310.1 9.8 %copy-start.14 = (f32[768,6,64]{0,2,1:T(8,128)S(1)}, f32[768,6,64]{0,2,1:T(8,128)}, u32[]{:S(2)}) copy-start(f32[768,6,64]{0,2,1:T(8,128)} %copy-done.13) | copy-start | bytes 3538948
  351.7 334.3 %reduce-scatter.15.cloned.1.call-start = ((), (), s32[]{:S(2)}) async-start(), calls=%async_computation.10 | async-start | bytes 12976128
  353.4 6.2 copy-start.54
  387.4 351.1 %reduce-scatter.13.cloned.1.call-start = ((), (), s32[]{:S(2)}) async-start(), calls=%async_computation.9 | async-start | bytes 10543104
  584.8 6.6 copy-start.30
  584.8 236.7 %reduce-scatter.9.cloned.1.call-start = ((), (), s32[]{:S(2)}) async-start(), calls=%async_computation.7 | async-start | bytes 2433024 | tf_op jit(solution)/shard_map/reduce_scatter | solution.py:243
  591.3 320.2 %reduce-scatter.11.cloned.1.call-start = ((), (), s32[]{:S(2)}) async-start(), calls=%async_computation.8 | async-start | bytes 6488064 | tf_op jit(solution)/shard_map/reduce_scatter | solution.py:245
  597.6 78.6 %copy-start.48 = (f32[768]{0:T(1024)S(1)}, f32[768]{0:T(1024)}, u32[]{:S(2)}) copy-start(f32[768]{0:T(1024)} %copy-done.47) | copy-start | bytes 9220
  672.3 12.3 %all-to-all-start = ((f32[32,1,22]{2,1,0:T(1,128)}), f32[32,1,22]{2,1,0:T(1,128)S(1)}, u32[]{:S(2)}, u32[]{:S(2)}) async-start(f32[32,1,22]{2,1,0:T(1,128)} %broadcast_in_dim.38), calls=%async_computation | async-start | bytes 32768 | tf_op jit(solution)/shard_map/all_to_all | solution.py:37
  676.2 235.4 %copy-start.1 = (bf16[1024,1536]{1,0:T(8,128)(2,1)S(1)}, bf16[1024,1536]{1,0:T(8,128)(2,1)}, u32[]{:S(2)}) copy-start(bf16[1024,1536]{1,0:T(8,128)(2,1)} %param.31) | copy-start | bytes 9437188
  (36 other events, 77.1 us)
Sparse Core Ops, SparseCore 0:
  58.0 103.7 all-reduce.5
  186.7 101.2 all-reduce.7
  351.9 177.3 all-reduce.9
  533.0 104.4 reduce-scatter.14
  641.6 96.8 reduce-scatter.12
  742.9 78.5 reduce-scatter.8
  825.9 85.6 reduce-scatter.10
where the time goes:
time: 930 us; the launch traced here: 919 us
  waiting for transfers between devices  546 us (59%)
  matrix products  119 us (13%)
  local copies, waits for them, and re-layouts  90.5 us (10%)
  other arithmetic  72.1 us (8%)
  blocking collectives  69.3 us (7%)
  between operations  17.2 us (2%)
    psum x1, waiting for transfers between devices, per_device(): branch_mlp = lax.psum(low_dot(hidden_low, w_down), 'mp')  128 us
    psum x1, waiting for transfers between devices, per_device(): branch_attn = lax.psum(low_dot(gated_low, w_out), 'mp')  103 us
    psum x1, waiting for transfers between devices, per_device(): lax.psum(trans_dot(gate_grad_low, w_gate) + trans_dot(up_grad_low, w_up),...  95.3 us
    reduce_scatter x1, waiting for transfers between devices, per_device(): lax.psum_scatter(grad_w_down, 'dp', scatter_dimension=1, tiled=True)  90 us
    reduce_scatter x1, waiting for transfers between devices, per_device(): lax.psum_scatter(grad_w_out, 'dp', scatter_dimension=1, tiled=True)  78.4 us
    unnamed x1, blocking collectives  69.3 us
    unnamed x9, waiting for transfers between devices  50.8 us
    unnamed x130, local copies, waits for them, and re-layouts  48 us
  transfers between devices with their start and end apart: 8, of which 6 were waited for; matrix products, arithmetic and copies ran while one was open for 15% of the time, Pallas kernels for 0%

commit v1 on v0

--- a/solution.py
+++ b/solution.py
@@ -1,35 +1,16 @@
-import math
+import functools
 
 import jax
 import jax.numpy as jnp
 from jax import lax
+from jax.experimental import pallas as pl
+from jax.experimental.pallas import tpu as pltpu
 from jax.sharding import PartitionSpec as P
 
 NBUCKET = 4
 
 
 EPSILON = 1e-06
-
-
-def sent_together(arrays, axis, dim, along):
-    widths = [math.prod(a.shape[along:]) for a in arrays]
-    both = jnp.concatenate(
-        [a.reshape(*a.shape[:along], w) for a, w in zip(arrays, widths)], axis=along
-    )
-    filled = lax.psum_scatter(both, axis, scatter_dimension=dim, tiled=True)
-    tiles = jnp.split(filled, [sum(widths[:k]) for k in range(1, len(widths))], axis=along)
-    return tuple(
-        (b.reshape(*filled.shape[:along], *a.shape[along:]) for a, b in zip(arrays, tiles))
-    )
-
-
-def side_by_side(arrays, axis, dim, along):
-    both = jnp.concatenate(arrays, axis=along)
-    filled, at, done = (lax.psum_scatter(both, axis, scatter_dimension=dim, tiled=True), 0, [])
-    for a in arrays:
-        done.append(lax.slice_in_dim(filled, at, at + a.shape[along], axis=along))
-        at += a.shape[along]
-    return tuple(done)
 
 
 def sent_to_all(array, axis):
@@ -77,6 +58,354 @@
     return lax.dot_general(
         left, right, (((1,), (1,)), ((), ())), preferred_element_type=jnp.float32
     )
+
+MESH = pl.DeviceIdType.MESH
+F32 = jnp.float32
+Y = 4
+STEPS = ("oR", "oL", "iR", "iL", "dR", "dL", "gRa", "gRb", "gLa", "gLb", "fR", "fL")
+
+
+def rows_of(ref, start, count):
+    return ref.at[pl.ds(pl.multiple_of(start, 8), count)]
+
+
+class YReduce:
+    def __init__(self, in_ref, out_ref, opp, nbr, held, ssem, rsem):
+        self.refs = (in_ref, out_ref, opp, nbr, held)
+        self.sems = (ssem, rsem)
+        self.dp, self.me = lax.axis_index("dp"), lax.axis_index("mp")
+        self.right, self.left = lax.rem(self.me + 1, Y), lax.rem(self.me + 3, Y)
+        self.far = lax.rem(self.me + 2, Y)
+        self.quarter = in_ref.shape[0] // Y
+        self.half = self.quarter // 2
+        self.sent = {}
+
+    def neighbours(self):
+        return [(self.dp, self.right), (self.dp, self.left)]
+
+    def send(self, name, src, dst, to):
+        k = STEPS.index(name)
+        copy = pltpu.make_async_remote_copy(
+            src_ref=src,
+            dst_ref=dst,
+            send_sem=self.sems[0].at[k],
+            recv_sem=self.sems[1].at[k],
+            device_id=(self.dp, to),
+            device_id_type=MESH,
+        )
+        copy.start()
+        self.sent[name] = copy
+
+    def start(self):
+        x, _, opp, nbr, _ = self.refs
+        q, h = self.quarter, self.half
+        self.send("oR", rows_of(x, self.far * q, h), opp.at[0], self.right)
+        self.send("oL", rows_of(x, self.far * q + h, h), opp.at[1], self.left)
+        self.send("iR", rows_of(x, self.right * q + h, h), nbr.at[0, h:q], self.right)
+        self.send("iL", rows_of(x, self.left * q, h), nbr.at[1, 0:h], self.left)
+
+    def relay(self):
+        x, _, opp, nbr, held = self.refs
+        q, h = self.quarter, self.half
+        self.sent["oR"].wait_recv()
+        held[0] = rows_of(x, self.right * q, h)[...] + opp[0]
+        self.send("dR", held.at[0], nbr.at[0, 0:h], self.right)
+        self.sent["oL"].wait_recv()
+        held[1] = rows_of(x, self.left * q + h, h)[...] + opp[1]
+        self.send("dL", held.at[1], nbr.at[1, h:q], self.left)
+
+    def spread(self):
+        x, out, _, nbr, _ = self.refs
+        q, h = self.quarter, self.half
+        for part, names, tag in ((0, ("dR", "iL"), "a"), (1, ("iR", "dL"), "b")):
+            for name in names:
+                self.sent[name].wait_recv()
+            at = self.me * q + part * h
+            own = rows_of(out, at, h)
+            own[...] = (
+                rows_of(x, at, h)[...]
+                + nbr[0, part * h : part * h + h]
+                + nbr[1, part * h : part * h + h]
+            )
+            self.send("gR" + tag, own, own, self.right)
+            self.send("gL" + tag, own, own, self.left)
+
+    def forward(self):
+        _, out, _, _, _ = self.refs
+        q, h = self.quarter, self.half
+        self.sent["gRa"].wait_recv()
+        block = rows_of(out, self.left * q, h)
+        self.send("fR", block, block, self.right)
+        self.sent["gLb"].wait_recv()
+        block = rows_of(out, self.right * q + h, h)
+        self.send("fL", block, block, self.left)
+
+    def finish(self):
+        for name in ("gRb", "gLa", "fR", "fL"):
+            self.sent[name].wait_recv()
+        for name in STEPS:
+            self.sent[name].wait_send()
+
+
+def y_scratch(rows, columns):
+    quarter = rows // Y
+    return [
+        pltpu.VMEM((2, quarter // 2, columns), F32),
+        pltpu.VMEM((2, quarter, columns), F32),
+        pltpu.VMEM((2, quarter // 2, columns), F32),
+        pltpu.SemaphoreType.DMA((12,)),
+        pltpu.SemaphoreType.DMA((12,)),
+    ]
+
+
+def y_reduce_kernel(in_ref, out_ref, *scratch):
+    ring = YReduce(in_ref, out_ref, *scratch)
+    meet(ring.neighbours())
+    ring.start()
+    ring.relay()
+    ring.spread()
+    ring.forward()
+    ring.finish()
+
+
+def meet(devices):
+    barrier = pltpu.get_barrier_semaphore()
+    for device in devices:
+        pl.semaphore_signal(barrier, inc=1, device_id=device, device_id_type=MESH)
+    pl.semaphore_wait(barrier, len(devices))
+
+
+def y_reduce(array, call_id):
+    return pl.pallas_call(
+        y_reduce_kernel,
+        out_shape=jax.ShapeDtypeStruct(array.shape, F32),
+        in_specs=[pl.BlockSpec(memory_space=pltpu.VMEM)],
+        out_specs=pl.BlockSpec(memory_space=pltpu.VMEM),
+        scratch_shapes=y_scratch(*array.shape),
+        compiler_params=pltpu.CompilerParams(
+            collective_id=call_id, has_side_effects=True, vmem_limit_bytes=20 << 20
+        ),
+    )(array)
+
+
+class ScatterSum:
+    def __init__(self, ins, pieces, own, other, near, last, psem, lsem, ssem, rsem):
+        self.ins, self.pieces = ins, pieces
+        self.own, self.other, self.near, self.last = own, other, near, last
+        self.psem, self.lsem, self.ssem, self.rsem = psem, lsem, ssem, rsem
+        dp, self.my = lax.axis_index("dp"), lax.axis_index("mp")
+        c, z, x = lax.rem(dp, 2), lax.rem(dp // 2, 4), dp // 8
+        self.c, self.sib = c, dp + 1 - 2 * c
+        self.st1, self.st2 = 4 - 3 * c, 1 + 3 * c
+        self.p1, self.p2 = x + c * (z - x), z + c * (x - z)
+        step = lambda p, by: lax.rem(p + by, 4)
+        self.r1, self.l1, self.o1 = (step(self.p1, by) for by in (1, 3, 2))
+        self.r2, self.l2, self.o2 = (step(self.p2, by) for by in (1, 3, 2))
+        device = lambda a, b: (a * self.st1 + b * self.st2) * 2 + c
+        self.to = (
+            (device(self.r1, self.p2), device(self.l1, self.p2)),
+            (device(self.p1, self.r2), device(self.p1, self.l2)),
+        )
+        self.sent = {}
+
+    def neighbours(self):
+        return [(n, self.my) for n in (self.sib, *self.to[0], *self.to[1])]
+
+    def send(self, name, k, stage, src, dst):
+        at = (k * 2 + stage) * 6 + STEPS.index(name)
+        copy = pltpu.make_async_remote_copy(
+            src_ref=src,
+            dst_ref=dst,
+            send_sem=self.ssem.at[at],
+            recv_sem=self.rsem.at[at],
+            device_id=(self.to[stage][0 if name[1] == "R" else 1], self.my),
+            device_id_type=MESH,
+        )
+        copy.start()
+        self.sent[name, k, stage] = copy
+
+    def source(self, k, block):
+        which, start, width = self.pieces[k]
+        rows = pl.ds(pl.multiple_of(block * 48, 16), 48)
+        return self.ins[which].at[rows, pl.ds(start, width)]
+
+    def whole(self, k):
+        return pltpu.make_async_remote_copy(
+            src_ref=self.own[k],
+            dst_ref=self.other[k],
+            send_sem=self.psem.at[0, k],
+            recv_sem=self.psem.at[1, k],
+            device_id=(self.sib, self.my),
+            device_id_type=MESH,
+        )
+
+    def exchange(self, k):
+        def cross(i, carry):
+            a, b = i // 4, lax.rem(i, 4)
+            pltpu.make_async_remote_copy(
+                src_ref=self.source(k, (a * self.st2 + b * self.st1) * 2 + 1 - self.c),
+                dst_ref=self.other[k].at[a, b],
+                send_sem=self.psem.at[0, k],
+                recv_sem=self.psem.at[1, k],
+                device_id=(self.sib, self.my),
+                device_id_type=MESH,
+            ).start()
+            return carry
+
+        def load(i, carry):
+            a, b = i // 4, lax.rem(i, 4)
+            pltpu.make_async_copy(
+                self.source(k, (a * self.st1 + b * self.st2) * 2 + self.c),
+                self.own[k].at[a, b],
+                self.lsem.at[k],
+            ).start()
+            return carry
+
+        lax.fori_loop(0, 16, cross, 0)
+        lax.fori_loop(0, 16, load, 0)
+
+    def first(self, k):
+        own, other, near = self.own[k], self.other[k], self.near[k]
+        pltpu.make_async_copy(own, own, self.lsem.at[k]).wait()
+        self.whole(k).wait_recv()
+
+        def add(p):
+            def body(b, carry):
+                own[p, b] = own[p, b] + other[p, b]
+                return carry
+
+            lax.fori_loop(0, 4, body, 0)
+
+        add(self.o1)
+        self.send("oR", k, 0, own.at[self.o1, 0:2], near.at[0])
+        self.send("oL", k, 0, own.at[self.o1, 2:4], near.at[1])
+        add(self.r1)
+        self.send("iR", k, 0, own.at[self.r1, 2:4], near.at[3])
+        add(self.l1)
+        self.send("iL", k, 0, own.at[self.l1, 0:2], near.at[4])
+        add(self.p1)
+
+    def first_relay(self, k):
+        own, near = self.own[k], self.near[k]
+
+        def add(p, at, slot):
+            def body(b, carry):
+                own[p, at + b] = own[p, at + b] + near[slot, b]
+                return carry
+
+            lax.fori_loop(0, 2, body, 0)
+
+        self.sent["oR", k, 0].wait_recv()
+        add(self.r1, 0, 0)
+        self.send("dR", k, 0, own.at[self.r1, 0:2], near.at[2])
+        self.sent["oL", k, 0].wait_recv()
+        add(self.l1, 2, 1)
+        self.send("dL", k, 0, own.at[self.l1, 2:4], near.at[5])
+
+    def second(self, k):
+        own, near, last = self.own[k], self.near[k], self.last[k]
+        for name in ("iR", "dR", "iL", "dL"):
+            self.sent[name, k, 0].wait_recv()
+
+        def add(p):
+            h, b = p // 2, lax.rem(p, 2)
+            own[self.p1, p] = own[self.p1, p] + near[2 + h, b] + near[4 + h, b]
+
+        mine = own.at[self.p1]
+        add(self.o2)
+        self.send("oR", k, 1, mine.at[self.o2, 0:24], last.at[0])
+        self.send("oL", k, 1, mine.at[self.o2, 24:48], last.at[1])
+        add(self.r2)
+        self.send("iR", k, 1, mine.at[self.r2, 24:48], last.at[3])
+        add(self.l2)
+        self.send("iL", k, 1, mine.at[self.l2, 0:24], last.at[4])
+        add(self.p2)
+
+    def second_relay(self, k):
+        own, last = self.own[k], self.last[k]
+        self.sent["oR", k, 1].wait_recv()
+        own[self.p1, self.r2, 0:24] = own[self.p1, self.r2, 0:24] + last[0]
+        self.send("dR", k, 1, own.at[self.p1, self.r2, 0:24], last.at[2])
+        self.sent["oL", k, 1].wait_recv()
+        own[self.p1, self.l2, 24:48] = own[self.p1, self.l2, 24:48] + last[1]
+        self.send("dL", k, 1, own.at[self.p1, self.l2, 24:48], last.at[5])
+
+    def result(self, k, outs):
+        own, last = self.own[k], self.last[k]
+        which, start, width = self.pieces[k]
+        for name in ("iR", "dR", "iL", "dL"):
+            self.sent[name, k, 1].wait_recv()
+        columns = pl.ds(start, width)
+        outs[which][0:24, columns] = own[self.p1, self.p2, 0:24] + last[2] + last[4]
+        outs[which][24:48, columns] = own[self.p1, self.p2, 24:48] + last[3] + last[5]
+
+    def finish(self):
+        for k in range(len(self.pieces)):
+            self.whole(k).wait_send()
+            for stage in (0, 1):
+                for name in STEPS[:6]:
+                    self.sent[name, k, stage].wait_send()
+
+
+def both_kernel(pieces, count, x_ref, *refs):
+    ins, out_ref, outs = refs[:count], refs[count], refs[count + 1 : 2 * count + 1]
+    scratch, n = refs[2 * count + 1 :], len(pieces)
+    ring = YReduce(x_ref, out_ref, *scratch[:5])
+    rest = scratch[5:]
+    total = ScatterSum(
+        ins, pieces, *(rest[j * n : j * n + n] for j in range(4)), *rest[4 * n :]
+    )
+    meet(ring.neighbours() + total.neighbours())
+    ring.start()
+    for k in range(n):
+        total.exchange(k)
+    early = (n + 1) // 2
+    for k in range(n):
+        if k == early:
+            ring.relay()
+        total.first(k)
+    for k in range(n):
+        total.first_relay(k)
+    ring.spread()
+    for k in range(n):
+        total.second(k)
+    for k in range(n):
+        total.second_relay(k)
+    for k in range(n):
+        total.result(k, outs)
+    ring.forward()
+    ring.finish()
+    total.finish()
+
+
+def reduce_both(partial, grads, step, call_id, limit):
+    pieces = []
+    for which, g in enumerate(grads):
+        for start in range(0, g.shape[1], step):
+            pieces.append((which, start, min(step, g.shape[1] - start)))
+    n, count = len(pieces), len(grads)
+    hbm, vmem = pl.BlockSpec(memory_space=pl.ANY), pl.BlockSpec(memory_space=pltpu.VMEM)
+    widths = [w for _, _, w in pieces]
+    return pl.pallas_call(
+        functools.partial(both_kernel, pieces, count),
+        out_shape=[jax.ShapeDtypeStruct(partial.shape, F32)]
+        + [jax.ShapeDtypeStruct((48, g.shape[1]), F32) for g in grads],
+        in_specs=[vmem] + [hbm] * count,
+        out_specs=[vmem] * (count + 1),
+        scratch_shapes=y_scratch(*partial.shape)
+        + [pltpu.VMEM((4, 4, 48, w), F32) for w in widths] * 2
+        + [pltpu.VMEM((6, 2, 48, w), F32) for w in widths]
+        + [pltpu.VMEM((6, 24, w), F32) for w in widths]
+        + [
+            pltpu.SemaphoreType.DMA((2, n)),
+            pltpu.SemaphoreType.DMA((n,)),
+            pltpu.SemaphoreType.DMA((12 * n,)),
+            pltpu.SemaphoreType.DMA((12 * n,)),
+        ],
+        compiler_params=pltpu.CompilerParams(
+            collective_id=call_id, has_side_effects=True, vmem_limit_bytes=limit << 20
+        ),
+    )(partial, *grads)
 
 
 def per_device(
@@ -142,7 +471,7 @@
     ).reshape(seq_len, head_count * head_dim)
     gate_sig = jax.nn.sigmoid(outgate_pre)
     gated_low = (attended * gate_sig).astype(jnp.bfloat16)
-    branch_attn = lax.psum(low_dot(gated_low, w_out), "mp")
+    branch_attn = y_reduce(low_dot(gated_low, w_out), 0)
     middle = inputs + branch_attn
     normed_mid, norm_back_mid = jax.vjp(gain_norm, middle, gain_mlp.astype(jnp.float32))
     mid_low = normed_mid.astype(jnp.bfloat16)
@@ -164,18 +493,21 @@
     bucket_count = valid_len.astype(jnp.float32) * bucket_hot
     grad_rows = out_cotangent[0].astype(jnp.float32) * valid_rows
     grad_rows_low = grad_rows.astype(jnp.bfloat16)
-    grad_w_down = back_dot(hidden_low, grad_rows_low)
+    grad_w_down = back_dot(grad_rows_low, hidden_low)
     grad_hidden = trans_dot(grad_rows_low, w_down)
     grad_gate_f, grad_up_f = swiglu_back(grad_hidden)
     gate_grad_low = grad_gate_f.astype(jnp.bfloat16)
     up_grad_low = grad_up_f.astype(jnp.bfloat16)
     grad_w_gate = back_dot(mid_low, gate_grad_low)
     grad_w_up = back_dot(mid_low, up_grad_low)
-    grad_mid_norm = lax.psum(trans_dot(gate_grad_low, w_gate) + trans_dot(up_grad_low, w_up), "mp")
+    grad_mid_local = trans_dot(gate_grad_low, w_gate) + trans_dot(up_grad_low, w_up)
+    grad_mid_norm, down_share, gate_share, up_share = reduce_both(
+        grad_mid_local, [grad_w_down, grad_w_gate, grad_w_up], 512, 1, 48
+    )
     grad_middle_part, grad_gain_mlp = norm_back_mid(grad_mid_norm)
     grad_middle = grad_rows + grad_middle_part
     middle_low = grad_middle.astype(jnp.bfloat16)
-    grad_w_out = back_dot(gated_low, middle_low)
+    grad_w_out = back_dot(middle_low, gated_low)
     grad_gated = trans_dot(middle_low, w_out)
     attended_grad_low = (grad_gated * gate_sig).astype(jnp.bfloat16)
     outgate_grad_low = (grad_gated * attended * gate_sig * (1.0 - gate_sig)).astype(jnp.bfloat16)
@@ -230,40 +562,46 @@
         + trans_dot(outgate_grad_low, w_outgate)
         + trans_dot(forget_grad_low, w_forget)
     )
-    grad_in_norm = lax.psum(grad_in_local, "mp")
-    grad_in_part, grad_gain_attn = norm_back_in(grad_in_norm)
+    rms_in = norm_rows(inputs)
+    gain_local = jnp.sum(grad_in_local * rms_in, axis=0)
+    small = jnp.concatenate(
+        [
+            grad_w_forget,
+            grad_gain_mlp[:, None] * (1.0 / Y),
+            gain_local[:, None],
+            jnp.zeros((model_width, 120), F32),
+        ],
+        axis=1,
+    )
+    grad_in_norm, query_share, key_share, value_share, outgate_share, out_share, small_share = (
+        reduce_both(
+            grad_in_local,
+            [grad_w_query, grad_w_key, grad_w_value, grad_w_outgate, grad_w_out, small],
+            512,
+            2,
+            40,
+        )
+    )
+    gains = lax.psum(small_share[:, 6:8], "mp")
+    grad_in_part, _ = norm_back_in(grad_in_norm)
     input_grad = grad_middle + grad_in_part
-    all_shares = (
-        *sent_together(
-            (grad_gain_attn, grad_w_query, grad_w_key, grad_w_value, grad_w_outgate, grad_w_forget),
-            "dp",
-            0,
-            1,
-        ),
-        lax.psum_scatter(grad_w_out, "dp", scatter_dimension=1, tiled=True),
-        *side_by_side((grad_w_gate, grad_w_up), "dp", 0, 1),
-        lax.psum_scatter(grad_w_down, "dp", scatter_dimension=1, tiled=True),
-        lax.psum_scatter(grad_gain_mlp, "dp", scatter_dimension=0, tiled=True),
-    )
-    attn_shares = all_shares[:7]
-    mlp_shares = all_shares[7:]
     bucket_total, bucket_rows, bias_sum = in_one((bucket_sums, bucket_count, grad_b_forget), "dp")
     rms = jnp.sqrt(bucket_total / (bucket_rows[None, :] * model_width))
     return (
         layer_out[None],
         input_grad[None],
-        attn_shares[0],
-        attn_shares[1],
-        attn_shares[2],
-        attn_shares[3],
-        attn_shares[4],
-        attn_shares[5],
+        gains[:, 1],
+        query_share,
+        key_share,
+        value_share,
+        outgate_share,
+        small_share[:, :6],
         bias_sum,
-        attn_shares[6],
-        mlp_shares[3],
-        mlp_shares[0],
-        mlp_shares[1],
-        mlp_shares[2],
+        out_share.T,
+        gains[:, 0],
+        gate_share,
+        up_share,
+        down_share.T,
         rms,
     )
 

time: 930 us -> 581 us (0.62)
  waiting for transfers between devices: 546 us -> 0.02 us
  Pallas kernels: 0 us -> 302 us
  blocking collectives: 69.3 us -> 17.6 us
  local copies, waits for them, and re-layouts: 90.5 us -> 42.4 us
  other arithmetic: 72.1 us -> 58.2 us
    pallas_call x0 -> x3, Pallas kernels: none -> 302 us  [the longest x2 221 us: reduce_both(): pl.pallas_call(functools.partial(both_kernel, pieces, count), out_shape=[...]
    psum x2 -> x0, waiting for transfers between devices: 199 us -> none  [the longest x1 103 us: per_device(): branch_attn = lax.psum(low_dot(gated_low, w_out), 'mp')]
    reduce_scatter x2 -> x0, waiting for transfers between devices: 168 us -> none  [the longest x1 90 us: per_device(): lax.psum_scatter(grad_w_down, 'dp', scatter_dimension=1, tiled=True)]
    psum x1, waiting for transfers between devices: 128 us -> 0.01 us  [per_device(): branch_mlp = lax.psum(low_dot(hidden_low, w_down), 'mp')]
    unnamed x1 -> x0, blocking collectives: 69.3 us -> none
    unnamed x9 -> x1, waiting for transfers between devices: 50.8 us -> 0.02 us
    concatenate x1, local copies, waits for them, and re-layouts: 34.5 us -> 0.08 us  [per_device(): jnp.concatenate([grad_w_forget, grad_gain_mlp[:, None] * (1.0 / Y), gain_...]
    psum x0 -> x1, blocking collectives: none -> 17.6 us  [per_device(): gains = lax.psum(small_share[:, 6:8], 'mp')]
  transfers between devices with their start and end apart: 8 -> 2, of which waited for: 6 -> 0; matrix products, arithmetic and copies ran while one was open for 15% -> 21% of each run, Pallas kernels for 0% -> 39%
where the time goes in v1:
time: 581 us; the launch traced here: 573 us
  Pallas kernels  302 us (52%)
  matrix products  128 us (22%)
  other arithmetic  58.2 us (10%)
  local copies, waits for them, and re-layouts  42.4 us (7%)
  blocking collectives  17.6 us (3%)
  between operations  16.7 us (3%)
  starting transfers between devices  7.79 us (1%)
    pallas_call x2, Pallas kernels, reduce_both(): pl.pallas_call(functools.partial(both_kernel, pieces, count), out_shape=[...  221 us
    pallas_call x1, Pallas kernels, y_reduce(): pl.pallas_call(y_reduce_kernel, out_shape=jax.ShapeDtypeStruct(array.shap...  81.6 us
    dot_general x9, matrix products, back_dot(): lax.dot_general(left, right, (((0,), (0,)), ((), ())), preferred_element_...  41.8 us
    unnamed x203, local copies, waits for them, and re-layouts  34.3 us
    dot_general x9, matrix products, trans_dot(): lax.dot_general(left, right, (((1,), (1,)), ((), ())), preferred_element_...  24.1 us
    dot_general x9, matrix products, low_dot(): return jnp.dot(left, right, preferred_element_type=jnp.float32)  23.3 us
    psum x1, blocking collectives, per_device(): gains = lax.psum(small_share[:, 6:8], 'mp')  17.6 us
    dot_general x1, matrix products, per_device(): jnp.einsum('ihd,jhd->hij', attended_heads, value_low, preferred_element_t...  12.8 us
  transfers between devices with their start and end apart: 2, of which 0 were waited for; matrix products, arithmetic and copies ran while one was open for 21% of the time, Pallas kernels for 39%

profile of v1, /device:TPU:0, one launch (start us, length us, event | category | flops | bytes accessed | tf_op | source)
XLA Modules:
  0.0 572.7 jit_solution(15128407642077580737)
XLA Ops:
  18.8 4.2 multiply_reduce_fusion.7
  23.0 2.4 copy.71
  25.4 3.3 multiply_reduce_fusion.6
  31.1 7.2 %fusion.80 = (f32[6,768]{1,0:T(8,128)S(1)}, f32[6,768,768]{1,2,0:T(8,128)}) fusion(f32[6,768]{1,0:T(8,128)S(1)} %bitcast.214, f32[768,6,64]{0,2,1:T(8,128)S(1)} %get-tuple-element.142, f32[768,6]{0,1:T(8,128)S(1)} %get-tuple-element.156, f32[768,6,64]{0,2,1:T(8,128)S(1)} %copy-done.25, f32[768,6]{0,1:T(8,128)S(1)} %get-tuple-element.155, ...), kind=kOutput, calls=%fused_computation.146 | convolution fusion | flops 471854592 | bytes 17178624 | tf_op jit(solution)/shard_map/ihd,jhd->hij/dot_general | solution.py:454
  38.2 6.9 %fusion = f32[6,768]{1,0:T(8,128)S(1)} fusion(f32[6,768,768]{1,2,0:T(8,128)} %get-tuple-element.144, f32[6,768]{1,0:T(8,128)S(1)} %get-tuple-element.143), kind=kLoop, calls=%fused_computation.8 | loop fusion | flops 7073280 | bytes 14192640 | tf_op jit(solution)/shard_map/reduce_sum | solution.py:463
  45.2 6.9 %fusion.5 = f32[6,64,768]{2,1,0:T(8,128)S(1)} fusion(bf16[768,6,64]{0,2,1:T(8,128)(2,1)S(1)} %bitcast.211, f32[6,768,768]{1,2,0:T(8,128)} %get-tuple-element.144, f32[6,768]{1,0:T(8,128)S(1)} %fusion, f32[6,768]{1,0:T(8,128)S(1)} %get-tuple-element.143), kind=kOutput, calls=%fused_computation.12 | convolution fusion | flops 463601664 | bytes 15962112 | tf_op jit(solution)/shard_map/hij,jhd->ihd/dot_general | solution.py:466
  55.9 81.6 %shard_map.271 = f32[768,1536]{1,0:T(8,128)S(1)} custom-call(f32[768,1536]{1,0:T(8,128)S(1)} %fusion.81.in_ref), custom_call_target="tpu_custom_call" | custom-call | tf_op jit(solution)/shard_map/pallas_call | solution.py:179
  143.2 2.6 fusion.82
  146.0 2.6 fusion.83
  148.6 5.3 multiply_convert_fusion.2
  155.0 4.4 fusion.84
  161.1 17.2 %fusion.86.refs_1_ = f32[1536,1024]{1,0:T(8,128)} fusion(bf16[768,1536]{1,0:T(8,128)(2,1)S(1)} %copy-done.43, bf16[768,1024]{1,0:T(8,128)(2,1)} %get-tuple-element.128), kind=kOutput, calls=%fused_computation.152 | convolution fusion | flops 2415919104 | bytes 10223616 | tf_op jit(solution)/shard_map/dot_general | solution.py:52
  178.4 2.6 fusion.85
  181.1 4.8 fusion.58.refs_0_
  185.9 4.5 fusion.87.refs_2_
  190.4 4.4 convolution_add_fusion.x_ref
  194.8 131.3 %shard_map.272 = (f32[768,1536]{1,0:T(8,128)S(1)}, f32[48,1024]{1,0:T(8,128)S(1)}, f32[48,1024]{1,0:T(8,128)S(1)}, f32[48,1024]{1,0:T(8,128)S(1)}) custom-call(f32[768,1536]{1,0:T(8,128)} %convolution_add_fusion.x_ref, f32[1536,1024]{1,0:T(8,128)} %fusion.58.refs_0_, f32[1536,1024]{1,0:T(8,128)} %fusion.86.refs_1_, f32[1536,1024]{1,0:T(8,128)} %fusion.87.refs_2_), custom_call_target="tpu_custom_call" | custom-call | tf_op jit(solution)/shard_map/pallas_call | solution.py:389
  332.1 12.8 %multiply_reduce_fusion = (f32[6,768]{1,0:T(8,128)S(1)}, f32[6,768,768]{1,2,0:T(8,128)}) fusion(f32[6,768,768]{1,2,0:T(8,128)} %get-tuple-element.144, f32[6,768]{1,0:T(8,128)S(1)} %log_add_fusion, bf16[768,6,64]{0,2,1:T(8,128)(2,1)S(1)} %bitcast.201, bf16[768,6,64]{0,2,1:T(8,128)(2,1)S(1)} %bitcast.212), kind=kOutput, calls=%fused_computation.3 | convolution fusion | flops 463597056 | bytes 29528064 | tf_op jit(solution)/shard_map/ihd,jhd->hij/dot_general | solution.py:516
  346.1 9.8 %convert_reduce_fusion = (f32[6,768]{1,0:T(8,128)S(1)}, f32[6,768]{1,0:T(8,128)S(1)}, bf16[6,768,768]{1,2,0:T(8,128)(2,1)}) fusion(f32[6,768,768]{1,2,0:T(8,128)} %get-tuple-element.148, f32[6,768]{1,0:T(8,128)S(1)} %get-tuple-element.147, f32[6,768,768]{1,2,0:T(8,128)S(1)} %bitcast.194, f32[6,768]{1,0:T(8,128)S(1)} %log_add_fusion), kind=kLoop, calls=%fused_computation | loop fusion | flops 24763392 | bytes 35463168 | tf_op jit(solution)/shard_map/reduce_sum | solution.py:540
  355.9 7.1 %multiply_reduce_fusion.4 = (f32[768,6]{0,1:T(8,128)}, f32[768,6,64]{0,2,1:T(8,128)}) fusion(f32[768,6,64]{0,2,1:T(8,128)S(1)} %copy-done.29, bf16[6,768,768]{1,2,0:T(8,128)(2,1)} %get-tuple-element.124, f32[768,6,64]{0,2,1:T(8,128)S(1)} %copy-done.26, f32[768,6]{0,1:T(8,128)S(1)} %copy-done.61), kind=kOutput, calls=%fused_computation.87 | convolution fusion | flops 454454784 | bytes 10653696 | tf_op jit(solution)/shard_map/hij,ihd->jhd/dot_general | solution.py:536
  363.0 2.4 multiply_reduce_fusion.5
  376.2 2.8 fusion.92.refs_3_
  381.0 3.1 fusion.39.refs_1_
  388.1 3.1 fusion.37.refs_2_
  397.6 2.9 fusion.54.refs_4_
  400.5 3.4 add_add_fusion.2.x_ref
  403.9 11.0 %fusion.22 = (f32[]{:T(128)}, f32[1536]{0:T(1024)S(1)}, f32[]{:T(128)}, f32[]{:T(128)}, bf16[1,768,1536]{2,1,0:T(8,128)(2,1)}) fusion(bf16[1,768,1536]{2,1,0:T(8,128)(2,1)} %param.16, f32[768]{0:T(1024)S(1)} %copy-done.72, f32[768,1536]{1,0:T(8,128)} %add_add_fusion.2.x_ref, f32[768]{0:T(1024)S(1)} %copy-done.63, f32[768,1536]{1,0:T(8,128)} %copy-done.2, ...), kind=kLoop, calls=%fused_computation.37 | loop fusion | flops 17693180 | bytes 23605260 | tf_op jit(solution)/shard_map/reduce_sum | solution.py:487
  417.8 7.7 %all-to-all-start = ((f32[32,1,22]{2,1,0:T(1,128)}), f32[32,1,22]{2,1,0:T(1,128)}, u32[]{:S(2)}, u32[]{:S(2)}) async-start(f32[32,1,22]{2,1,0:T(1,128)} %broadcast_in_dim.44), calls=%async_computation | async-start | bytes 32768 | tf_op jit(solution)/shard_map/all_to_all | solution.py:18
  432.8 89.3 %shard_map.273 = (f32[768,1536]{1,0:T(8,128)}, f32[48,384]{1,0:T(8,128)S(1)}, f32[48,384]{1,0:T(8,128)S(1)}, f32[48,384]{1,0:T(8,128)S(1)}, f32[48,384]{1,0:T(8,...) custom-call(f32[768,1536]{1,0:T(8,128)} %add_add_fusion.2.x_ref, f32[1536,384]{1,0:T(8,128)S(1)} %fusion.35.refs_0_, ...), custom_call_target="tpu_custom_call" | custom-call | tf_op jit(solution)/shard_map/pallas_call | solution.py:389
  522.2 3.2 fusion.16
  526.0 5.8 %fusion.21 = f32[1,768,1536]{2,1,0:T(8,128)} fusion(f32[768,1536]{1,0:T(8,128)} %copy-done.20, bf16[1,768,1536]{2,1,0:T(8,128)(2,1)S(1)} %copy-done.19, f32[768,1536]{1,0:T(8,128)S(1)} %copy-done.24, f32[768]{0:T(1024)S(1)} %multiply_multiply_fusion.5, f32[1536]{0:T(1024)S(1)} %convert_element_type.141, f32[768]{0:T(1024)S(1)} %copy-done.63), kind=kLoop, calls=%fused_computation.36 | loop fusion | flops 8257536 | bytes 16527360 | tf_op jit(solution)/shard_map/broadcast_in_dim | solution.py:592
  532.5 17.6 %psum.15 = f32[48,2]{1,0:T(8,128)} all-reduce(f32[48,2]{1,0:T(8,128)} %slice.37), channel_id=1, replica_groups=mesh['dp'=32,'mp'=4] {'mp'}, use_global_device_ids=true, to_apply=%region_20.21 | all-reduce | flops 96 | bytes 768 | tf_op jit(solution)/shard_map/psum | solution.py:585
  (277 shorter events, 81.7 us)
Async XLA Ops:
  7.2 141.4 %copy-start = (bf16[1024,1536]{1,0:T(8,128)(2,1)S(1)}, bf16[1024,1536]{1,0:T(8,128)(2,1)}, u32[]{:S(2)}) copy-start(bf16[1024,1536]{1,0:T(8,128)(2,1)} %param.31) | copy-start | bytes 9437188
  7.2 396.7 %all-reduce.2.cloned.1.call-start = ((), (), s32[]{:S(2)}) async-start(), calls=%async_computation.1 | async-start | bytes 9437184 | tf_op jit(solution)/shard_map/psum | solution.py:482
  9.6 15.8 %copy-start.62 = (f32[768]{0:T(1024)}, f32[768]{0:T(1024)S(1)}, u32[]{:S(2)}) copy-start(f32[768]{0:T(1024)S(1)} %fusion.70) | copy-start | bytes 9220
  23.0 7.9 %copy-start.58 = (f32[768,6]{0,1:T(8,128)}, f32[768,6]{0,1:T(8,128)S(1)}, u32[]{:S(2)}) copy-start(f32[768,6]{0,1:T(8,128)S(1)} %get-tuple-element.139) | copy-start | bytes 55300
  29.5 151.5 %copy-start.70 = (f32[768]{0:T(1024)}, f32[768]{0:T(1024)S(1)}, u32[]{:S(2)}) copy-start(f32[768]{0:T(1024)S(1)} %get-tuple-element.154) | copy-start | bytes 9220
  30.9 14.2 %copy-start.53 = (bf16[768,384]{0,1:T(8,128)(2,1)}, bf16[768,384]{0,1:T(8,128)(2,1)S(1)}, u32[]{:S(2)}) copy-start(bf16[768,384]{0,1:T(8,128)(2,1)S(1)} %convolution_convert_fusion) | copy-start | bytes 1769476
  31.0 7.2 %copy-start.51 = (f32[768,6]{0,1:T(8,128)}, f32[768,6]{0,1:T(8,128)S(1)}, u32[]{:S(2)}) copy-start(f32[768,6]{0,1:T(8,128)S(1)} %get-tuple-element.156) | copy-start | bytes 55300
  31.0 7.2 %copy-start.60 = (f32[768,6]{0,1:T(8,128)}, f32[768,6]{0,1:T(8,128)S(1)}, u32[]{:S(2)}) copy-start(f32[768,6]{0,1:T(8,128)S(1)} %get-tuple-element.155) | copy-start | bytes 55300
  45.2 6.9 %copy-start.49 = (bf16[1536,384]{1,0:T(8,128)(2,1)S(1)}, bf16[1536,384]{1,0:T(8,128)(2,1)}, u32[]{:S(2)}) copy-start(bf16[1536,384]{1,0:T(8,128)(2,1)} %param.24) | copy-start | bytes 3538948
  55.8 81.6 %copy-start.17 = (bf16[1,768,1536]{2,1,0:T(8,128)(2,1)S(1)}, bf16[1,768,1536]{2,1,0:T(8,128)(2,1)}, u32[]{:S(2)}) copy-start(bf16[1,768,1536]{2,1,0:T(8,128)(2,1)} %param.16) | copy-start | bytes 7077892
  161.1 17.2 %copy-start.76 = (bf16[1536,1024]{1,0:T(8,128)(2,1)S(1)}, bf16[1536,1024]{1,0:T(8,128)(2,1)}, u32[]{:S(2)}) copy-start(bf16[1536,1024]{1,0:T(8,128)(2,1)} %param.29) | copy-start | bytes 9437188
  161.1 17.2 %copy-start.82 = (bf16[768,1024]{1,0:T(8,128)(2,1)S(1)}, bf16[768,1024]{1,0:T(8,128)(2,1)}, u32[]{:S(2)}) copy-start(bf16[768,1024]{1,0:T(8,128)(2,1)} %get-tuple-element.128) | copy-start | bytes 4718596
  185.9 140.3 %slice-start.8 = ((s8[4718592]{0:T(1024)(128)(4,1)}), s8[4194304]{0:T(1024)(128)(4,1)S(1)}, s32[]{:S(2)}) async-start(s8[4718592]{0:T(1024)(128)(4,1)} %bitcast.197), calls=%async_computation.10 | async-start | bytes 8388608
  190.4 135.8 %slice-start.9 = ((s8[4718592]{0:T(1024)(128)(4,1)}), s8[524288]{0:T(1024)(128)(4,1)S(1)}, s32[]{:S(2)}) async-start(s8[4718592]{0:T(1024)(128)(4,1)} %bitcast.197), calls=%async_computation.11 | async-start | bytes 1048576
  194.8 131.4 %copy-start.65 = (f32[768]{0:T(1024)S(1)}, f32[768]{0:T(1024)}, u32[]{:S(2)}) copy-start(f32[768]{0:T(1024)} %copy-done.64) | copy-start | bytes 9220
  332.1 12.9 %slice-start = ((s8[14155776]{0:T(1024)(128)(4,1)}), s8[4194304]{0:T(1024)(128)(4,1)S(1)}, s32[]{:S(2)}) async-start(s8[14155776]{0:T(1024)(128)(4,1)} %bitcast.193), calls=%async_computation.2 | async-start | bytes 8388608
  332.1 12.9 %slice-start.1 = ((s8[14155776]{0:T(1024)(128)(4,1)}), s8[4194304]{0:T(1024)(128)(4,1)S(1)}, s32[]{:S(2)}) async-start(s8[14155776]{0:T(1024)(128)(4,1)} %bitcast.193), calls=%async_computation.3 | async-start | bytes 8388608
  332.1 12.9 %slice-start.2 = ((s8[14155776]{0:T(1024)(128)(4,1)}), s8[4194304]{0:T(1024)(128)(4,1)S(1)}, s32[]{:S(2)}) async-start(s8[14155776]{0:T(1024)(128)(4,1)} %bitcast.193), calls=%async_computation.4 | async-start | bytes 8388608
  332.1 14.0 %slice-start.3 = ((s8[14155776]{0:T(1024)(128)(4,1)}), s8[1572864]{0:T(1024)(128)(4,1)S(1)}, s32[]{:S(2)}) async-start(s8[14155776]{0:T(1024)(128)(4,1)} %bitcast.193), calls=%async_computation.5 | async-start | bytes 3145728
  346.1 9.8 %copy-start.26 = (f32[768,6,64]{0,2,1:T(8,128)S(1)}, f32[768,6,64]{0,2,1:T(8,128)}, u32[]{:S(2)}) copy-start(f32[768,6,64]{0,2,1:T(8,128)} %get-tuple-element.140) | copy-start | bytes 3538948
  346.1 9.8 %copy-start.29 = (f32[768,6,64]{0,2,1:T(8,128)S(1)}, f32[768,6,64]{0,2,1:T(8,128)}, u32[]{:S(2)}) copy-start(f32[768,6,64]{0,2,1:T(8,128)} %copy-done.28) | copy-start | bytes 3538948
  346.1 9.8 %copy-start.61 = (f32[768,6]{0,1:T(8,128)S(1)}, f32[768,6]{0,1:T(8,128)}, u32[]{:S(2)}) copy-start(f32[768,6]{0,1:T(8,128)} %copy-done.60) | copy-start | bytes 55300
  355.9 7.1 %copy-start.15 = (bf16[6,768,768]{1,2,0:T(8,128)(2,1)S(1)}, bf16[6,768,768]{1,2,0:T(8,128)(2,1)}, u32[]{:S(2)}) copy-start(bf16[6,768,768]{1,2,0:T(8,128)(2,1)} %get-tuple-element.124) | copy-start | bytes 21233668
  355.9 7.1 %copy-start.52 = (f32[768,6]{0,1:T(8,128)S(1)}, f32[768,6]{0,1:T(8,128)}, u32[]{:S(2)}) copy-start(f32[768,6]{0,1:T(8,128)} %copy-done.51) | copy-start | bytes 55300
  363.0 9.5 %copy-start.57 = (f32[768,6]{0,1:T(8,128)S(1)}, f32[768,6]{0,1:T(8,128)}, u32[]{:S(2)}) copy-start(f32[768,6]{0,1:T(8,128)} %get-tuple-element.138) | copy-start | bytes 55300
  363.0 10.3 %copy-start.23 = (bf16[768,1536]{1,0:T(8,128)(2,1)S(1)}, bf16[768,1536]{1,0:T(8,128)(2,1)}, u32[]{:S(2)}) copy-start(bf16[768,1536]{1,0:T(8,128)(2,1)} %copy-done.21) | copy-start | bytes 7077892
  365.8 9.2 %copy-start.73 = (f32[1536]{0:T(1024)S(1)}, f32[1536]{0:T(1024)}, u32[]{:S(2)}) copy-start(f32[1536]{0:T(1024)} %get-tuple-element.112) | copy-start | bytes 18436
  376.2 9.5 %slice-start.4 = ((s8[14155776]{0:T(1024)(128)(4,1)}), s8[4194304]{0:T(1024)(128)(4,1)S(1)}, s32[]{:S(2)}) async-start(s8[14155776]{0:T(1024)(128)(4,1)} %bitcast.195), calls=%async_computation.6 | async-start | bytes 8388608
  417.8 135.2 %all-to-all-start = ((f32[32,1,22]{2,1,0:T(1,128)}), f32[32,1,22]{2,1,0:T(1,128)}, u32[]{:S(2)}, u32[]{:S(2)}) async-start(f32[32,1,22]{2,1,0:T(1,128)} %broadcast_in_dim.44), calls=%async_computation | async-start | bytes 32768 | tf_op jit(solution)/shard_map/all_to_all | solution.py:18
  432.8 89.3 %copy-start.19 = (bf16[1,768,1536]{2,1,0:T(8,128)(2,1)S(1)}, bf16[1,768,1536]{2,1,0:T(8,128)(2,1)}, u32[]{:S(2)}) copy-start(bf16[1,768,1536]{2,1,0:T(8,128)(2,1)} %param.16) | copy-start | bytes 7077892
  522.1 9.7 %copy-start.8 = (f32[48,128]{1,0:T(8,128)}, f32[48,128]{1,0:T(8,128)S(1)}, u32[]{:S(2)}) copy-start(f32[48,128]{1,0:T(8,128)S(1)} %get-tuple-element.28) | copy-start | bytes 73732
  526.0 39.7 %copy-start.1 = (bf16[1024,1536]{1,0:T(8,128)(2,1)S(1)}, bf16[1024,1536]{1,0:T(8,128)(2,1)}, u32[]{:S(2)}) copy-start(bf16[1024,1536]{1,0:T(8,128)(2,1)} %param.31) | copy-start | bytes 9437188
  (65 other events, 173.2 us)
Sparse Core Ops, SparseCore 0:
  159.6 147.7 all-reduce.1

commit v2 on v1

--- a/solution.py
+++ b/solution.py
@@ -32,32 +32,9 @@
     return tuple((subtotal[b:e].reshape(a.shape) for a, b, e in zip(arrays, ends, ends[1:])))
 
 
-def norm_rows(values):
-    return values * lax.rsqrt(jnp.mean(values * values, axis=-1, keepdims=True) + EPSILON)
-
-
-def gain_norm(values, gain_row):
-    return norm_rows(values) * gain_row
-
-
-def swiglu(gate_pre, up_pre):
-    return jax.nn.silu(gate_pre) * up_pre
-
-
 def low_dot(left, right):
     return jnp.dot(left, right, preferred_element_type=jnp.float32)
 
-
-def back_dot(left, right):
-    return lax.dot_general(
-        left, right, (((0,), (0,)), ((), ())), preferred_element_type=jnp.float32
-    )
-
-
-def trans_dot(left, right):
-    return lax.dot_general(
-        left, right, (((1,), (1,)), ((), ())), preferred_element_type=jnp.float32
-    )
 
 MESH = pl.DeviceIdType.MESH
 F32 = jnp.float32
@@ -114,7 +91,7 @@
         held[1] = rows_of(x, self.left * q + h, h)[...] + opp[1]
         self.send("dL", held.at[1], nbr.at[1, h:q], self.left)
 
-    def spread(self):
+    def spread(self, change=lambda value, part: value):
         x, out, _, nbr, _ = self.refs
         q, h = self.quarter, self.half
         for part, names, tag in ((0, ("dR", "iL"), "a"), (1, ("iR", "dL"), "b")):
@@ -122,10 +99,11 @@
                 self.sent[name].wait_recv()
             at = self.me * q + part * h
             own = rows_of(out, at, h)
-            own[...] = (
+            own[...] = change(
                 rows_of(x, at, h)[...]
                 + nbr[0, part * h : part * h + h]
-                + nbr[1, part * h : part * h + h]
+                + nbr[1, part * h : part * h + h],
+                part,
             )
             self.send("gR" + tag, own, own, self.right)
             self.send("gL" + tag, own, own, self.left)
@@ -330,14 +308,15 @@
         own[self.p1, self.l2, 24:48] = own[self.p1, self.l2, 24:48] + last[1]
         self.send("dL", k, 1, own.at[self.p1, self.l2, 24:48], last.at[5])
 
-    def result(self, k, outs):
+    def result(self, k, out):
         own, last = self.own[k], self.last[k]
-        which, start, width = self.pieces[k]
+        width = self.pieces[k][2]
+        start = sum(piece[2] for piece in self.pieces[:k])
         for name in ("iR", "dR", "iL", "dL"):
             self.sent[name, k, 1].wait_recv()
         columns = pl.ds(start, width)
-        outs[which][0:24, columns] = own[self.p1, self.p2, 0:24] + last[2] + last[4]
-        outs[which][24:48, columns] = own[self.p1, self.p2, 24:48] + last[3] + last[5]
+        out[0:24, columns] = own[self.p1, self.p2, 0:24] + last[2] + last[4]
+        out[24:48, columns] = own[self.p1, self.p2, 24:48] + last[3] + last[5]
 
     def finish(self):
         for k in range(len(self.pieces)):
@@ -347,16 +326,73 @@
                     self.sent[name, k, stage].wait_send()
 
 
-def both_kernel(pieces, count, x_ref, *refs):
-    ins, out_ref, outs = refs[:count], refs[count], refs[count + 1 : 2 * count + 1]
-    scratch, n = refs[2 * count + 1 :], len(pieces)
-    ring = YReduce(x_ref, out_ref, *scratch[:5])
-    rest = scratch[5:]
+class SmallSum:
+    def __init__(self, total, ring, bufs, landed, ssem, rsem):
+        self.bufs, self.landed, self.ssem, self.rsem = bufs, landed, ssem, rsem
+        dp, my = lax.axis_index("dp"), lax.axis_index("mp")
+        device = lambda a, b: ((a * total.st1 + b * total.st2) * 2 + total.c, my)
+        turn = lambda p, by: lax.rem(p + by, 4)
+        self.stages = [
+            [(total.sib, my)],
+            [device(turn(total.p1, by), total.p2) for by in (1, 2, 3)],
+            [device(total.p1, turn(total.p2, by)) for by in (1, 2, 3)],
+            [(dp, turn(my, by)) for by in (1, 2, 3)],
+        ]
+        self.far = [self.stages[1][1], self.stages[2][1], self.stages[3][1]]
+        self.sent = []
+
+    def slot(self, stage, j):
+        return 3 * stage - 2 + j if stage else 0
+
+    def send(self, stage):
+        for j, to in enumerate(self.stages[stage]):
+            at = self.slot(stage, j)
+            copy = pltpu.make_async_remote_copy(
+                src_ref=self.bufs.at[stage],
+                dst_ref=self.landed.at[at],
+                send_sem=self.ssem.at[at],
+                recv_sem=self.rsem.at[at],
+                device_id=to,
+                device_id_type=MESH,
+            )
+            copy.start()
+            self.sent.append(copy)
+
+    def take(self, stage):
+        value = self.bufs[stage]
+        for j in range(len(self.stages[stage])):
+            at = self.slot(stage, j)
+            self.sent[at].wait_recv()
+            value = value + self.landed[at]
+        self.bufs[stage + 1] = value
+
+    def finish(self):
+        for copy in self.sent:
+            copy.wait_send()
+
+
+def both_kernel(pieces, count, small, x_ref, source_ref, base_ref, gain_ref, *refs):
+    if small:
+        other_ref, refs = refs[0], refs[1:]
+    ins, out_ref, share_ref, sums_ref = refs[:count], *refs[count : count + 3]
+    scratch, n = refs[count + 3 :], len(pieces)
+    source_s, base_s, csem = scratch[:3]
+    ring = YReduce(x_ref, out_ref, *scratch[3:8])
+    rest = scratch[8:]
     total = ScatterSum(
-        ins, pieces, *(rest[j * n : j * n + n] for j in range(4)), *rest[4 * n :]
-    )
-    meet(ring.neighbours() + total.neighbours())
+        ins, pieces, *(rest[j * n : j * n + n] for j in range(4)), *rest[4 * n : 4 * n + 4]
+    )
+    peers = ring.neighbours() + total.neighbours()
+    if small:
+        tiny = SmallSum(total, ring, *rest[4 * n + 4 :])
+        peers = peers + tiny.far
+    meet(peers)
     ring.start()
+    loads = []
+    for j, (ref, scr) in enumerate(((source_ref, source_s), (base_ref, base_s))):
+        copy = pltpu.make_async_copy(rows_of(ref, ring.me * ring.quarter, ring.quarter), scr, csem.at[j])
+        copy.start()
+        loads.append(copy)
     for k in range(n):
         total.exchange(k)
     early = (n + 1) // 2
@@ -366,33 +402,85 @@
         total.first(k)
     for k in range(n):
         total.first_relay(k)
-    ring.spread()
+    for copy in loads:
+        copy.wait()
+    parts = []
+
+    def change(value, part):
+        at = slice(part * ring.half, part * ring.half + ring.half)
+        source = source_s[at, :].astype(F32)
+        r = lax.rsqrt(jnp.mean(source * source, axis=1, keepdims=True) + EPSILON)
+        n = source * r
+        e = value * gain_ref[...]
+        parts.append(jnp.sum(value * n, axis=0, keepdims=True))
+        inner = jnp.mean(e * n, axis=1, keepdims=True)
+        return base_s[at, :].astype(F32) + r * (e - n * inner)
+
+    ring.spread(change)
+    if small:
+        tiny.bufs[0, 0:1, :] = parts[0] + parts[1]
+        tiny.bufs[0, 1:2, :] = other_ref[...]
+        tiny.bufs[0, 2:8, :] = jnp.zeros_like(tiny.bufs[0, 2:8, :])
+        tiny.send(0)
+    else:
+        sums_ref[...] = parts[0] + parts[1]
     for k in range(n):
         total.second(k)
+    if small:
+        tiny.take(0)
+        tiny.send(1)
     for k in range(n):
         total.second_relay(k)
+    if small:
+        tiny.take(1)
+        tiny.send(2)
     for k in range(n):
-        total.result(k, outs)
+        total.result(k, share_ref)
+    if small:
+        tiny.take(2)
+        tiny.send(3)
     ring.forward()
+    if small:
+        tiny.take(3)
+        sums_ref[...] = tiny.bufs[4]
+        tiny.finish()
     ring.finish()
     total.finish()
 
 
-def reduce_both(partial, grads, step, call_id, limit):
+def reduce_both(partial, source, base, gain, grads, step, call_id, limit, other=None):
     pieces = []
     for which, g in enumerate(grads):
         for start in range(0, g.shape[1], step):
             pieces.append((which, start, min(step, g.shape[1] - start)))
     n, count = len(pieces), len(grads)
+    small = other is not None
     hbm, vmem = pl.BlockSpec(memory_space=pl.ANY), pl.BlockSpec(memory_space=pltpu.VMEM)
     widths = [w for _, _, w in pieces]
+    rows, columns = partial.shape
+    quarter = (rows // Y, columns)
+    sums = (8, columns) if small else (1, columns)
+    extra = [
+        pltpu.VMEM((5, 8, columns), F32),
+        pltpu.VMEM((10, 8, columns), F32),
+        pltpu.SemaphoreType.DMA((10,)),
+        pltpu.SemaphoreType.DMA((10,)),
+    ]
     return pl.pallas_call(
-        functools.partial(both_kernel, pieces, count),
-        out_shape=[jax.ShapeDtypeStruct(partial.shape, F32)]
-        + [jax.ShapeDtypeStruct((48, g.shape[1]), F32) for g in grads],
-        in_specs=[vmem] + [hbm] * count,
-        out_specs=[vmem] * (count + 1),
-        scratch_shapes=y_scratch(*partial.shape)
+        functools.partial(both_kernel, pieces, count, small),
+        out_shape=[
+            jax.ShapeDtypeStruct(partial.shape, F32),
+            jax.ShapeDtypeStruct((48, sum(widths)), F32),
+            jax.ShapeDtypeStruct(sums, F32),
+        ],
+        in_specs=[vmem, hbm, hbm, vmem] + [vmem] * small + [hbm] * count,
+        out_specs=[vmem] * 3,
+        scratch_shapes=[
+            pltpu.VMEM(quarter, source.dtype),
+            pltpu.VMEM(quarter, base.dtype),
+            pltpu.SemaphoreType.DMA((2,)),
+        ]
+        + y_scratch(*partial.shape)
         + [pltpu.VMEM((4, 4, 48, w), F32) for w in widths] * 2
         + [pltpu.VMEM((6, 2, 48, w), F32) for w in widths]
         + [pltpu.VMEM((6, 24, w), F32) for w in widths]
@@ -401,207 +489,525 @@
             pltpu.SemaphoreType.DMA((n,)),
             pltpu.SemaphoreType.DMA((12 * n,)),
             pltpu.SemaphoreType.DMA((12 * n,)),
-        ],
+        ]
+        + extra * small,
         compiler_params=pltpu.CompilerParams(
             collective_id=call_id, has_side_effects=True, vmem_limit_bytes=limit << 20
         ),
-    )(partial, *grads)
+    )(partial, source, base, gain, *([other] * small), *grads)
+
+
+HEAD = 64
+PAIR = 128
+NEG = -1e30
+
+
+def rows_at(i, size):
+    return pl.ds(pl.multiple_of(i * size, size), size)
+
+
+def lane_is(shape, index):
+    return lax.broadcasted_iota(jnp.int32, shape, len(shape) - 1) == index
+
+
+def first_head(shape):
+    return lax.broadcasted_iota(jnp.int32, shape, len(shape) - 1) < HEAD
+
+
+def halves_mean(values):
+    first = first_head(values.shape)
+    low = jnp.sum(jnp.where(first, values, 0.0), axis=1, keepdims=True) * (1.0 / HEAD)
+    high = jnp.sum(jnp.where(first, 0.0, values), axis=1, keepdims=True) * (1.0 / HEAD)
+    return low, high
+
+
+def one_row(ref, index):
+    rows = ref[...]
+    picked = lax.broadcasted_iota(jnp.int32, rows.shape, 0) == index
+    return jnp.sum(jnp.where(picked, rows, 0.0), axis=0, keepdims=True)
+
+
+def running_sum(values, backward=False):
+    count = values.shape[0]
+    row = lax.broadcasted_iota(jnp.int32, values.shape, 0)
+    shift = 1
+    while shift < count:
+        if backward:
+            moved = jnp.where(row < count - shift, pltpu.roll(values, count - shift, 0), 0.0)
+        else:
+            moved = jnp.where(row >= shift, pltpu.roll(values, shift, 0), 0.0)
+        values = values + moved
+        shift *= 2
+    return values
+
+
+def forward_kernel(
+    length_ref, x_ref, gain_ref, wq_ref, wk_ref, wv_ref, wo_ref, wf_ref, bf_ref,
+    low_ref, qn_ref, kn_ref, v_ref, sig_ref, att_ref, gated_ref, stat_ref, decay_ref,
+    top_s, row_s, q_s, k_s, v_s,
+):
+    step = pl.program_id(0)
+    seq = x_ref.shape[0]
+    length = length_ref[0]
+
+    @pl.when(step == 0)
+    def _():
+        def norm(i, carry):
+            at = rows_at(i, 128)
+            x = x_ref[at, :].astype(F32)
+            r = lax.rsqrt(jnp.mean(x * x, axis=1, keepdims=True) + EPSILON)
+            low_ref[at, :] = (x * r * gain_ref[...]).astype(jnp.bfloat16)
+            return carry
+
+        lax.fori_loop(0, seq // 128, norm, 0)
+        pre = jnp.dot(low_ref[...], wf_ref[...], preferred_element_type=F32) + bf_ref[...]
+        fall = jnp.minimum(pre, 0.0) - jnp.log1p(jnp.exp(-jnp.abs(pre)))
+        decay = running_sum(fall)
+        row = lax.broadcasted_iota(jnp.int32, decay.shape, 0)
+        final = jnp.sum(jnp.where(row == length - 1, decay, 0.0), axis=0, keepdims=True)
+        decay_ref[0] = decay
+        decay_ref[1] = jax.nn.sigmoid(-pre)
+        top_s[...] = jnp.where(row < length, decay, final)
+        row_s[...] = jnp.where(row < length, decay, -NEG).T[0:8]
+
+    def project(i, carry):
+        at = rows_at(i, 256)
+        low = low_ref[at, :]
+        for w, n_ref, s, col in ((wq_ref, qn_ref, q_s, 0), (wk_ref, kn_ref, k_s, 2)):
+            pre = jnp.dot(low, w[...], preferred_element_type=F32)
+            a, b = halves_mean(pre * pre)
+            a, b = lax.rsqrt(a + EPSILON), lax.rsqrt(b + EPSILON)
+            n = pre * jnp.where(first_head(pre.shape), a, b)
+            n_ref[at, :] = n
+            s[at, :] = n.astype(jnp.bfloat16)
+            here = jnp.where(lane_is(pre.shape, col), a, jnp.where(lane_is(pre.shape, col + 1), b, 0.0))
+            stat_ref[at, :] = here if col == 0 else stat_ref[at, :] + here
+        value = jnp.dot(low, wv_ref[...], preferred_element_type=F32).astype(jnp.bfloat16)
+        v_s[at, :] = value
+        v_ref[at, :] = value
+        sig_ref[at, :] = jax.nn.sigmoid(jnp.dot(low, wo_ref[...], preferred_element_type=F32))
+        return carry
+
+    lax.fori_loop(0, seq // 256, project, 0)
+    lines = [one_row(row_s, 2 * step + head) for head in (0, 1)]
+    first = first_head((128, PAIR))
+    zero = jnp.zeros((128, PAIR), jnp.bfloat16)
+    upper = lax.broadcasted_iota(jnp.int32, (128, 128), 1) > lax.broadcasted_iota(
+        jnp.int32, (128, 128), 0
+    )
+    for i in range(seq // 128):
+        at, n = slice(i * 128, i * 128 + 128), i * 128 + 128
+        q = q_s[at, :]
+        both = []
+        for head in (0, 1):
+            own = jnp.where(first, q, zero) if head == 0 else jnp.where(first, zero, q)
+            s = lax.dot_general(
+                own, k_s[0:n, :], (((1,), (1,)), ((), ())), preferred_element_type=F32
+            )
+            column = jnp.sum(
+                jnp.where(lane_is((128, PAIR), 2 * step + head), top_s[at, :], 0.0), axis=1, keepdims=True
+            )
+            line = lines[head][:, 0:n]
+            s = s * (HEAD ** (-0.5)) + (column - line)
+            diagonal = jnp.where(upper, NEG, s[:, n - 128 :])
+            s = diagonal if i == 0 else jnp.concatenate([s[:, : n - 128], diagonal], axis=1)
+            p = jnp.exp(s)
+            p = p * (1.0 / jnp.sum(p, axis=1, keepdims=True))
+            both.append(
+                jnp.dot(p.astype(jnp.bfloat16), v_s[0:n, :], preferred_element_type=F32)
+            )
+        out = jnp.where(first, both[0], both[1])
+        att_ref[at, :] = out
+        gated_ref[at, :] = (out * sig_ref[at, :]).astype(jnp.bfloat16)
+
+
+def whole(shape):
+    return pl.BlockSpec(shape, lambda *_: (0,) * len(shape), pipeline_mode=pl.Buffered(1))
+
+
+def forward_attention(tokens, length, gain, wq, wk, wv, wo, wf, bf):
+    seq, width = tokens.shape
+    heads = wq.shape[1]
+    weights = pl.BlockSpec((width, PAIR), lambda i, _: (0, i))
+    lanes = pl.BlockSpec((seq, PAIR), lambda i, _: (0, i))
+    shape = lambda *s, t=F32: jax.ShapeDtypeStruct(s, t)
+    low = jnp.bfloat16
+    return pl.pallas_call(
+        forward_kernel,
+        grid_spec=pltpu.PrefetchScalarGridSpec(
+            num_scalar_prefetch=1,
+            grid=(heads // PAIR,),
+            in_specs=[whole((seq, width)), whole((1, width))]
+            + [weights] * 4
+            + [whole((width, PAIR)), whole((1, PAIR))],
+            out_specs=[whole((seq, width))] + [lanes] * 7 + [whole((2, seq, PAIR))],
+            scratch_shapes=[
+                pltpu.VMEM((seq, PAIR), F32),
+                pltpu.VMEM((8, seq), F32),
+                pltpu.VMEM((seq, PAIR), low),
+                pltpu.VMEM((seq, PAIR), low),
+                pltpu.VMEM((seq, PAIR), low),
+            ],
+        ),
+        out_shape=[
+            shape(seq, width, t=low), shape(seq, heads), shape(seq, heads), shape(seq, heads, t=low),
+            shape(seq, heads), shape(seq, heads), shape(seq, heads, t=low), shape(seq, heads),
+            shape(2, seq, PAIR),
+        ],
+        compiler_params=pltpu.CompilerParams(vmem_limit_bytes=40 << 20),
+        cost_estimate=pl.CostEstimate(flops=6 * 10**9, bytes_accessed=20 * 10**6, transcendentals=4 * 10**6),
+    )(length, tokens, gain, wq, wk, wv, wo, wf, bf)
+
+
+def mlp_kernel(
+    length_ref, x_ref, branch_ref, cot_ref, gain_ref, wg_ref, wu_ref, wd_ref,
+    mid_ref, grad_ref, out_ref, back_ref, gd_ref, gg_ref, gu_ref, sums_ref,
+    low_s, low_t, grad_t, hid_s, pair_s,
+):
+    step = pl.program_id(0)
+    seq, width = x_ref.shape
+    length = length_ref[0]
+    tile = wg_ref.shape[1]
+
+    @pl.when(step == 0)
+    def _():
+        def norm(i, carry):
+            at = rows_at(i, 128)
+            x, branch = x_ref[at, :].astype(F32), branch_ref[at, :]
+            mid = x + branch
+            r = lax.rsqrt(jnp.mean(mid * mid, axis=1, keepdims=True) + EPSILON)
+            low = (mid * r * gain_ref[...]).astype(jnp.bfloat16)
+            mid_ref[at, :] = mid
+            low_s[at, :] = low
+            low_t[:, at] = low.T
+            valid = lax.broadcasted_iota(jnp.int32, (128, 1), 0) + i * 128 < length
+            grad = jnp.where(valid, cot_ref[at, :].astype(F32), 0.0).astype(jnp.bfloat16)
+            grad_ref[at, :] = grad
+            grad_t[:, at] = grad.T
+            kept = jnp.where(valid, 1.0, 0.0)
+            a = jnp.sum(kept * (x * x), axis=0, keepdims=True)
+            b = jnp.sum(kept * (branch * branch), axis=0, keepdims=True)
+            return carry[0] + a, carry[1] + b
+
+        zero = jnp.zeros((1, width), F32)
+        a, b = lax.fori_loop(0, seq // 128, norm, (zero, zero))
+        sums_ref[0:1, :] = a
+        sums_ref[1:2, :] = b
+
+    def hidden(i, carry):
+        at = rows_at(i, 256)
+        gate = jnp.dot(low_s[at, :], wg_ref[...], preferred_element_type=F32)
+        up = jnp.dot(low_s[at, :], wu_ref[...], preferred_element_type=F32)
+        grad = lax.dot_general(
+            grad_ref[at, :], wd_ref[...], (((1,), (1,)), ((), ())), preferred_element_type=F32
+        )
+        sig = jax.nn.sigmoid(gate)
+        silu = gate * sig
+        hid_s[at, :] = (silu * up).astype(jnp.bfloat16)
+        pair_s[at, 0:tile] = (grad * up * (sig * (1.0 + gate * (1.0 - sig)))).astype(jnp.bfloat16)
+        pair_s[at, tile : 2 * tile] = (grad * silu).astype(jnp.bfloat16)
+        return carry
+
+    lax.fori_loop(0, seq // 256, hidden, 0)
+    both = jnp.concatenate([wg_ref[...], wu_ref[...]], axis=1)
+
+    def rows(i, carry):
+        at = rows_at(i, 256)
+        out = jnp.dot(hid_s[at, :], wd_ref[...], preferred_element_type=F32)
+        back = lax.dot_general(
+            pair_s[at, :], both, (((1,), (1,)), ((), ())), preferred_element_type=F32
+        )
+
+        @pl.when(step == 0)
+        def _():
+            out_ref[at, :] = out
+            back_ref[at, :] = back
+
+        @pl.when(step > 0)
+        def _():
+            out_ref[at, :] = out_ref[at, :] + out
+            back_ref[at, :] = back_ref[at, :] + back
+
+        return carry
+
+    lax.fori_loop(0, seq // 256, rows, 0)
+
+    def grads(i, carry):
+        at = rows_at(i, 512)
+        gd_ref[at, :] = jnp.dot(grad_t[at, :], hid_s[...], preferred_element_type=F32)
+        two = jnp.dot(low_t[at, :], pair_s[...], preferred_element_type=F32)
+        gg_ref[at, :] = two[:, 0:tile]
+        gu_ref[at, :] = two[:, tile:]
+        return carry
+
+    lax.fori_loop(0, width // 512, grads, 0)
+
+
+def mlp(tokens, length, branch, cotangent, gain, wg, wu, wd):
+    seq, width = tokens.shape
+    units, tile = wg.shape[1], 256
+    columns = pl.BlockSpec((width, tile), lambda i, _: (0, i))
+    full = whole((seq, width))
+    shape = lambda *s, t=F32: jax.ShapeDtypeStruct(s, t)
+    low = jnp.bfloat16
+    return pl.pallas_call(
+        mlp_kernel,
+        grid_spec=pltpu.PrefetchScalarGridSpec(
+            num_scalar_prefetch=1,
+            grid=(units // tile,),
+            in_specs=[full, full, full, whole((1, width)), columns, columns]
+            + [pl.BlockSpec((tile, width), lambda i, _: (i, 0))],
+            out_specs=[full] * 4 + [columns] * 3 + [whole((2, width))],
+            scratch_shapes=[
+                pltpu.VMEM((seq, width), low),
+                pltpu.VMEM((width, seq), low),
+                pltpu.VMEM((width, seq), low),
+                pltpu.VMEM((seq, tile), low),
+                pltpu.VMEM((seq, 2 * tile), low),
+            ],
+        ),
+        out_shape=[
+            shape(seq, width), shape(seq, width, t=low), shape(seq, width), shape(seq, width),
+            shape(width, units), shape(width, units), shape(width, units), shape(2, width),
+        ],
+        compiler_params=pltpu.CompilerParams(vmem_limit_bytes=56 << 20),
+        cost_estimate=pl.CostEstimate(flops=20 * 10**9, bytes_accessed=60 * 10**6, transcendentals=10**6),
+    )(length, tokens, branch, cotangent, gain, wg, wu, wd)
+
+
+def backward_kernel(
+    length_ref, grad_ref, low_ref, qn_ref, kn_ref, v_ref, sig_ref, att_ref, gated_ref, stat_ref,
+    decay_ref, wq_ref, wk_ref, wv_ref, wo_ref, wf_ref, wout_ref,
+    back_ref, gq_ref, gk_ref, gv_ref, go_ref, gout_ref, gf_ref, bias_ref,
+    low_t, grad_s, grad_t, k_s, do_s, line_s, dq_s, dk_s, dv_s, all_s, fall_s,
+):
+    step = pl.program_id(0)
+    seq, width = low_ref.shape
+    length = length_ref[0]
+    low16 = jnp.bfloat16
+
+    @pl.when(step == 0)
+    def _():
+        def turn(i, carry):
+            at = rows_at(i, 128)
+            grad = grad_ref[at, :].astype(low16)
+            grad_s[at, :] = grad
+            grad_t[:, at] = grad.T
+            low_t[:, at] = low_ref[at, :].T
+            return carry
+
+        lax.fori_loop(0, seq // 128, turn, 0)
+        decay = decay_ref[0]
+        row = lax.broadcasted_iota(jnp.int32, decay.shape, 0)
+        final = jnp.sum(jnp.where(row == length - 1, decay, 0.0), axis=0, keepdims=True)
+        line_s[...] = jnp.where(row < length, decay, final).T[0:8]
+        fall_s[...] = jnp.zeros_like(fall_s)
+
+    first = first_head((seq, PAIR))
+    gg = lax.dot_general(
+        grad_s[...], wout_ref[...], (((1,), (1,)), ((), ())), preferred_element_type=F32
+    )
+    sig = sig_ref[...]
+    do_s[...] = (gg * sig).astype(low16)
+    all_s[:, 3 * PAIR : 4 * PAIR] = (gg * att_ref[...] * sig * (1.0 - sig)).astype(low16)
+    k_s[...] = kn_ref[...].astype(low16)
+    dk_s[...] = jnp.zeros_like(dk_s)
+    dv_s[...] = jnp.zeros_like(dv_s)
+    row = lax.broadcasted_iota(jnp.int32, (seq, PAIR), 0)
+    columns, lines = [], [one_row(line_s, 2 * step + head) for head in (0, 1)]
+    for head in (0, 1):
+        column = jnp.sum(
+            jnp.where(lane_is((seq, PAIR), 2 * step + head), decay_ref[0], 0.0), axis=1, keepdims=True
+        )
+        columns.append(jnp.where(row[:, 0:1] < length, column, -NEG))
+    block = first_head((128, PAIR))
+    zero = jnp.zeros((128, PAIR), low16)
+    lower = lax.broadcasted_iota(jnp.int32, (128, 128), 0) > lax.broadcasted_iota(
+        jnp.int32, (128, 128), 1
+    )
+    for i in range(seq // 128):
+        at, n = slice(i * 128, i * 128 + 128), i * 128 + 128
+        q = qn_ref[at, :].astype(low16)
+        do = do_s[at, :]
+        pieces = []
+        for head in (0, 1):
+            pick = (lambda t: jnp.where(block, t, zero)) if head == 0 else (lambda t: jnp.where(block, zero, t))
+            own_q, own_do = pick(q), pick(do)
+            one = jnp.where(lane_is((128, PAIR), 2 * step + head), 1.0, 0.0).astype(low16)
+            s = lax.dot_general(
+                k_s[0:n, :], own_q, (((1,), (1,)), ((), ())), preferred_element_type=F32
+            )
+            s = s * (HEAD ** (-0.5)) + (lines[head][:, at] - columns[head][0:n])
+            diagonal = jnp.where(lower, NEG, s[n - 128 :, :])
+            s = diagonal if i == 0 else jnp.concatenate([s[: n - 128, :], diagonal], axis=0)
+            p = jnp.exp(s)
+            p = p * (1.0 / jnp.sum(p, axis=0, keepdims=True))
+            dp = lax.dot_general(
+                v_ref[0:n, :], own_do, (((1,), (1,)), ((), ())), preferred_element_type=F32
+            )
+            ds = (p * (dp - jnp.sum(p * dp, axis=0, keepdims=True))).astype(low16)
+            dv_s[0:n, :] = dv_s[0:n, :] + jnp.dot(
+                p.astype(low16), own_do, preferred_element_type=F32
+            )
+            dk_s[0:n, :] = dk_s[0:n, :] + jnp.dot(
+                ds, jnp.concatenate([own_q, one], axis=1), preferred_element_type=F32
+            )
+            keys = k_s[0:n, :]
+            mark = jnp.where(lane_is((n, PAIR), 2 * step + head), 1.0, 0.0).astype(low16)
+            pieces.append(
+                lax.dot_general(
+                    ds, jnp.concatenate([keys, mark], axis=1), (((0,), (0,)), ((), ())),
+                    preferred_element_type=F32,
+                )
+            )
+        dq_s[at, :] = jnp.where(block, pieces[0][:, 0:PAIR], pieces[1][:, 0:PAIR])
+        fall_s[at, :] = fall_s[at, :] + pieces[0][:, PAIR:] + pieces[1][:, PAIR:]
+    fall_s[...] = fall_s[...] - dk_s[:, PAIR:]
+    stat = stat_ref[...]
+    for e, n_ref, col, to in ((dq_s, qn_ref, 0, 0), (dk_s, kn_ref, 2, PAIR)):
+        e = e[:, 0:PAIR] * (HEAD ** (-0.5))
+        n = n_ref[...]
+        a, b = halves_mean(e * n)
+        r = jnp.where(first, stat[:, col : col + 1], stat[:, col + 1 : col + 2])
+        all_s[:, to : to + PAIR] = (r * (e - n * jnp.where(first, a, b))).astype(low16)
+    all_s[:, 2 * PAIR : 3 * PAIR] = dv_s[...].astype(low16)
+    weights = jnp.concatenate([wq_ref[...], wk_ref[...], wv_ref[...], wo_ref[...]], axis=1)
+
+    def rows(i, carry):
+        at = rows_at(i, 256)
+        back = lax.dot_general(
+            all_s[at, :], weights, (((1,), (1,)), ((), ())), preferred_element_type=F32
+        )
+
+        @pl.when(step == 0)
+        def _():
+            back_ref[at, :] = back
+
+        @pl.when(step > 0)
+        def _():
+            back_ref[at, :] = back_ref[at, :] + back
+
+        return carry
+
+    lax.fori_loop(0, seq // 256, rows, 0)
+
+    def grads(i, carry):
+        at = rows_at(i, 512)
+        four = jnp.dot(low_t[at, :], all_s[...], preferred_element_type=F32)
+        for j, ref in enumerate((gq_ref, gk_ref, gv_ref, go_ref)):
+            ref[at, :] = four[:, j * PAIR : j * PAIR + PAIR]
+        gout_ref[at, :] = jnp.dot(grad_t[at, :], gated_ref[...], preferred_element_type=F32)
+        return carry
+
+    lax.fori_loop(0, width // 512, grads, 0)
+
+    @pl.when(step == pl.num_programs(0) - 1)
+    def _():
+        back = running_sum(fall_s[...], backward=True) * decay_ref[1]
+        back = back.astype(low16)
+        bias_ref[...] = jnp.sum(back.astype(F32), axis=0, keepdims=True)
+        gf_ref[...] = jnp.dot(low_t[...], back, preferred_element_type=F32)
+        back_ref[...] = back_ref[...] + lax.dot_general(
+            back, wf_ref[...], (((1,), (1,)), ((), ())), preferred_element_type=F32
+        )
+
+
+def backward_attention(length, grad, low, qn, kn, v, sig, att, gated, stat, decay, wq, wk, wv, wo, wf, wout):
+    seq, width = low.shape
+    heads = wq.shape[1]
+    weights = pl.BlockSpec((width, PAIR), lambda i, _: (0, i))
+    lanes = pl.BlockSpec((seq, PAIR), lambda i, _: (0, i))
+    full = whole((seq, width))
+    shape = lambda *s: jax.ShapeDtypeStruct(s, F32)
+    low16 = jnp.bfloat16
+    return pl.pallas_call(
+        backward_kernel,
+        grid_spec=pltpu.PrefetchScalarGridSpec(
+            num_scalar_prefetch=1,
+            grid=(heads // PAIR,),
+            in_specs=[full, full] + [lanes] * 7 + [whole((2, seq, PAIR))] + [weights] * 4
+            + [whole((width, PAIR)), pl.BlockSpec((PAIR, width), lambda i, _: (i, 0))],
+            out_specs=[full] + [weights] * 5 + [whole((width, PAIR)), whole((1, PAIR))],
+            scratch_shapes=[
+                pltpu.VMEM((width, seq), low16),
+                pltpu.VMEM((seq, width), low16),
+                pltpu.VMEM((width, seq), low16),
+                pltpu.VMEM((seq, PAIR), low16),
+                pltpu.VMEM((seq, PAIR), low16),
+                pltpu.VMEM((8, seq), F32),
+                pltpu.VMEM((seq, PAIR), F32),
+                pltpu.VMEM((seq, 2 * PAIR), F32),
+                pltpu.VMEM((seq, PAIR), F32),
+                pltpu.VMEM((seq, 4 * PAIR), low16),
+                pltpu.VMEM((seq, PAIR), F32),
+            ],
+        ),
+        out_shape=[shape(seq, width)] + [shape(width, heads)] * 5 + [shape(width, PAIR), shape(1, PAIR)],
+        compiler_params=pltpu.CompilerParams(vmem_limit_bytes=56 << 20),
+        cost_estimate=pl.CostEstimate(flops=14 * 10**9, bytes_accessed=50 * 10**6, transcendentals=4 * 10**6),
+    )(length, grad, low, qn, kn, v, sig, att, gated, stat, decay, wq, wk, wv, wo, wf, wout)
 
 
 def per_device(
-    tokens,
-    lengths,
-    buckets,
-    out_cotangent,
-    gain_attn,
-    w_query,
-    w_key,
-    w_value,
-    w_outgate,
-    w_forget,
-    b_forget,
-    w_out,
-    gain_mlp,
-    w_gate,
-    w_up,
-    w_down,
+    tokens, lengths, buckets, out_cotangent, gain_attn, w_query, w_key, w_value, w_outgate,
+    w_forget, b_forget, w_out, gain_mlp, w_gate, w_up, w_down,
 ):
-    inputs = tokens[0].astype(jnp.float32)
-    seq_len, model_width = inputs.shape
-    head_count = w_forget.shape[1]
-    head_dim = w_query.shape[1] // head_count
-    score_scale = head_dim ** (-0.5)
-    valid_len = lengths[0]
-    positions = jnp.arange(seq_len)
-    valid_rows = (positions < valid_len).astype(jnp.float32)[:, None]
-    allowed = (positions[None, :] <= positions[:, None]) & (positions[None, :] < valid_len)
-    normed_in, norm_back_in = jax.vjp(gain_norm, inputs, gain_attn.astype(jnp.float32))
-    in_low = normed_in.astype(jnp.bfloat16)
-    query_pre = low_dot(in_low, w_query)
-    key_pre = low_dot(in_low, w_key)
-    value_pre = low_dot(in_low, w_value)
-    outgate_pre = low_dot(in_low, w_outgate)
-    forget_pre = low_dot(in_low, w_forget) + b_forget.astype(jnp.float32)
-    query_norm, query_back = jax.vjp(norm_rows, query_pre.reshape(seq_len, head_count, head_dim))
-    key_norm, key_back = jax.vjp(norm_rows, key_pre.reshape(seq_len, head_count, head_dim))
-    query_low = query_norm.astype(jnp.bfloat16)
-    key_low = key_norm.astype(jnp.bfloat16)
-    value_low = value_pre.astype(jnp.bfloat16).reshape(seq_len, head_count, head_dim)
-    log_decay = jnp.cumsum(jax.nn.log_sigmoid(forget_pre), axis=0).T
-
-    def masked_scores():
-        base_scores = (
-            jnp.einsum("ihd,jhd->hij", query_low, key_low, preferred_element_type=jnp.float32)
-            * score_scale
-        )
-        base_scores = base_scores + log_decay[:, :, None] - log_decay[:, None, :]
-        return jnp.where(allowed[None], base_scores, -1e30)
-
-    masked = masked_scores()
-    row_top = jnp.max(masked, axis=-1, keepdims=True)
-    exponent = jnp.exp(masked - row_top)
-    row_total = jnp.sum(exponent, axis=-1, keepdims=True)
-    attn_probs = exponent / row_total
-    log_total = row_top + jnp.log(row_total)
-    attended = jnp.einsum(
-        "hij,jhd->ihd",
-        attn_probs.astype(jnp.bfloat16),
-        value_low,
-        preferred_element_type=jnp.float32,
-    ).reshape(seq_len, head_count * head_dim)
-    gate_sig = jax.nn.sigmoid(outgate_pre)
-    gated_low = (attended * gate_sig).astype(jnp.bfloat16)
-    branch_attn = y_reduce(low_dot(gated_low, w_out), 0)
-    middle = inputs + branch_attn
-    normed_mid, norm_back_mid = jax.vjp(gain_norm, middle, gain_mlp.astype(jnp.float32))
-    mid_low = normed_mid.astype(jnp.bfloat16)
-    gate_pre = low_dot(mid_low, w_gate)
-    up_pre = low_dot(mid_low, w_up)
-    hidden_f, swiglu_back = jax.vjp(swiglu, gate_pre, up_pre)
-    hidden_low = hidden_f.astype(jnp.bfloat16)
-    branch_mlp = lax.psum(low_dot(hidden_low, w_down), "mp")
+    x, cotangent = tokens[0], out_cotangent[0]
+    model_width = x.shape[1]
+    heads = w_forget.shape[1]
+    gain_in = gain_attn.astype(F32)[None]
+    gain_mid = gain_mlp.astype(F32)[None]
+    w_fall = jnp.pad(w_forget, ((0, 0), (0, PAIR - heads)))
+    b_fall = jnp.pad(b_forget.astype(F32), (0, PAIR - heads))[None]
+    weights = (w_query, w_key, w_value, w_outgate, w_fall)
+    low, *saved = forward_attention(x, lengths, gain_in, *weights, b_fall)
+    branch_attn = y_reduce(low_dot(saved[5], w_out), 0)
+    middle, grad_rows, mlp_local, mid_local, g_down, g_gate, g_up, squares = mlp(
+        x, lengths, branch_attn, cotangent, gain_mid, w_gate, w_up, w_down
+    )
+    grad_middle, mlp_share, mlp_gain = reduce_both(
+        mid_local, middle, grad_rows, gain_mid, [g_down, g_gate, g_up], 512, 1, 52
+    )
+    mlp_local, grad_middle = lax.optimization_barrier((mlp_local, grad_middle))
+    branch_mlp = lax.psum(mlp_local, "mp")
+    in_local, g_query, g_key, g_value, g_outgate, g_out, g_fall, bias = backward_attention(
+        lengths, grad_middle, low, *saved, *weights, w_out
+    )
+    input_grad, share, gains = reduce_both(
+        in_local, x, grad_middle, gain_in,
+        [g_query, g_key, g_value, g_outgate, g_out, g_fall], 512, 2, 48, mlp_gain,
+    )
     layer_out = (middle + branch_mlp).astype(jnp.bfloat16)
-    bucket_hot = (buckets[0] == jnp.arange(NBUCKET)).astype(jnp.float32)
-    square_sums = jnp.stack(
-        [
-            jnp.sum(valid_rows * inputs * inputs),
-            jnp.sum(valid_rows * branch_attn * branch_attn),
-            jnp.sum(valid_rows * branch_mlp * branch_mlp),
-        ]
+    valid = (jnp.arange(x.shape[0]) < lengths[0]).astype(F32)[:, None]
+    bucket_hot = (buckets[0] == jnp.arange(NBUCKET)).astype(F32)
+    square_sums = jnp.concatenate(
+        [jnp.sum(squares, axis=1), jnp.sum(valid * branch_mlp * branch_mlp)[None]]
     )
     bucket_sums = square_sums[:, None] * bucket_hot[None, :]
-    bucket_count = valid_len.astype(jnp.float32) * bucket_hot
-    grad_rows = out_cotangent[0].astype(jnp.float32) * valid_rows
-    grad_rows_low = grad_rows.astype(jnp.bfloat16)
-    grad_w_down = back_dot(grad_rows_low, hidden_low)
-    grad_hidden = trans_dot(grad_rows_low, w_down)
-    grad_gate_f, grad_up_f = swiglu_back(grad_hidden)
-    gate_grad_low = grad_gate_f.astype(jnp.bfloat16)
-    up_grad_low = grad_up_f.astype(jnp.bfloat16)
-    grad_w_gate = back_dot(mid_low, gate_grad_low)
-    grad_w_up = back_dot(mid_low, up_grad_low)
-    grad_mid_local = trans_dot(gate_grad_low, w_gate) + trans_dot(up_grad_low, w_up)
-    grad_mid_norm, down_share, gate_share, up_share = reduce_both(
-        grad_mid_local, [grad_w_down, grad_w_gate, grad_w_up], 512, 1, 48
-    )
-    grad_middle_part, grad_gain_mlp = norm_back_mid(grad_mid_norm)
-    grad_middle = grad_rows + grad_middle_part
-    middle_low = grad_middle.astype(jnp.bfloat16)
-    grad_w_out = back_dot(middle_low, gated_low)
-    grad_gated = trans_dot(middle_low, w_out)
-    attended_grad_low = (grad_gated * gate_sig).astype(jnp.bfloat16)
-    outgate_grad_low = (grad_gated * attended * gate_sig * (1.0 - gate_sig)).astype(jnp.bfloat16)
-    attended_heads = attended_grad_low.reshape(seq_len, head_count, head_dim)
-    again_probs = jnp.exp(masked_scores() - log_total)
-    grad_probs = jnp.einsum(
-        "ihd,jhd->hij", attended_heads, value_low, preferred_element_type=jnp.float32
-    )
-    row_delta = jnp.sum(again_probs * grad_probs, axis=-1, keepdims=True)
-    scores_grad_low = (again_probs * (grad_probs - row_delta)).astype(jnp.bfloat16)
-    value_grad_low = (
-        jnp.einsum(
-            "hij,ihd->jhd",
-            again_probs.astype(jnp.bfloat16),
-            attended_heads,
-            preferred_element_type=jnp.float32,
-        )
-        .reshape(seq_len, head_count * head_dim)
-        .astype(jnp.bfloat16)
-    )
-    grad_query_norm = (
-        jnp.einsum("hij,jhd->ihd", scores_grad_low, key_low, preferred_element_type=jnp.float32)
-        * score_scale
-    )
-    grad_key_norm = (
-        jnp.einsum("hij,ihd->jhd", scores_grad_low, query_low, preferred_element_type=jnp.float32)
-        * score_scale
-    )
-    score_grad = scores_grad_low.astype(jnp.float32)
-    grad_decay = jnp.sum(score_grad, axis=2) - jnp.sum(score_grad, axis=1)
-    grad_log_forget = jnp.flip(jnp.cumsum(jnp.flip(grad_decay, 1), axis=1), 1).T
-    forget_grad_low = (grad_log_forget * jax.nn.sigmoid(-forget_pre)).astype(jnp.bfloat16)
-    query_grad_low = (
-        query_back(grad_query_norm)[0].reshape(seq_len, head_count * head_dim).astype(jnp.bfloat16)
-    )
-    key_grad_low = (
-        key_back(grad_key_norm)[0].reshape(seq_len, head_count * head_dim).astype(jnp.bfloat16)
-    )
-    grad_w_query = back_dot(in_low, query_grad_low)
-    grad_w_key = back_dot(in_low, key_grad_low)
-    grad_w_value = back_dot(in_low, value_grad_low)
-    grad_w_outgate = back_dot(in_low, outgate_grad_low)
-    grad_w_forget = back_dot(in_low, forget_grad_low)
-    grad_b_forget = jnp.sum(forget_grad_low.astype(jnp.float32), axis=0)
-    grad_in_local = (
-        trans_dot(query_grad_low, w_query)
-        + trans_dot(key_grad_low, w_key)
-        + trans_dot(value_grad_low, w_value)
-    )
-    grad_in_local = (
-        grad_in_local
-        + trans_dot(outgate_grad_low, w_outgate)
-        + trans_dot(forget_grad_low, w_forget)
-    )
-    rms_in = norm_rows(inputs)
-    gain_local = jnp.sum(grad_in_local * rms_in, axis=0)
-    small = jnp.concatenate(
-        [
-            grad_w_forget,
-            grad_gain_mlp[:, None] * (1.0 / Y),
-            gain_local[:, None],
-            jnp.zeros((model_width, 120), F32),
-        ],
-        axis=1,
-    )
-    grad_in_norm, query_share, key_share, value_share, outgate_share, out_share, small_share = (
-        reduce_both(
-            grad_in_local,
-            [grad_w_query, grad_w_key, grad_w_value, grad_w_outgate, grad_w_out, small],
-            512,
-            2,
-            40,
-        )
-    )
-    gains = lax.psum(small_share[:, 6:8], "mp")
-    grad_in_part, _ = norm_back_in(grad_in_norm)
-    input_grad = grad_middle + grad_in_part
-    bucket_total, bucket_rows, bias_sum = in_one((bucket_sums, bucket_count, grad_b_forget), "dp")
+    bucket_count = lengths[0].astype(F32) * bucket_hot
+    bucket_total, bucket_rows, bias_sum = in_one(
+        (bucket_sums, bucket_count, bias[0, :heads]), "dp"
+    )
     rms = jnp.sqrt(bucket_total / (bucket_rows[None, :] * model_width))
+    rows = model_width // lax.axis_size("dp")
+    mine = lax.dynamic_slice_in_dim(gains, lax.axis_index("dp") * rows, rows, axis=1)
+    units, inner = w_gate.shape[1], w_query.shape[1]
+    part = lambda i: share[:, i * inner : i * inner + inner]
     return (
         layer_out[None],
         input_grad[None],
-        gains[:, 1],
-        query_share,
-        key_share,
-        value_share,
-        outgate_share,
-        small_share[:, :6],
+        mine[0],
+        part(0),
+        part(1),
+        part(2),
+        part(3),
+        share[:, 5 * inner : 5 * inner + heads],
         bias_sum,
-        out_share.T,
-        gains[:, 0],
-        gate_share,
-        up_share,
-        down_share.T,
+        part(4).T,
+        mine[1],
+        mlp_share[:, units : 2 * units],
+        mlp_share[:, 2 * units :],
+        mlp_share[:, :units].T,
         rms,
     )
 

time: 581 us -> 480 us (0.83); the launches traced: 573 us -> 478 us
  matrix products: 128 us -> 1.38 us
  Pallas kernels: 302 us -> 414 us
  other arithmetic: 58.2 us -> 8.81 us
  local copies, waits for them, and re-layouts: 42.4 us -> 24.1 us
  blocking collectives: 17.6 us -> 0 us
  waiting for transfers between devices: 0.02 us -> 6.11 us
    pallas_call x2 -> x5, Pallas kernels: 221 us -> 332 us  [the longest x2 213 us: reduce_both(): pl.pallas_call(functools.partial(both_kernel, pieces, count, small), out_...]
    dot_general x24 -> x0, matrix products: 105 us -> none  [the longest x9 41.8 us: back_dot(): lax.dot_general(left, right, (((0,), (0,)), ((), ())), preferred_element_...]
    reduce_sum x8 -> x2, other arithmetic: 36.5 us -> 6.55 us  [the longest x1 6.42 us: per_device(): jnp.sum(valid * branch_mlp * branch_mlp)[None]]
    dot_general x9 -> x1, matrix products: 23.3 us -> 1.38 us  [low_dot(): return jnp.dot(left, right, preferred_element_type=jnp.float32)]
    psum x1 -> x0, blocking collectives: 17.6 us -> none  [per_device(): gains = lax.psum(small_share[:, 6:8], 'mp')]
    unnamed x203 -> x45, local copies, waits for them, and re-layouts: 34.3 us -> 18.5 us
    all_to_all x1, waiting for transfers between devices: 0.01 us -> 6.1 us  [sent_to_all(): lax.all_to_all(jnp.broadcast_to(array[None], (devices, *array.shape)), ax...]
  transfers between devices with their start and end apart: 2 -> 2, of which waited for: 0 -> 1; matrix products, arithmetic and copies ran while one was open for 21% -> 1% of each run, Pallas kernels for 39% -> 36%
where the time goes in v2:
time: 480 us; the launch traced here: 478 us
  Pallas kernels  414 us (86%)
  local copies, waits for them, and re-layouts  24.1 us (5%)
  between operations  15.6 us (3%)
  other arithmetic  8.81 us (2%)
  starting transfers between devices  8.52 us (2%)
  waiting for transfers between devices  6.11 us (1%)
    pallas_call x2, Pallas kernels, reduce_both(): pl.pallas_call(functools.partial(both_kernel, pieces, count, small), out_...  213 us
    pallas_call x1, Pallas kernels, y_reduce(): pl.pallas_call(y_reduce_kernel, out_shape=jax.ShapeDtypeStruct(array.shap...  81.5 us
    pallas_call x1, Pallas kernels, mlp(): pl.pallas_call(mlp_kernel, grid_spec=pltpu.PrefetchScalarGridSpec(num_sca...  48.2 us
    pallas_call x1, Pallas kernels, backward_attention(): pl.pallas_call(backward_kernel, grid_spec=pltpu.PrefetchScalarGridSpec(nu...  46.7 us
    pallas_call x1, Pallas kernels, forward_attention(): pl.pallas_call(forward_kernel, grid_spec=pltpu.PrefetchScalarGridSpec(num...  24.6 us
    unnamed x45, local copies, waits for them, and re-layouts  18.5 us
  transfers between devices with their start and end apart: 2, of which 1 were waited for; matrix products, arithmetic and copies ran while one was open for 1% of the time, Pallas kernels for 36%

profile of v2, /device:TPU:0, one launch (start us, length us, event | category | flops | bytes accessed | tf_op | source)
XLA Modules:
  0.0 478.2 jit_solution(18073330142776882382)
XLA Ops:
  7.9 0.7 bitcast_convert_fusion.bf_ref
  8.5 0.7 reshape.57.gain_ref
  9.2 1.3 reshape.59.gain_ref
  10.5 1.0 copy.38
  11.6 1.4 copy-done.7
  13.0 1.3 copy-done.8
  14.3 1.3 copy-done.9
  15.6 1.3 copy-done.10
  16.9 24.6 %shard_map.271 = (bf16[768,1536]{1,0:T(8,128)(2,1)}, f32[768,384]{1,0:T(8,128)S(1)}, f32[768,384]{1,0:T(8,128)S(1)}, bf16[768,384]{1,0:T(8,128)(2,1)S(1)}, f32[7...) custom-call(s32[1]{0:T(128)} %copy.47.length_ref, ...), custom_call_target="tpu_custom_call" | custom-call | flops 6000000000 | bytes 20000000 | tf_op jit(solution)/shard_map/pallas_call | solution.py:635
  41.5 1.4 fusion.3.in_ref
  43.1 0.3 copy-done.13
  44.0 0.3 copy-done.16
  44.6 81.5 %shard_map.272.branch_ref = f32[768,1536]{1,0:T(8,128)S(1)} custom-call(f32[768,1536]{1,0:T(8,128)S(1)} %fusion.3.in_ref), custom_call_target="tpu_custom_call" | custom-call | tf_op jit(solution)/shard_map/pallas_call | solution.py:157
  126.1 2.2 copy-done
  128.3 48.2 %shard_map.273 = (f32[768,1536]{1,0:T(8,128)}, bf16[768,1536]{1,0:T(8,128)(2,1)}, f32[768,1536]{1,0:T(8,128)}, f32[768,1536]{1,0:T(8,128)}, f32[1536,1024]{1,0:T...) custom-call(s32[1]{0:T(128)} %copy.47.length_ref, bf16[768,1536]{1,0:T(8,128)(2,1)} %bitcast.29, ...), custom_call_target="tpu_custom_call" | custom-call | flops 20000000000 | bytes 60000000 | tf_op jit(solution)/shard_map/pallas_call | solution.py:753
  176.5 86.2 %shard_map.274 = (f32[768,1536]{1,0:T(8,128)}, f32[48,3072]{1,0:T(8,128)S(1)}, f32[1,1536]{1,0:T(1,128)S(1)}) custom-call(f32[768,1536]{1,0:T(8,128)} %get-tuple-element.51.x_ref, f32[768,1536]{1,0:T(8,128)} %get-tuple-element.49.source_ref, bf16[768,1536]{1,0:T(8,128)(2,1)} %get-tuple-element.52.base_ref, f32[1,1536]{1,0:T(1,128)S(1)} %copy-done.6, ...), custom_call_target="tpu_custom_call" | custom-call | tf_op jit(solution)/shard_map/pallas_call | solution.py:469
  263.6 46.7 %shard_map.275 = (f32[768,1536]{1,0:T(8,128)}, f32[1536,384]{1,0:T(8,128)}, f32[1536,384]{1,0:T(8,128)}, f32[1536,384]{1,0:T(8,128)}, f32[1536,384]{1,0:T(8,128)...) custom-call(s32[1]{0:T(128)} %copy.47.length_ref, f32[768,1536]{1,0:T(8,128)} %get-tuple-element.58.grad_ref.base_ref, ...), custom_call_target="tpu_custom_call" | custom-call | flops 14000000000 | bytes 50000000 | tf_op jit(solution)/shard_map/pallas_call | solution.py:923
  310.4 1.7 copy-done.2
  312.0 1.1 copy-done.4
  313.2 126.4 %shard_map.276 = (f32[768,1536]{1,0:T(8,128)}, f32[48,2048]{1,0:T(8,128)S(1)}, f32[8,1536]{1,0:T(8,128)S(1)}) custom-call(f32[768,1536]{1,0:T(8,128)} %get-tuple-element.67.x_ref, bf16[768,1536]{1,0:T(8,128)(2,1)S(1)} %bitcast.30, f32[768,1536]{1,0:T(8,128)} %get-tuple-element.58.grad_ref.base_ref, f32[1,1536]{1,0:T(1,128)S(1)} %reshape.57.gain_ref, ...), custom_call_target="tpu_custom_call" | custom-call | tf_op jit(solution)/shard_map/pallas_call | solution.py:469
  439.7 0.7 slice_bitcast_fusion.1
  440.5 0.8 slice_bitcast_fusion
  441.3 6.4 %fusion = (f32[]{:T(128)}, bf16[1,768,1536]{2,1,0:T(8,128)(2,1)}) fusion(f32[768,1536]{1,0:T(8,128)} %all-reduce.4.cloned.1.call-done, f32[768]{0:T(1024)S(1)} %fusion.2, f32[768,1536]{1,0:T(8,128)} %get-tuple-element.49.source_ref), kind=kLoop, calls=%fused_computation.1 | loop fusion | flops 5898239 | bytes 11799556 | tf_op jit(solution)/shard_map/reduce_sum | solution.py:984
  447.7 0.7 pad_maximum_fusion
  448.7 0.6 broadcast_in_dim.43
  449.3 8.5 %all-to-all-start = ((f32[32,1,22]{2,1,0:T(1,128)}), f32[32,1,22]{2,1,0:T(1,128)S(1)}, u32[]{:S(2)}, u32[]{:S(2)}) async-start(f32[32,1,22]{2,1,0:T(1,128)} %broadcast_in_dim.43), calls=%async_computation | async-start | bytes 32768 | tf_op jit(solution)/shard_map/all_to_all | solution.py:18
  457.8 0.5 slice_bitcast_fusion.2
  458.3 0.7 copy.40
  459.0 6.1 %all-to-all-done = f32[32,1,22]{2,1,0:T(1,128)S(1)} async-done(((f32[32,1,22]{2,1,0:T(1,128)}), f32[32,1,22]{2,1,0:T(1,128)S(1)}, u32[]{:S(2)}, u32[]{:S(2)}) %all-to-all-start) | async-done | bytes 2848 | tf_op jit(solution)/shard_map/all_to_all | solution.py:18
  465.1 0.6 slice.52
  465.9 0.6 divide_sqrt_fusion
  466.5 4.8 %copy.49 = f32[1,768,1536]{2,1,0:T(8,128)} copy(f32[1,768,1536]{2,1,0:T(8,128)} %bitcast.31) | data formatting | bytes 9437184
  (50 shorter events, 1.9 us)
Async XLA Ops:
  7.2 434.1 %all-reduce.4.cloned.1.call-start = ((), (), s32[]{:S(2)}) async-start(), calls=%async_computation.1 | async-start | bytes 9437184 | tf_op jit(solution)/shard_map/psum | solution.py:972
  11.6 29.8 %copy-start.5 = (bf16[1536,128]{1,0:T(8,128)(2,1)}, bf16[1536,128]{1,0:T(8,128)(2,1)S(1)}, u32[]{:S(2)}) copy-start(bf16[1536,128]{1,0:T(8,128)(2,1)S(1)} %pad.9.wf_ref) | copy-start | bytes 1179652
  11.6 1.4 copy-start.7
  13.0 1.3 copy-start.8
  14.3 1.3 copy-start.9
  15.6 1.3 copy-start.10
  16.9 24.7 %copy-start.18 = (bf16[384,1536]{1,0:T(8,128)(2,1)S(1)}, bf16[384,1536]{1,0:T(8,128)(2,1)}, u32[]{:S(2)}) copy-start(bf16[384,1536]{1,0:T(8,128)(2,1)} %wout_ref.1) | copy-start | bytes 3538948
  41.4 1.5 copy-start.3
  41.4 1.5 copy-start.11
  41.5 1.6 copy-start.12
  41.5 1.9 copy-start.13
  41.5 2.3 copy-start.14
  41.5 2.6 copy-start.15
  41.5 2.9 copy-start.16
  41.5 3.1 copy-start.17
  126.1 2.2 copy-start
  128.3 48.2 %copy-start.6 = (f32[1,1536]{1,0:T(1,128)S(1)}, f32[1,1536]{1,0:T(1,128)}, u32[]{:S(2)}) copy-start(f32[1,1536]{1,0:T(1,128)} %reshape.59.gain_ref) | copy-start | bytes 18436
  262.8 0.7 copy-start.19
  263.6 46.7 %copy-start.1 = (bf16[1,768,1536]{2,1,0:T(8,128)(2,1)S(1)}, bf16[1,768,1536]{2,1,0:T(8,128)(2,1)}, u32[]{:S(2)}) copy-start(bf16[1,768,1536]{2,1,0:T(8,128)(2,1)} %param.16) | copy-start | bytes 7077892
  310.4 1.7 copy-start.2
  312.0 1.1 copy-start.4
  313.2 126.6 %copy-start.20 = (f32[1,128]{1,0:T(1,128)S(1)}, f32[1,128]{1,0:T(1,128)}, u32[]{:S(2)}) copy-start(f32[1,128]{1,0:T(1,128)} %get-tuple-element.79) | copy-start | bytes 1540
  449.3 15.8 %all-to-all-start = ((f32[32,1,22]{2,1,0:T(1,128)}), f32[32,1,22]{2,1,0:T(1,128)S(1)}, u32[]{:S(2)}, u32[]{:S(2)}) async-start(f32[32,1,22]{2,1,0:T(1,128)} %broadcast_in_dim.43), calls=%async_computation | async-start | bytes 32768 | tf_op jit(solution)/shard_map/all_to_all | solution.py:18
Sparse Core Ops, SparseCore 0:
  262.9 142.0 all-reduce.3

commit v3 on v0

v3 whole, which is shorter than its diff:
```python
import functools

import jax
import jax.numpy as jnp
from jax import lax
from jax.experimental import pallas as pl
from jax.experimental.pallas import tpu as pltpu
from jax.sharding import PartitionSpec as P

NBUCKET = 4


EPSILON = 1e-06


MESH = pl.DeviceIdType.MESH
F32 = jnp.float32
Y = 4
STEP = 512
STEPS = ("oR", "oL", "iR", "iL", "dR", "dL", "gRa", "gRb", "gLa", "gLb", "fR", "fL")


def rows_of(ref, start, count):
    return ref.at[pl.ds(pl.multiple_of(start, 8), count)]


def meet(devices):
    barrier = pltpu.get_barrier_semaphore()
    for device in devices:
        pl.semaphore_signal(barrier, inc=1, device_id=device, device_id_type=MESH)
    pl.semaphore_wait(barrier, len(devices))


def link(src, dst, ssem, rsem, at, device):
    return pltpu.make_async_remote_copy(
        src_ref=src,
        dst_ref=dst,
        send_sem=ssem.at[at],
        recv_sem=rsem.at[at],
        device_id=device,
        device_id_type=MESH,
    )


def push(*args):
    copy = link(*args)
    copy.start()
    return copy


class YRing:
    def __init__(self, rows, ssem, rsem):
        self.sems = (ssem, rsem)
        self.dp, self.me = lax.axis_index("dp"), lax.axis_index("mp")
        self.right, self.left = lax.rem(self.me + 1, Y), lax.rem(self.me + 3, Y)
        self.far = lax.rem(self.me + 2, Y)
        self.quarter, self.half = rows // Y, rows // Y // 2
        self.sent = {}

    def neighbours(self):
        return [(self.dp, self.right), (self.dp, self.left)]

    def send(self, name, src, dst, to):
        self.sent[name] = push(src, dst, *self.sems, STEPS.index(name), (self.dp, to))

    def start(self, x, opp, nbr):
        q, h = self.quarter, self.half
        self.send("oR", rows_of(x, self.far * q, h), opp.at[0], self.right)
        self.send("oL", rows_of(x, self.far * q + h, h), opp.at[1], self.left)
        self.send("iR", rows_of(x, self.right * q + h, h), nbr.at[0, h:q], self.right)
        self.send("iL", rows_of(x, self.left * q, h), nbr.at[1, 0:h], self.left)

    def relay(self, x, opp, nbr, held):
        q, h = self.quarter, self.half
        self.sent["oR"].wait_recv()
        held[0] = rows_of(x, self.right * q, h)[...] + opp[0]
        self.send("dR", held.at[0], nbr.at[0, 0:h], self.right)
        self.sent["oL"].wait_recv()
        held[1] = rows_of(x, self.left * q + h, h)[...] + opp[1]
        self.send("dL", held.at[1], nbr.at[1, h:q], self.left)

    def collect(self, x, nbr, part):
        h = self.half
        for name in (("dR", "iL"), ("iR", "dL"))[part]:
            self.sent[name].wait_recv()
        at = slice(part * h, part * h + h)
        return rows_of(x, self.me * self.quarter + part * h, h)[...] + nbr[0, at] + nbr[1, at]

    def spread(self, part, block):
        own, tag = block(self.me, part), "ab"[part]
        self.send("gR" + tag, own, own, self.right)
        self.send("gL" + tag, own, own, self.left)

    def forward(self, block):
        self.sent["gRa"].wait_recv()
        self.send("fR", block(self.left, 0), block(self.left, 0), self.right)
        self.sent["gLb"].wait_recv()
        self.send("fL", block(self.right, 1), block(self.right, 1), self.left)

    def arrive(self):
        for name in ("gRb", "gLa", "fR", "fL"):
            self.sent[name].wait_recv()

    def finish(self):
        for copy in self.sent.values():
            copy.wait_send()


def ring_scratch(quarter, columns):
    return [
        pltpu.VMEM((2, quarter // 2, columns), F32),
        pltpu.VMEM((2, quarter, columns), F32),
        pltpu.VMEM((2, quarter // 2, columns), F32),
    ]


def sems(*counts):
    return [pltpu.SemaphoreType.DMA((n,)) for n in counts for _ in (0, 1)]


class Place:
    def __init__(self):
        self.dp, self.my = lax.axis_index("dp"), lax.axis_index("mp")
        c, z, x = lax.rem(self.dp, 2), lax.rem(self.dp // 2, 4), self.dp // 8
        self.c, self.sib, self.chip = c, self.dp + 1 - 2 * c, x * 4 + z
        self.st1, self.st2 = 4 - 3 * c, 1 + 3 * c
        self.p1, self.p2 = x + c * (z - x), z + c * (x - z)
        step = lambda p, by: lax.rem(p + by, 4)
        self.r1, self.l1, self.o1 = (step(self.p1, by) for by in (1, 3, 2))
        self.r2, self.l2, self.o2 = (step(self.p2, by) for by in (1, 3, 2))

    def device(self, a, b):
        return ((a * self.st1 + b * self.st2) * 2 + self.c, self.my)

    def peers(self):
        return [
            (self.sib, self.my),
            self.device(self.r1, self.p2),
            self.device(self.l1, self.p2),
            self.device(self.p1, self.r2),
            self.device(self.p1, self.l2),
        ]


class ScatterSum:
    def __init__(self, here, sources, own, other, near, last, asem, bsem, lsem, ssem, rsem):
        self.here, self.sources = here, sources
        self.own, self.other, self.near, self.last = own, other, near, last
        self.asem, self.bsem, self.lsem, self.ssem, self.rsem = asem, bsem, lsem, ssem, rsem
        self.n = own.shape[0]
        self.sibling, *to = here.peers()
        self.to = (to[0:2], to[2:4])

    def message(self, name, k, stage):
        at = (k * 2 + stage) * 6 + STEPS.index(name)
        device = self.to[stage][0 if name[1] == "R" else 1]
        here, own = self.here, self.own.at[k]
        if stage:
            own, into, cut = own.at[here.p1], self.last.at[k], (slice(0, 24), slice(24, 48))
            far, right, left = here.o2, here.r2, here.l2
        else:
            into, cut = self.near.at[k], (slice(0, 2), slice(2, 4))
            far, right, left = here.o1, here.r1, here.l1
        row, part, slot = {
            "oR": (far, 0, 0),
            "oL": (far, 1, 1),
            "iR": (right, 1, 3),
            "iL": (left, 0, 4),
            "dR": (right, 0, 2),
            "dL": (left, 1, 5),
        }[name]
        return link(own.at[row, cut[part]], into.at[slot], self.ssem, self.rsem, at, device)

    def whole(self, k):
        own, other = self.own.at[k], self.other.at[k]
        return link(own, other, self.asem, self.bsem, k, self.sibling)

    def exchange(self, k):
        here = self.here
        ref, start, width = self.sources[k]

        def source(block):
            return ref.at[pl.ds(pl.multiple_of(block * 48, 16), 48), pl.ds(start, width)]

        def cross(i, carry):
            a, b = i // 4, lax.rem(i, 4)
            block = source((a * here.st2 + b * here.st1) * 2 + 1 - here.c)
            push(block, self.other.at[k, a, b], self.asem, self.bsem, k, self.sibling)
            return carry

        def fetch(i, carry):
            a, b = i // 4, lax.rem(i, 4)
            block = source((a * here.st1 + b * here.st2) * 2 + here.c)
            pltpu.make_async_copy(block, self.own.at[k, a, b], self.lsem.at[k]).start()
            return carry

        lax.fori_loop(0, 16, cross, 0)
        lax.fori_loop(0, 16, fetch, 0)

    def first(self, k):
        here, own, other = self.here, self.own, self.other
        pltpu.make_async_copy(own.at[k], own.at[k], self.lsem.at[k]).wait()
        self.whole(k).wait_recv()

        def add(p):
            def body(b, carry):
                own[k, p, b] = own[k, p, b] + other[k, p, b]
                return carry

            lax.fori_loop(0, 4, body, 0)

        add(here.o1)
        self.message("oR", k, 0).start()
        self.message("oL", k, 0).start()
        add(here.r1)
        self.message("iR", k, 0).start()
        add(here.l1)
        self.message("iL", k, 0).start()
        add(here.p1)

    def first_relay(self, k):
        here, own, near = self.here, self.own, self.near

        def add(p, at, slot):
            def body(b, carry):
                own[k, p, at + b] = own[k, p, at + b] + near[k, slot, b]
                return carry

            lax.fori_loop(0, 2, body, 0)

        self.message("oR", k, 0).wait_recv()
        add(here.r1, 0, 0)
        self.message("dR", k, 0).start()
        self.message("oL", k, 0).wait_recv()
        add(here.l1, 2, 1)
        self.message("dL", k, 0).start()

    def second(self, k):
        here, own, near = self.here, self.own, self.near
        for name in ("iR", "dR", "iL", "dL"):
            self.message(name, k, 0).wait_recv()

        def add(p):
            h, b = p // 2, lax.rem(p, 2)
            own[k, here.p1, p] = own[k, here.p1, p] + near[k, 2 + h, b] + near[k, 4 + h, b]

        add(here.o2)
        self.message("oR", k, 1).start()
        self.message("oL", k, 1).start()
        add(here.r2)
        self.message("iR", k, 1).start()
        add(here.l2)
        self.message("iL", k, 1).start()
        add(here.p2)

    def second_relay(self, k):
        here, own, last = self.here, self.own, self.last
        self.message("oR", k, 1).wait_recv()
        own[k, here.p1, here.r2, 0:24] = own[k, here.p1, here.r2, 0:24] + last[k, 0]
        self.message("dR", k, 1).start()
        self.message("oL", k, 1).wait_recv()
        own[k, here.p1, here.l2, 24:48] = own[k, here.p1, here.l2, 24:48] + last[k, 1]
        self.message("dL", k, 1).start()

    def result(self, k, out, at):
        here, own, last = self.here, self.own, self.last
        width = own.shape[4]
        for name in ("iR", "dR", "iL", "dL"):
            self.message(name, k, 1).wait_recv()
        columns = pl.ds(pl.multiple_of(at * width, 128), width)
        out[0:24, columns] = own[k, here.p1, here.p2, 0:24] + last[k, 2] + last[k, 4]
        out[24:48, columns] = own[k, here.p1, here.p2, 24:48] + last[k, 3] + last[k, 5]

    def sent(self, k):
        self.whole(k).wait_send()
        for stage in (0, 1):
            for name in STEPS[:6]:
                self.message(name, k, stage).wait_send()


def each(low, high, step):
    def body(k, carry):
        step(k)
        return carry

    lax.fori_loop(low, high, body, 0)


class SmallSum:
    def __init__(self, here, bufs, landed, ssem, rsem):
        self.bufs, self.landed, self.ssem, self.rsem = bufs, landed, ssem, rsem
        turn = lambda p, by: lax.rem(p + by, 4)
        self.stages = [
            [(here.sib, here.my)],
            [here.device(turn(here.p1, by), here.p2) for by in (1, 2, 3)],
            [here.device(here.p1, turn(here.p2, by)) for by in (1, 2, 3)],
            [(here.dp, turn(here.my, by)) for by in (1, 2, 3)],
        ]
        self.far = [self.stages[1][1], self.stages[2][1], self.stages[3][1]]
        self.sent = []

    def send(self, stage):
        for to in self.stages[stage]:
            at = len(self.sent)
            copy = push(self.bufs.at[stage], self.landed.at[at], self.ssem, self.rsem, at, to)
            self.sent.append(copy)

    def take(self, stage):
        value, count = self.bufs[stage], len(self.stages[stage])
        for at in range(len(self.sent) - count, len(self.sent)):
            self.sent[at].wait_recv()
            value = value + self.landed[at]
        self.bufs[stage + 1] = value

    def finish(self):
        for copy in self.sent:
            copy.wait_send()


def scatter_scratch(n, w):
    return [
        pltpu.VMEM((n, 4, 4, 48, w), F32),
        pltpu.VMEM((n, 4, 4, 48, w), F32),
        pltpu.VMEM((n, 6, 2, 48, w), F32),
        pltpu.VMEM((n, 6, 24, w), F32),
        pltpu.SemaphoreType.DMA((n,)),
        pltpu.SemaphoreType.DMA((n,)),
        pltpu.SemaphoreType.DMA((n,)),
        pltpu.SemaphoreType.DMA((12 * n,)),
        pltpu.SemaphoreType.DMA((12 * n,)),
    ]


def scatter_sources(refs, step):
    return [(ref, start, step) for ref in refs for start in range(0, ref.shape[1], step)]


def norm_back(value, source, base, gain):
    source = source.astype(F32)
    r = lax.rsqrt(jnp.mean(source * source, axis=1, keepdims=True) + EPSILON)
    n = source * r
    e = value * gain.astype(F32)
    inner = jnp.mean(e * n, axis=1, keepdims=True)
    return base.astype(F32) + r * (e - n * inner), jnp.sum(value * n, axis=0, keepdims=True)


def load(ref, scratch, sem):
    copy = pltpu.make_async_copy(ref, scratch, sem)
    copy.start()
    return copy


def middle_kernel(count, x_ref, source_ref, base_ref, gain_ref, w_ref, *refs):
    ins, refs = refs[:count], refs[count:]
    grad_ref, gg_ref, share_ref, sums_ref = refs[:4]
    source_s, base_s, w_s, opp, nbr, held, blocks, csem, *sem = refs[4:16]
    here, ring = Place(), YRing(x_ref.shape[0], *sem[0:2])
    total = ScatterSum(here, scatter_sources(ins, STEP), *refs[16:])
    n = total.n
    far = (ring.dp, ring.far)
    meet(ring.neighbours() + [far] + here.peers())
    ring.start(x_ref, opp, nbr)
    q, h = ring.quarter, ring.half
    loads = [
        load(rows_of(source_ref, ring.me * q, q), source_s, csem.at[0]),
        load(rows_of(base_ref, ring.me * q, q), base_s, csem.at[1]),
        load(w_ref, w_s, csem.at[2]),
    ]
    for k in range(n):
        total.exchange(k)
    each(0, n // 2, total.first)
    ring.relay(x_ref, opp, nbr, held)
    each(n // 2, n, total.first)
    each(0, n - 2, total.first_relay)
    for copy in loads:
        copy.wait()
    sums = 0.0
    for part in (0, 1):
        at = slice(part * h, part * h + h)
        value, more = norm_back(
            ring.collect(x_ref, nbr, part), source_s[at, :], base_s[at, :], gain_ref[...]
        )
        grad_ref[at, :] = value
        sums = sums + more
    sums_ref[...] = sums
    low = grad_ref[...].astype(jnp.bfloat16)
    inner = gg_ref.shape[1]
    swaps = []
    for j, by in enumerate((2, 1, 3, 0)):
        to = lax.rem(ring.me + by, Y)
        block = lax.dot_general(
            low, rows_of(w_s, to * inner, inner)[...], (((1,), (1,)), ((), ())),
            preferred_element_type=F32,
        )
        place = rows_of(gg_ref, ring.me * q, q)
        if by:
            blocks[j] = block
            swaps.append(push(blocks.at[j], place, *sem[2:4], j, (ring.dp, to)))
        else:
            place[...] = block
    each(n - 2, n, total.first_relay)
    each(0, n, total.second)
    each(0, n, total.second_relay)
    each(0, n, lambda k: total.result(k, share_ref, k))
    for copy in swaps:
        copy.wait_recv()
    for copy in swaps:
        copy.wait_send()
    ring.finish()
    each(0, n, total.sent)


def reduce_middle(partial, source, base, gain, w_full, grads, call_id):
    n = sum(g.shape[1] for g in grads) // STEP
    hbm, vmem = pl.BlockSpec(memory_space=pl.ANY), pl.BlockSpec(memory_space=pltpu.VMEM)
    rows, columns = partial.shape
    quarter, inner = rows // Y, w_full.shape[0] // Y
    return pl.pallas_call(
        functools.partial(middle_kernel, len(grads)),
        out_shape=[
            jax.ShapeDtypeStruct((quarter, columns), F32),
            jax.ShapeDtypeStruct((rows, inner), F32),
            jax.ShapeDtypeStruct((48, n * STEP), F32),
            jax.ShapeDtypeStruct((1, columns), F32),
        ],
        in_specs=[vmem, hbm, hbm, vmem, hbm] + [hbm] * len(grads),
        out_specs=[vmem] * 4,
        scratch_shapes=[
            pltpu.VMEM((quarter, columns), source.dtype),
            pltpu.VMEM((quarter, columns), base.dtype),
            pltpu.VMEM(w_full.shape, w_full.dtype),
        ]
        + ring_scratch(quarter, columns)
        + [pltpu.VMEM((3, quarter, inner), F32), pltpu.SemaphoreType.DMA((3,))]
        + sems(12, 3)
        + scatter_scratch(n, STEP),
        compiler_params=pltpu.CompilerParams(
            collective_id=call_id, has_side_effects=True, vmem_limit_bytes=56 << 20
        ),
    )(partial, source, base, gain, w_full, *grads)


def input_kernel(count, x_ref, source_ref, base_ref, gain_ref, other_ref, fall_ref, misc_ref, bias_ref, *refs):
    ins, refs = refs[:count], refs[count:]
    out_ref, out_share_ref, share_ref, sums_ref = refs[:4]
    source_s, opp, nbr, held, wide_s, landed, csem, *sem = refs[4:15]
    bufs, arrived, asem, bsem = refs[15:19]
    here, ring = Place(), YRing(x_ref.shape[0], *sem[0:2])
    total = ScatterSum(here, scatter_sources(ins, STEP), *refs[19:])
    tiny = SmallSum(here, bufs, arrived, asem, bsem)
    n, first = total.n, ins[0].shape[1] // STEP
    meet(ring.neighbours() + here.peers() + tiny.far)
    ring.start(x_ref, opp, nbr)
    q, h = ring.quarter, ring.half
    copy = load(rows_of(source_ref, ring.me * q, q), source_s, csem.at[0])
    for k in range(n):
        total.exchange(k)
    each(0, n // 2, total.first)
    ring.relay(x_ref, opp, nbr, held)
    each(n // 2, n, total.first)
    each(0, n - 2, total.first_relay)
    copy.wait()
    block = lambda owner, part: rows_of(out_ref, owner * q + part * h, h)
    sums = 0.0
    for part in (0, 1):
        at = slice(part * h, part * h + h)
        value, more = norm_back(
            ring.collect(x_ref, nbr, part), source_s[at, :], base_ref[at, :], gain_ref[...]
        )
        block(ring.me, part)[...] = value
        ring.spread(part, block)
        sums = sums + more
    bufs[0, 0:1, :] = sums
    bufs[0, 1:2, :] = other_ref[...]
    bufs[0, 8:16, :] = jnp.zeros_like(bufs[0, 8:16, :])
    bufs[0, 2:3, :] = jnp.zeros((1, sums_ref.shape[1]), F32)
    bufs[0, 2:3, 0:PAIR] = misc_ref[1:2, :]
    bufs[0, 3:9, :] = fall_ref[0:6, :]
    bufs[0, 9:10, 0:PAIR] = misc_ref[0:1, :]
    bufs[0, 10:11, 0:PAIR] = bias_ref[...]
    tiny.send(0)
    each(n - 2, n, total.first_relay)
    each(0, n, total.second)
    tiny.take(0)
    tiny.send(1)
    each(0, n, total.second_relay)
    tiny.take(1)
    tiny.send(2)
    each(0, first, lambda k: total.result(k, wide_s, k))
    inner = landed.shape[2]
    swaps = []
    for j, by in enumerate((2, 1, 3)):
        to = lax.rem(ring.me + by, Y)
        columns = pl.ds(pl.multiple_of(to * inner, 128), inner)
        swaps.append(push(wide_s.at[:, columns], landed.at[j], *sem[2:4], j, (ring.dp, to)))
    each(first, n, lambda k: total.result(k, share_ref, k - first))
    ring.forward(block)
    tiny.take(2)
    tiny.send(3)
    own = wide_s[:, pl.ds(pl.multiple_of(ring.me * inner, 128), inner)]
    for j, copy in enumerate(swaps):
        copy.wait_recv()
        own = own + landed[j]
    out_share_ref[...] = own
    tiny.take(3)
    rows = lax.broadcasted_iota(jnp.int32, sums_ref.shape, 0)
    sums_ref[...] = jnp.where(rows < 3, bufs[4], bufs[3])
    ring.arrive()
    for copy in swaps:
        copy.wait_send()
    tiny.finish()
    ring.finish()
    each(0, n, total.sent)


def reduce_input(partial, source, base, gain, small, grads, call_id):
    n = sum(g.shape[1] for g in grads) // STEP
    hbm, vmem = pl.BlockSpec(memory_space=pl.ANY), pl.BlockSpec(memory_space=pltpu.VMEM)
    rows, columns = partial.shape
    quarter, inner = rows // Y, grads[0].shape[1] // Y
    wide = grads[0].shape[1]
    shares = sum(g.shape[1] for g in grads[1:])
    return pl.pallas_call(
        functools.partial(input_kernel, len(grads)),
        out_shape=[
            jax.ShapeDtypeStruct(partial.shape, F32),
            jax.ShapeDtypeStruct((48, inner), F32),
            jax.ShapeDtypeStruct((48, shares), F32),
            jax.ShapeDtypeStruct((16, columns), F32),
        ],
        in_specs=[vmem, hbm, vmem, vmem] + [vmem] * 4 + [hbm] * len(grads),
        out_specs=[vmem] * 4,
        scratch_shapes=[pltpu.VMEM((quarter, columns), source.dtype)]
        + ring_scratch(quarter, columns)
        + [
            pltpu.VMEM((48, wide), F32),
            pltpu.VMEM((3, 48, inner), F32),
            pltpu.SemaphoreType.DMA((1,)),
        ]
        + sems(12, 3)
        + [pltpu.VMEM((5, 16, columns), F32), pltpu.VMEM((10, 16, columns), F32)]
        + sems(10)
        + scatter_scratch(n, STEP),
        compiler_params=pltpu.CompilerParams(
            collective_id=call_id, has_side_effects=True, vmem_limit_bytes=56 << 20
        ),
    )(partial, source, base, gain, *small, *grads)


HEAD = 64
PAIR = 128
NEG = -1e30


def rows_at(i, size):
    return pl.ds(pl.multiple_of(i * size, size), size)


def lane_is(shape, index):
    return lax.broadcasted_iota(jnp.int32, shape, len(shape) - 1) == index


def first_head(shape):
    return lax.broadcasted_iota(jnp.int32, shape, len(shape) - 1) < HEAD


def halves_mean(values):
    first = first_head(values.shape)
    low = jnp.sum(jnp.where(first, values, 0.0), axis=1, keepdims=True) * (1.0 / HEAD)
    high = jnp.sum(jnp.where(first, 0.0, values), axis=1, keepdims=True) * (1.0 / HEAD)
    return low, high


def one_row(ref, index):
    rows = ref[...]
    picked = lax.broadcasted_iota(jnp.int32, rows.shape, 0) == index
    return jnp.sum(jnp.where(picked, rows, 0.0), axis=0, keepdims=True)


def running_sum(values, backward=False):
    count = values.shape[0]
    row = lax.broadcasted_iota(jnp.int32, values.shape, 0)
    shift = 1
    while shift < count:
        if backward:
            moved = jnp.where(row < count - shift, pltpu.roll(values, count - shift, 0), 0.0)
        else:
            moved = jnp.where(row >= shift, pltpu.roll(values, shift, 0), 0.0)
        values = values + moved
        shift *= 2
    return values


def mm(left, right):
    return jnp.dot(left, right, preferred_element_type=F32)


def mm_t(left, right):
    return lax.dot_general(left, right, (((1,), (1,)), ((), ())), preferred_element_type=F32)


def t_mm(left, right):
    return lax.dot_general(left, right, (((0,), (0,)), ((), ())), preferred_element_type=F32)


def whole(shape):
    return pl.BlockSpec(shape, lambda *_: (0,) * len(shape), pipeline_mode=pl.Buffered(1))


def struct(*shape, t=F32):
    return jax.ShapeDtypeStruct(shape, t)


def local_call(kernel, grid, in_specs, out_specs, out_shape, scratch, limit, flops, moved, call_id=None):
    return pl.pallas_call(
        kernel,
        grid_spec=pltpu.PrefetchScalarGridSpec(
            num_scalar_prefetch=1,
            grid=(grid,),
            in_specs=in_specs,
            out_specs=out_specs,
            scratch_shapes=scratch,
        ),
        out_shape=out_shape,
        compiler_params=pltpu.CompilerParams(
            vmem_limit_bytes=limit << 20,
            collective_id=call_id,
            has_side_effects=call_id is not None,
        ),
        cost_estimate=pl.CostEstimate(
            flops=flops * 10**9, bytes_accessed=moved * 10**6, transcendentals=4 * 10**6
        ),
    )


def forward_kernel(
    length_ref, x_ref, gain_ref, wq_ref, wk_ref, wv_ref, wo_ref, wf_ref, bf_ref, w_ref,
    low_ref, qn_ref, kn_ref, v_ref, sig_ref, att_ref, stat_ref, decay_ref, gated_ref, full_ref,
    top_s, row_s, q_s, k_s, w_s, pre_s, gs, ws, wf_s, bf_s, *sem,
):
    step = pl.program_id(0)
    seq = x_ref.shape[0]
    length = length_ref[0]
    here = Place()
    me, right, left, far = (lax.rem(here.my + by, Y) for by in (0, 1, 3, 2))
    sibling, right1, left1, right2, left2 = here.peers()
    c, p1, p2, half = here.c, here.p1, here.p2, seq // 2
    mine = ws.at[c, p2, p1, me]
    cross_order = (p2, here.l2, here.r2, here.o2)

    def plane(j):
        return link(mine, mine, *sem[2:4], j, (here.dp, (right, far, left)[j]))

    def torus(stage, j):
        if stage == 0:
            at, spots, to = (lambda p: ws.at[c, p2, p]), (p1, here.l1, here.r1), (right1, left1)
        else:
            at, spots, to = (lambda p: ws.at[c, p]), (p2, here.l2, here.r2), (right2, left2)
        spot, part, side = ((0, 0, 0), (0, 1, 0), (0, 0, 1), (0, 1, 1), (1, 0, 0), (2, 1, 1))[j]
        piece = at(spots[spot]).at[2 * part : 2 * part + 2]
        return link(piece, piece, *sem[4 + 2 * stage : 6 + 2 * stage], j, to[side])

    def cross(j):
        piece = ws.at[c, cross_order[j]]
        return link(piece, piece, *sem[8:10], j, sibling)

    def gate(pair, j):
        owner, part, to = (
            (me, 0, right), (me, 1, right), (me, 0, left), (me, 1, left), (left, 0, right), (right, 1, left)
        )[j]
        piece = gs.at[pair, owner, part * half : part * half + half]
        return link(piece, piece, *sem[0:2], pair * 6 + j, (here.dp, to))

    def pass_on(make):
        make(0).wait_recv()
        make(4).start()
        make(3).wait_recv()
        make(5).start()

    def arrived(make):
        for j in (1, 2, 4, 5):
            make(j).wait_recv()

    @pl.when(step == 0)
    def _():
        tall, wide = ws.shape[4], ws.shape[5]
        two = w_ref[
            pl.ds(pl.multiple_of(here.chip // 2 * (2 * tall), 16), 2 * tall),
            pl.ds(pl.multiple_of(c * wide, 128), wide),
        ].astype(F32)
        mine[...] = jnp.where(lax.rem(here.chip, 2) == 0, two[0:tall], two[tall:])
        meet([(here.dp, right), (here.dp, left), (here.dp, far)] + here.peers())
        for j in range(3):
            plane(j).start()

    @pl.when(step == 0)
    def _():
        def norm(i, carry):
            at = rows_at(i, 128)
            x = x_ref[at, :].astype(F32)
            r = lax.rsqrt(jnp.mean(x * x, axis=1, keepdims=True) + EPSILON)
            low_ref[at, :] = (x * r * gain_ref[...].astype(F32)).astype(jnp.bfloat16)
            return carry

        lax.fori_loop(0, seq // 128, norm, 0)
        heads = wf_ref.shape[1]
        wf_s[...] = jnp.zeros_like(wf_s)
        wf_s[:, 0:heads] = wf_ref[...]
        bf_s[...] = jnp.zeros_like(bf_s)
        bf_s[0:1, 0:heads] = bf_ref[...].astype(F32)
        pre = mm(low_ref[...], wf_s[...]) + bf_s[0:1, :]
        fall = jnp.minimum(pre, 0.0) - jnp.log1p(jnp.exp(-jnp.abs(pre)))
        decay = running_sum(fall)
        row = lax.broadcasted_iota(jnp.int32, decay.shape, 0)
        final = jnp.sum(jnp.where(row == length - 1, decay, 0.0), axis=0, keepdims=True)
        decay_ref[0] = decay
        decay_ref[1] = jax.nn.sigmoid(-pre)
        top_s[...] = jnp.where(row < length, decay, final)
        row_s[...] = jnp.where(row < length, decay, -NEG).T[0:8]

    for j, ref in enumerate((wq_ref, wk_ref, wv_ref, wo_ref)):
        w_s[:, j * PAIR : j * PAIR + PAIR] = ref[...]
    pre_s[...] = mm(low_ref[...], w_s[...])

    def norms(i, carry):
        at = rows_at(i, 128)
        for j, n_ref, s, col in ((0, qn_ref, q_s, 0), (1, kn_ref, k_s, 2)):
            pre = pre_s[at, j * PAIR : j * PAIR + PAIR]
            a, b = halves_mean(pre * pre)
            a, b = lax.rsqrt(a + EPSILON), lax.rsqrt(b + EPSILON)
            n = pre * jnp.where(first_head(pre.shape), a, b)
            n_ref[at, :] = n
            s[at, :] = n.astype(jnp.bfloat16)
            here = jnp.where(lane_is(pre.shape, col), a, jnp.where(lane_is(pre.shape, col + 1), b, 0.0))
            stat_ref[at, :] = here if col == 0 else stat_ref[at, :] + here
        v_ref[at, :] = pre_s[at, 2 * PAIR : 3 * PAIR].astype(jnp.bfloat16)
        sig_ref[at, :] = jax.nn.sigmoid(pre_s[at, 3 * PAIR : 4 * PAIR])
        return carry

    lax.fori_loop(0, seq // 128, norms, 0)

    @pl.when(step == 0)
    def _():
        for j in range(3):
            plane(j).wait_recv()
        for j in range(4):
            torus(0, j).start()

    @pl.when(step == 1)
    def _():
        arrived(lambda j: torus(0, j))
        for j in range(4):
            torus(1, j).start()
        cross(0).start()

    @pl.when(step == 2)
    def _():
        pass_on(lambda j: torus(1, j))

    lines = [one_row(row_s, 2 * step + head) for head in (0, 1)]
    first = first_head((128, PAIR))
    zero = jnp.zeros((128, PAIR), jnp.bfloat16)
    upper = lax.broadcasted_iota(jnp.int32, (128, 128), 1) > lax.broadcasted_iota(
        jnp.int32, (128, 128), 0
    )
    for i in range(seq // 128):
        at, n = slice(i * 128, i * 128 + 128), i * 128 + 128
        q = q_s[at, :]
        both = []
        for head in (0, 1):
            own = jnp.where(first, q, zero) if head == 0 else jnp.where(first, zero, q)
            s = mm_t(own, k_s[0:n, :])
            column = jnp.sum(
                jnp.where(lane_is((128, PAIR), 2 * step + head), top_s[at, :], 0.0), axis=1, keepdims=True
            )
            s = s * (HEAD ** (-0.5)) + (column - lines[head][:, 0:n])
            diagonal = jnp.where(upper, NEG, s[:, n - 128 :])
            s = diagonal if i == 0 else jnp.concatenate([s[:, : n - 128], diagonal], axis=1)
            p = jnp.exp(s)
            p = p * (1.0 / jnp.sum(p, axis=1, keepdims=True))
            both.append(mm(p.astype(jnp.bfloat16), v_ref[0:n, :]))
        out = jnp.where(first, both[0], both[1])
        att_ref[at, :] = out
        gs[step, me, at, :] = (out * sig_ref[at, :]).astype(jnp.bfloat16).astype(F32)
    for j in range(4):
        gate(step, j).start()

    @pl.when(step == 0)
    def _():
        pass_on(lambda j: torus(0, j))

    @pl.when(step > 0)
    def _():
        pass_on(lambda j: gate(step - 1, j))

    @pl.when(step == pl.num_programs(0) - 1)
    def _():
        torus(1, 1).wait_recv()
        cross(1).start()
        torus(1, 2).wait_recv()
        cross(2).start()
        torus(1, 4).wait_recv()
        torus(1, 5).wait_recv()
        cross(3).start()
        pass_on(lambda j: gate(step, j))
        for j in range(4):
            cross(j).wait_recv()
        tall, wide, shard = ws.shape[4], ws.shape[5], w_ref.shape[0]

        def turn(k, carry):
            y, m = k // 8, lax.rem(k, 8)
            x, z = m // 2, lax.rem(m, 2) * 2
            rows = pl.ds(pl.multiple_of(y * shard + m * 2 * tall, 16), 2 * tall)
            for h, one, two in (
                (0, ws[0, z, x, y], ws[0, z + 1, x, y]),
                (1, ws[1, x, z, y], ws[1, x, z + 1, y]),
            ):
                both = jnp.concatenate([one, two], axis=0).astype(jnp.bfloat16)
                full_ref[rows, h * wide : h * wide + wide] = both
            return carry

        lax.fori_loop(0, 8 * Y, turn, 0)
        pairs = gs.shape[0]
        for pair in range(pairs):
            arrived(lambda j: gate(pair, j))
            for y in range(Y):
                lane = (y * pairs + pair) * PAIR
                gated_ref[:, lane : lane + PAIR] = gs[pair, y].astype(jnp.bfloat16)
        for j in range(3):
            plane(j).wait_send()
        for stage in (0, 1):
            for j in range(6):
                torus(stage, j).wait_send()
        for j in range(4):
            cross(j).wait_send()
        for pair in range(pairs):
            for j in range(6):
                gate(pair, j).wait_send()


def forward_attention(tokens, length, gain, wq, wk, wv, wo, wf, bf, w_out, call_id):
    seq, width = tokens.shape
    heads = wq.shape[1]
    weights = pl.BlockSpec((width, PAIR), lambda i, _: (0, i))
    lanes = pl.BlockSpec((seq, PAIR), lambda i, _: (0, i))
    low = jnp.bfloat16
    return local_call(
        forward_kernel,
        heads // PAIR,
        [whole((seq, width)), whole((1, width))] + [weights] * 4 + [whole(wf.shape), whole(bf.shape), whole(w_out.shape)],
        [whole((seq, width))] + [lanes] * 6 + [whole((2, seq, PAIR)), whole((seq, width)), whole((width, width))],
        [
            struct(seq, width, t=low), struct(seq, heads), struct(seq, heads), struct(seq, heads, t=low),
            struct(seq, heads), struct(seq, heads), struct(seq, heads),
            struct(2, seq, PAIR), struct(seq, heads * Y, t=low), struct(heads * Y, width, t=low),
        ],
        [
            pltpu.VMEM((seq, PAIR), F32),
            pltpu.VMEM((8, seq), F32),
            pltpu.VMEM((seq, PAIR), low),
            pltpu.VMEM((seq, PAIR), low),
            pltpu.VMEM((width, 4 * PAIR), low),
            pltpu.VMEM((seq, 4 * PAIR), F32),
            pltpu.VMEM((heads // PAIR, Y, seq, PAIR), F32),
            pltpu.VMEM((2, 4, 4, Y, heads // 16, width // 2), F32),
            pltpu.VMEM((width, PAIR), low),
            pltpu.VMEM((8, PAIR), F32),
        ]
        + sems(6 * (heads // PAIR), 3, 6, 6, 4),
        56, 6, 20, call_id,
    )(length, tokens, gain, wq, wk, wv, wo, wf, bf, w_out)


def mlp_forward_kernel(
    length_ref, x_ref, cot_ref, gated_ref, gain_ref, wo_ref, wg_ref, wu_ref, wd_ref,
    mid_ref, low_ref, grad_ref, gate_ref, up_ref, hid_ref, out_ref, sums_ref,
    all_s,
):
    step = pl.program_id(0)
    seq = x_ref.shape[0]
    length = length_ref[0]
    tile, units = wo_ref.shape[1], wg_ref.shape[1]

    @pl.when(step < 2)
    def _():
        at = pl.ds(pl.multiple_of(step * tile, tile), tile)
        branch = mm(gated_ref[...], wo_ref[...])
        x = x_ref[:, at].astype(F32)
        mid_ref[:, at] = x + branch
        kept = lax.broadcasted_iota(jnp.int32, (seq, 1), 0) < length
        grad_ref[:, at] = jnp.where(kept, cot_ref[:, at].astype(F32), 0.0).astype(jnp.bfloat16)
        sums_ref[0:1, at] = jnp.sum(jnp.where(kept, x * x, 0.0), axis=0, keepdims=True)
        sums_ref[1:2, at] = jnp.sum(jnp.where(kept, branch * branch, 0.0), axis=0, keepdims=True)

    @pl.when(step == 2)
    def _():
        def norm(i, carry):
            at = rows_at(i, 128)
            mid = mid_ref[at, :]
            r = lax.rsqrt(jnp.mean(mid * mid, axis=1, keepdims=True) + EPSILON)
            low_ref[at, :] = (mid * r * gain_ref[...].astype(F32)).astype(jnp.bfloat16)
            return carry

        lax.fori_loop(0, seq // 128, norm, 0)

    @pl.when((step == 2) | (step == 3))
    def _():
        at = pl.ds(pl.multiple_of((step - 2) * units, units), units)
        gate_ref[...] = mm(low_ref[...], wg_ref[...])
        up_ref[...] = mm(low_ref[...], wu_ref[...])
        gate = gate_ref[...]
        hid = (gate * jax.nn.sigmoid(gate) * up_ref[...]).astype(jnp.bfloat16)
        hid_ref[...] = hid
        all_s[:, at] = hid

    @pl.when(step > 3)
    def _():
        out_ref[...] = mm(all_s[...], wd_ref[...])


def mlp_forward(tokens, cotangent, length, gated, gain, wo, wg, wu, wd):
    seq, width = tokens.shape
    hidden = wg.shape[1]
    tile, units = width // 2, hidden // 2
    low = jnp.bfloat16
    stage = lambda first: (lambda i, _: (0, jnp.clip(i - first, 0, 1)))
    columns = pl.BlockSpec((width, units), stage(2))
    values = pl.BlockSpec((seq, units), stage(2))
    full = whole((seq, width))
    return local_call(
        mlp_forward_kernel,
        6,
        [full, full, full, whole((1, width)), pl.BlockSpec((width, tile), stage(0)), columns, columns]
        + [pl.BlockSpec((hidden, tile), stage(4))],
        [full, full, full, values, values, values, pl.BlockSpec((seq, tile), stage(4)), whole((2, width))],
        [
            struct(seq, width), struct(seq, width, t=low), struct(seq, width, t=low),
            struct(seq, hidden), struct(seq, hidden),
            struct(seq, hidden, t=low), struct(seq, width), struct(2, width),
        ],
        [pltpu.VMEM((seq, hidden), low)],
        56, 11, 40,
    )(length, tokens, cotangent, gated, gain, wo, wg, wu, wd)


def reduce_links(rows, x, opp, nbr, held, sem):
    dp, me = lax.axis_index("dp"), lax.axis_index("mp")
    right, left, far = lax.rem(me + 1, Y), lax.rem(me + 3, Y), lax.rem(me + 2, Y)
    q, h = rows // Y, rows // Y // 2

    def message(name):
        src, dst, to = {
            "oR": (lambda: rows_of(x, far * q, h), lambda: opp.at[0], right),
            "oL": (lambda: rows_of(x, far * q + h, h), lambda: opp.at[1], left),
            "iR": (lambda: rows_of(x, right * q + h, h), lambda: nbr.at[0, h:q], right),
            "iL": (lambda: rows_of(x, left * q, h), lambda: nbr.at[1, 0:h], left),
            "dR": (lambda: held.at[0], lambda: nbr.at[0, 0:h], right),
            "dL": (lambda: held.at[1], lambda: nbr.at[1, h:q], left),
        }[name]
        return link(src(), dst(), *sem, STEPS.index(name), (dp, to))

    return message, me, right, left, [(dp, right), (dp, left)]


def mlp_backward_kernel(
    length_ref, grad_ref, low_ref, gate_ref, up_ref, hid_ref, wd_ref, wg_ref, wu_ref, x_ref, mid_ref,
    back_ref, gd_ref, gg_ref, gu_ref, layer_ref, square_ref,
    dg_s, du_s, opp, nbr, held, own_s, mid_s, csem, *sem,
):
    step = pl.program_id(0)
    seq = grad_ref.shape[0]
    units = wd_ref.shape[0]
    low16 = jnp.bfloat16
    message, me, right, left, peers = reduce_links(seq, x_ref, opp, nbr, held, sem)
    q = seq // Y
    h = q // 2

    def fetch(j):
        src, dst = (
            (rows_of(x_ref, right * q, h), held.at[0]),
            (rows_of(x_ref, left * q + h, h), held.at[1]),
            (rows_of(x_ref, me * q, q), own_s),
            (rows_of(mid_ref, me * q, q), mid_s),
        )[j]
        return pltpu.make_async_copy(src, dst, csem.at[j])

    @pl.when(step == 0)
    def _():
        meet(peers)
        for name in STEPS[:4]:
            message(name).start()
        for j in range(4):
            fetch(j).start()

    @pl.when(step == 2)
    def _():
        for j, (come, go) in enumerate((("oR", "dR"), ("oL", "dL"))):
            message(come).wait_recv()
            fetch(j).wait()
            held[j] = held[j] + opp[j]
            message(go).start()

    @pl.when(step < 2)
    def _():
        at = pl.ds(pl.multiple_of(step * units, units), units)
        grad = mm_t(grad_ref[...], wd_ref[...])
        gate = gate_ref[...]
        sig = jax.nn.sigmoid(gate)
        dg_s[:, at] = (grad * up_ref[...] * (sig * (1.0 + gate * (1.0 - sig)))).astype(low16)
        du_s[:, at] = (grad * (gate * sig)).astype(low16)

        def grads(k, carry):
            rows = rows_at(k, 768)
            gd_ref[rows, :] = t_mm(grad_ref[:, rows], hid_ref[...])
            gg_ref[rows, :] = t_mm(low_ref[:, rows], dg_s[:, at])
            gu_ref[rows, :] = t_mm(low_ref[:, rows], du_s[:, at])
            return carry

        lax.fori_loop(0, gd_ref.shape[0] // 768, grads, 0)

    @pl.when(step >= 2)
    def _():
        back_ref[...] = mm_t(dg_s[...], wg_ref[...])
        back_ref[...] = back_ref[...] + mm_t(du_s[...], wu_ref[...])

    @pl.when(step == 3)
    def _():
        fetch(2).wait()
        fetch(3).wait()
        sums = 0.0
        for part, names in enumerate((("dR", "iL"), ("iR", "dL"))):
            for name in names:
                message(name).wait_recv()
            at = slice(part * h, part * h + h)
            branch = own_s[at, :] + nbr[0, at] + nbr[1, at]
            layer_ref[at, :] = (mid_s[at, :] + branch).astype(low16).astype(F32)
            row = lax.broadcasted_iota(jnp.int32, (h, 1), 0) + (me * q + part * h)
            kept = jnp.where(row < length_ref[0], branch * branch, 0.0)
            sums = sums + jnp.sum(kept, axis=0, keepdims=True)
        square_ref[...] = sums
        for name in STEPS[:6]:
            message(name).wait_send()


def mlp_backward(length, grad, low, gate, up, hid, wg, wu, wd, branch, mid, call_id):
    seq, width = low.shape
    hidden = wg.shape[1]
    tile, units, quarter = width // 2, hidden // 2, seq // Y
    stage = lambda first: (lambda i, _: (0, jnp.clip(i - first, 0, 1)))
    down = lambda first: (lambda i, _: (jnp.clip(i - first, 0, 1), 0))
    values = pl.BlockSpec((seq, units), stage(0))
    grads = pl.BlockSpec((width, units), stage(0))
    weights = pl.BlockSpec((tile, hidden), down(2))
    full, hbm = whole((seq, width)), pl.BlockSpec(memory_space=pl.ANY)
    return local_call(
        mlp_backward_kernel,
        4,
        [full, full, values, values, values, pl.BlockSpec((units, width), down(0)), weights, weights, hbm, hbm],
        [pl.BlockSpec((seq, tile), stage(2)), grads, grads, grads, whole((quarter, width)), whole((1, width))],
        [struct(seq, width)] + [struct(width, hidden)] * 3 + [struct(quarter, width), struct(1, width)],
        [pltpu.VMEM((seq, hidden), jnp.bfloat16)] * 2
        + ring_scratch(quarter, width)
        + [pltpu.VMEM((quarter, width), F32)] * 2
        + [pltpu.SemaphoreType.DMA((4,))]
        + sems(6),
        62, 13, 60, call_id,
    )(length, grad, low, gate, up, hid, wd, wg, wu, branch, mid)


def backward_kernel(
    length_ref, gg_ref, low_ref, qn_ref, kn_ref, v_ref, sig_ref, att_ref, stat_ref,
    decay_ref, wq_ref, wk_ref, wv_ref, wo_ref, wf_ref, own_ref, gated_ref, layer_ref,
    back_ref, four_ref, gout_ref, gf_ref, bias_ref, out_ref,
    k_s, do_s, line_s, dq_s, dk_s, dv_s, all_s, fall_s, w_s, wf_s, lay_s, *sem,
):
    step = pl.program_id(0)
    seq, width = low_ref.shape
    length = length_ref[0]
    low16 = jnp.bfloat16
    wide = 4 * PAIR
    dp, me = lax.axis_index("dp"), lax.axis_index("mp")
    right, left = lax.rem(me + 1, Y), lax.rem(me + 3, Y)
    q, h = seq // Y, seq // Y // 2

    def spread(j):
        owner, part, to = (
            (me, 0, right), (me, 1, right), (me, 0, left), (me, 1, left), (left, 0, right), (right, 1, left)
        )[j]
        piece = rows_of(lay_s, owner * q + part * h, h)
        return link(piece, piece, *sem, j, (dp, to))

    @pl.when(step == 0)
    def _():
        rows_of(lay_s, me * q, q)[...] = layer_ref[...]
        meet([(dp, right), (dp, left)])
        for j in range(4):
            spread(j).start()

    @pl.when(step == 1)
    def _():
        spread(0).wait_recv()
        spread(4).start()
        spread(3).wait_recv()
        spread(5).start()

    @pl.when(step == 0)
    def _():
        heads = wf_ref.shape[1]
        wf_s[...] = jnp.zeros_like(wf_s)
        wf_s[:, 0:heads] = wf_ref[...]
        decay = decay_ref[0]
        row = lax.broadcasted_iota(jnp.int32, decay.shape, 0)
        final = jnp.sum(jnp.where(row == length - 1, decay, 0.0), axis=0, keepdims=True)
        line_s[...] = jnp.where(row < length, decay, final).T[0:8]
        fall_s[...] = jnp.zeros_like(fall_s)

    base = pl.multiple_of(step * wide, wide)
    part = lambda j: pl.ds(pl.multiple_of(base + j * PAIR, PAIR), PAIR)
    for j, w_ref in enumerate((wq_ref, wk_ref, wv_ref, wo_ref)):
        w_s[:, part(j)] = w_ref[...]
    first = first_head((seq, PAIR))
    gg, sig = gg_ref[...], sig_ref[...]
    do_s[...] = (gg * sig).astype(low16)
    all_s[:, part(3)] = (gg * att_ref[...] * sig * (1.0 - sig)).astype(low16)
    k_s[...] = kn_ref[...].astype(low16)
    dk_s[...] = jnp.zeros_like(dk_s)
    dv_s[...] = jnp.zeros_like(dv_s)
    row = lax.broadcasted_iota(jnp.int32, (seq, PAIR), 0)
    columns, lines = [], [one_row(line_s, 2 * step + head) for head in (0, 1)]
    for head in (0, 1):
        column = jnp.sum(
            jnp.where(lane_is((seq, PAIR), 2 * step + head), decay_ref[0], 0.0), axis=1, keepdims=True
        )
        columns.append(jnp.where(row[:, 0:1] < length, column, -NEG))
    block = first_head((128, PAIR))
    zero = jnp.zeros((128, PAIR), low16)
    lower = lax.broadcasted_iota(jnp.int32, (128, 128), 0) > lax.broadcasted_iota(
        jnp.int32, (128, 128), 1
    )
    for i in range(seq // 128):
        at, n = slice(i * 128, i * 128 + 128), i * 128 + 128
        query = qn_ref[at, :].astype(low16)
        do = do_s[at, :]
        pieces = []
        for head in (0, 1):
            pick = (lambda t: jnp.where(block, t, zero)) if head == 0 else (lambda t: jnp.where(block, zero, t))
            own_q, own_do = pick(query), pick(do)
            one = jnp.where(lane_is((128, PAIR), 2 * step + head), 1.0, 0.0).astype(low16)
            s = mm_t(k_s[0:n, :], own_q)
            s = s * (HEAD ** (-0.5)) + (lines[head][:, at] - columns[head][0:n])
            diagonal = jnp.where(lower, NEG, s[n - 128 :, :])
            s = diagonal if i == 0 else jnp.concatenate([s[: n - 128, :], diagonal], axis=0)
            p = jnp.exp(s)
            p = p * (1.0 / jnp.sum(p, axis=0, keepdims=True))
            gp = mm_t(v_ref[0:n, :], own_do)
            ds = (p * (gp - jnp.sum(p * gp, axis=0, keepdims=True))).astype(low16)
            dv_s[0:n, :] = dv_s[0:n, :] + mm(p.astype(low16), own_do)
            dk_s[0:n, :] = dk_s[0:n, :] + mm(ds, jnp.concatenate([own_q, one], axis=1))
            mark = jnp.where(lane_is((n, PAIR), 2 * step + head), 1.0, 0.0).astype(low16)
            pieces.append(t_mm(ds, jnp.concatenate([k_s[0:n, :], mark], axis=1)))
        dq_s[at, :] = jnp.where(block, pieces[0][:, 0:PAIR], pieces[1][:, 0:PAIR])
        fall_s[at, :] = fall_s[at, :] + pieces[0][:, PAIR:] + pieces[1][:, PAIR:]
    fall_s[...] = fall_s[...] - dk_s[:, PAIR:]
    stat = stat_ref[...]
    for e, n_ref, col, to in ((dq_s, qn_ref, 0, 0), (dk_s, kn_ref, 2, 1)):
        e = e[:, 0:PAIR] * (HEAD ** (-0.5))
        n = n_ref[...]
        a, b = halves_mean(e * n)
        r = jnp.where(first, stat[:, col : col + 1], stat[:, col + 1 : col + 2])
        all_s[:, part(to)] = (r * (e - n * jnp.where(first, a, b))).astype(low16)
    all_s[:, part(2)] = dv_s[...].astype(low16)

    def grads(k, carry):
        rows = rows_at(k, 768)
        four_ref[rows, :] = t_mm(low_ref[:, rows], all_s[:, pl.ds(base, wide)])
        gout_ref[rows, :] = t_mm(own_ref[:, rows].astype(low16), gated_ref[...])
        return carry

    lax.fori_loop(0, width // 768, grads, 0)

    @pl.when(step == pl.num_programs(0) - 1)
    def _():
        fall = running_sum(fall_s[...], backward=True) * decay_ref[1]
        fall = fall.astype(low16)
        bias_ref[...] = jnp.sum(fall.astype(F32), axis=0, keepdims=True)
        gf_ref[...] = t_mm(fall, low_ref[...])[0:8]

        def tail(k, carry):
            rows = rows_at(k, 768)
            back_ref[:, rows] = mm_t(all_s[...], w_s[rows, :])
            back_ref[:, rows] = back_ref[:, rows] + mm_t(fall, wf_s[rows, :])
            return carry

        lax.fori_loop(0, width // 768, tail, 0)
        for j in (1, 2, 4, 5):
            spread(j).wait_recv()
        out_ref[...] = lay_s[...].astype(low16)
        for j in range(6):
            spread(j).wait_send()


def backward_attention(place, gg, low, qn, kn, v, sig, att, stat, decay, wq, wk, wv, wo, wf, own, gated, layer, call_id):
    seq, width = low.shape
    heads = wq.shape[1]
    weights = pl.BlockSpec((width, PAIR), lambda i, _: (0, i))
    lanes = pl.BlockSpec((seq, PAIR), lambda i, _: (0, i))
    wide = pl.BlockSpec((width, 4 * PAIR), lambda i, _: (0, i))
    full = whole((seq, width))
    low16 = jnp.bfloat16
    return local_call(
        backward_kernel,
        heads // PAIR,
        [lanes, full] + [lanes] * 6 + [whole((2, seq, PAIR))] + [weights] * 4
        + [whole(wf.shape), whole(own.shape)]
        + [pl.BlockSpec((own.shape[0], 4 * PAIR), lambda i, _: (lax.axis_index("mp"), i)), whole(layer.shape)],
        [full, wide, wide, whole((8, width)), whole((1, PAIR)), full],
        [
            struct(seq, width), struct(width, 4 * heads), struct(width, width), struct(8, width),
            struct(1, PAIR), struct(seq, width, t=low16),
        ],
        [
            pltpu.VMEM((seq, PAIR), low16),
            pltpu.VMEM((seq, PAIR), low16),
            pltpu.VMEM((8, seq), F32),
            pltpu.VMEM((seq, PAIR), F32),
            pltpu.VMEM((seq, 2 * PAIR), F32),
            pltpu.VMEM((seq, PAIR), F32),
            pltpu.VMEM((seq, 4 * heads), low16),
            pltpu.VMEM((seq, PAIR), F32),
            pltpu.VMEM((width, 4 * heads), low16),
            pltpu.VMEM((width, PAIR), low16),
            pltpu.VMEM((seq, width), F32),
        ]
        + sems(6),
        60, 14, 50, call_id,
    )(place, gg, low, qn, kn, v, sig, att, stat, decay, wq, wk, wv, wo, wf, own, gated, layer)


def finish_kernel(
    grad_in, layer_in, wout_in, four_in, mlp_in,
    grad_ref, layer_ref, wout_ref, q_ref, k_ref, v_ref, o_ref, gate_ref, up_ref, down_ref,
    sem,
):
    rows = grad_in.shape[0] // 4
    copies = []
    for j in range(4):
        for src, dst, at in ((grad_in, grad_ref, j), (layer_in, layer_ref, 4 + j)):
            part = slice(j * rows, j * rows + rows)
            copies.append(load(src.at[part], dst.at[part], sem.at[at]))
    wout_ref[...] = wout_in[...].T
    for j, ref in enumerate((q_ref, k_ref, v_ref, o_ref)):
        for pair in range(q_ref.shape[1] // PAIR):
            lane = (pair * 4 + j) * PAIR
            ref[:, pair * PAIR : pair * PAIR + PAIR] = four_in[:, lane : lane + PAIR]
    units = gate_ref.shape[1]
    down_ref[...] = mlp_in[:, 0:units].T
    gate_ref[...] = mlp_in[:, units : 2 * units]
    up_ref[...] = mlp_in[:, 2 * units : 3 * units]
    for copy in copies:
        copy.wait()


def finish(grad, layer, out_share, share, mlp_share):
    rows, inner = out_share.shape
    units = mlp_share.shape[1] // 3
    hbm, vmem = pl.BlockSpec(memory_space=pl.ANY), pl.BlockSpec(memory_space=pltpu.VMEM)
    return pl.pallas_call(
        finish_kernel,
        out_shape=[
            struct(*grad.shape), struct(*layer.shape, t=layer.dtype), struct(inner, rows),
            *[struct(rows, inner)] * 4, struct(rows, units), struct(rows, units), struct(units, rows),
        ],
        in_specs=[hbm, hbm, vmem, vmem, vmem],
        out_specs=[hbm, hbm] + [vmem] * 8,
        scratch_shapes=[pltpu.SemaphoreType.DMA((8,))],
        compiler_params=pltpu.CompilerParams(vmem_limit_bytes=16 << 20),
    )(grad, layer, out_share, share, mlp_share)


def per_device(
    tokens, lengths, buckets, out_cotangent, gain_attn, w_query, w_key, w_value, w_outgate,
    w_forget, b_forget, w_out, gain_mlp, w_gate, w_up, w_down,
):
    x, cotangent = tokens[0], out_cotangent[0]
    model_width = x.shape[1]
    heads = w_forget.shape[1]
    gain_in, gain_mid = gain_attn[None], gain_mlp[None]
    weights = (w_query, w_key, w_value, w_outgate, w_forget)
    low, qn, kn, value, sig, attended, stat, decay, gated, w_full = forward_attention(
        x, lengths, gain_in, *weights, b_forget[None], w_out, 0
    )
    middle, mid_low, grad_rows, gate, up, hidden, mlp_local, squares = mlp_forward(
        x, cotangent, lengths, gated, gain_mid, w_full, w_gate, w_up, w_down
    )
    mid_local, g_down, g_gate, g_up, layer_own, mlp_square = mlp_backward(
        lengths, grad_rows, mid_low, gate, up, hidden, w_gate, w_up, w_down, mlp_local, middle, 1
    )
    grad_own, gg, mlp_share, mlp_gain = reduce_middle(
        mid_local, middle, grad_rows, gain_mid, w_full, [g_down, g_gate, g_up], 2
    )
    in_local, g_four, g_out, g_fall, bias, layer_out = backward_attention(
        lengths, gg, low, qn, kn, value, sig, attended, stat, decay, *weights, grad_own, gated,
        layer_own, 3,
    )
    bucket_hot = (buckets[0] == jnp.arange(NBUCKET)).astype(F32)
    square_sums = jnp.concatenate([squares, mlp_square]).sum(axis=1)
    misc = jnp.stack([square_sums[0], square_sums[1], lengths[0].astype(F32), square_sums[2]])
    misc = misc[:, None] * bucket_hot[None, :]
    misc = jnp.stack([misc[:3].reshape(-1), jnp.pad(misc[3], (0, 2 * NBUCKET))])
    misc = jnp.pad(misc, ((0, 0), (0, PAIR - 3 * NBUCKET)))
    input_grad, out_share, share, sums = reduce_input(
        in_local, x, grad_own, gain_in, (mlp_gain, g_fall, misc, bias), [g_out, g_four], 4
    )
    input_grad, layer_out, g_out, g_query, g_key, g_value, g_outgate, g_gate, g_up, g_down = finish(
        input_grad, layer_out, out_share, share, mlp_share
    )
    totals = jnp.stack([sums[9, :NBUCKET], sums[9, NBUCKET : 2 * NBUCKET], sums[2, :NBUCKET]])
    rms = jnp.sqrt(totals / (sums[9, 2 * NBUCKET : 3 * NBUCKET] * model_width)[None, :])
    rows = model_width // lax.axis_size("dp")
    mine = lax.dynamic_slice_in_dim(sums[:9], lax.axis_index("dp") * rows, rows, axis=1)
    return (
        layer_out[None],
        input_grad[None],
        mine[0],
        g_query,
        g_key,
        g_value,
        g_outgate,
        mine[3 : 3 + heads].T,
        sums[10, :heads],
        g_out,
        mine[1],
        g_gate,
        g_up,
        g_down,
        rms,
    )


def solution(mesh):
    placed = (
        P("dp", None, None),
        P("dp"),
        P("dp"),
        P("dp", None, None),
        P(),
        P(None, "mp"),
        P(None, "mp"),
        P(None, "mp"),
        P(None, "mp"),
        P(None, "mp"),
        P("mp"),
        P("mp", None),
        P(),
        P(None, "mp"),
        P(None, "mp"),
        P("mp", None),
    )
    return jax.shard_map(
        per_device,
        mesh=mesh,
        in_specs=placed,
        out_specs=(
            P("dp", None, None),
            P("dp", None, None),
            P("dp"),
            P("dp", "mp"),
            P("dp", "mp"),
            P("dp", "mp"),
            P("dp", "mp"),
            P("dp", "mp"),
            P("mp"),
            P("mp", "dp"),
            P("dp"),
            P("dp", "mp"),
            P("dp", "mp"),
            P("mp", "dp"),
            P(),
        ),
        check_vma=False,
    )
```

time: 930 us -> 388 us (0.42); the launches traced: 919 us -> 388 us
  waiting for transfers between devices: 546 us -> 0 us
  Pallas kernels: 0 us -> 368 us
  matrix products: 119 us -> 0 us
  local copies, waits for them, and re-layouts: 90.5 us -> 14 us
  blocking collectives: 69.3 us -> 0 us
  other arithmetic: 72.1 us -> 3.65 us
  between operations: 17.2 us -> 2.06 us
    pallas_call x0 -> x7, Pallas kernels: none -> 368 us  [the longest x1 97 us: reduce_input(): pl.pallas_call(functools.partial(input_kernel, len(grads)), out_shape=[ja...]
    psum x3 -> x0, waiting for transfers between devices: 327 us -> none  [the longest x1 128 us: per_device(): branch_mlp = lax.psum(low_dot(hidden_low, w_down), 'mp')]
    reduce_scatter x2 -> x0, waiting for transfers between devices: 168 us -> none  [the longest x1 90 us: per_device(): lax.psum_scatter(grad_w_down, 'dp', scatter_dimension=1, tiled=True)]
    dot_general x33 -> x0, matrix products: 119 us -> none  [the longest x9 33 us: back_dot(): lax.dot_general(left, right, (((0,), (0,)), ((), ())), preferred_element_...]
    unnamed x1 -> x0, blocking collectives: 69.3 us -> none
    unnamed x9 -> x0, waiting for transfers between devices: 50.8 us -> none
    unnamed x130 -> x17, local copies, waits for them, and re-layouts: 48 us -> 7.52 us
    reduce_sum x8 -> x1, other arithmetic: 38.4 us -> 0.82 us  [per_device(): square_sums = jnp.concatenate([squares, mlp_square]).sum(axis=1)]
  transfers between devices with their start and end apart: 8 -> 0, of which waited for: 6 -> 0; matrix products, arithmetic and copies ran while one was open for 15% -> 0% of each run, Pallas kernels for 0% -> 0%
where the time goes in v3:
time: 388 us
  Pallas kernels  368 us (95%)
  local copies, waits for them, and re-layouts  14 us (4%)
    pallas_call x1, Pallas kernels, reduce_input(): pl.pallas_call(functools.partial(input_kernel, len(grads)), out_shape=[ja...  97 us
    pallas_call x1, Pallas kernels, reduce_middle(): pl.pallas_call(functools.partial(middle_kernel, len(grads)), out_shape=[j...  68 us
    pallas_call x1, Pallas kernels, forward_attention(): local_call(forward_kernel, heads // PAIR, [whole((seq, width)), whole((1,...  64.8 us
    pallas_call x1, Pallas kernels, backward_attention(): local_call(backward_kernel, heads // PAIR, [lanes, full] + [lanes] * 6 +...  57.7 us
    pallas_call x1, Pallas kernels, mlp_backward(): local_call(mlp_backward_kernel, 4, [full, full, values, values, values, p...  51.3 us
    pallas_call x1, Pallas kernels, mlp_forward(): local_call(mlp_forward_kernel, 6, [full, full, full, whole((1, width)), p...  25.6 us

profile of v3, /device:TPU:0, one launch (start us, length us, event | category | flops | bytes accessed | tf_op | source)
XLA Modules:
  0.0 387.9 jit_solution(2501975723889733979)
XLA Ops:
  1.3 1.7 copy.31.wf_ref
  3.0 1.3 broadcast_in_dim.18.gain_ref
  4.3 64.8 %shard_map.271 = (bf16[768,1536]{1,0:T(8,128)(2,1)}, f32[768,384]{1,0:T(8,128)}, f32[768,384]{1,0:T(8,128)}, bf16[768,384]{1,0:T(8,128)(2,1)}, f32[768,384]{1,0:...) custom-call(s32[1]{0:T(128)S(6)} %copy.35.length_ref, ...), custom_call_target="tpu_custom_call" | custom-call | flops 6000000000 | bytes 20000000 | tf_op jit(solution)/shard_map/pallas_call | solution.py:847
  69.1 0.0 copy-done.6
  69.1 0.6 broadcast_in_dim.20.gain_ref
  69.7 25.6 %shard_map.272 = (f32[768,1536]{1,0:T(8,128)}, bf16[768,1536]{1,0:T(8,128)(2,1)}, bf16[768,1536]{1,0:T(8,128)(2,1)}, f32[768,1024]{1,0:T(8,128)}, f32[768,1024]{...) custom-call(s32[1]{0:T(128)S(6)} %copy.35.length_ref, ...), custom_call_target="tpu_custom_call" | custom-call | flops 11000000512 | bytes 40000000 | tf_op jit(solution)/shard_map/pallas_call | solution.py:930
  95.3 0.0 copy-start.5
  95.3 51.3 %shard_map.273 = (f32[768,1536]{1,0:T(8,128)}, f32[1536,1024]{1,0:T(8,128)}, f32[1536,1024]{1,0:T(8,128)}, f32[1536,1024]{1,0:T(8,128)}, f32[192,1536]{1,0:T(8,128)}, /*index=5*/f32[1,1536]{1,0:T(1,128)}) custom-call(s32[1]{0:T(128)S(6)} %copy.35.length_ref, bf16[768,1536]{1,0:T(8,128)(2,1)} %get-tuple-element.65.grad_ref.base_ref, ...), custom_call_target="tpu_custom_call" | custom-call | flops 12999999488 | bytes 60000000 | tf_op jit(solution)/shard_map/pallas_call | solution.py:1055
  146.6 0.0 copy-done.5
  146.6 0.8 maximum_reduce_fusion
  147.4 0.6 slice.42
  148.0 0.7 pad_maximum_fusion
  149.4 0.1 broadcast_multiply_fusion
  149.5 0.1 stack_reshape.3
  149.6 0.6 select_maximum_fusion.misc_ref
  150.2 68.0 %shard_map.274 = (f32[192,1536]{1,0:T(8,128)}, f32[768,384]{1,0:T(8,128)}, f32[48,3072]{1,0:T(8,128)}, f32[1,1536]{1,0:T(1,128)}) custom-call(f32[768,1536]{1,0:T(8,128)} %get-tuple-element.72.x_ref, f32[768,1536]{1,0:T(8,128)} %get-tuple-element.71.mid_ref.source_ref, bf16[768,1536]{1,0:T(8,128)(2,1)} %get-tuple-element.65.grad_ref.base_ref, ...), custom_call_target="tpu_custom_call" | custom-call | tf_op jit(solution)/shard_map/pallas_call | solution.py:418
  218.1 57.7 %shard_map.275 = (f32[768,1536]{1,0:T(8,128)}, f32[1536,1536]{1,0:T(8,128)}, f32[1536,1536]{1,0:T(8,128)}, f32[8,1536]{1,0:T(8,128)}, f32[1,128]{1,0:T(1,128)}, /*index=5*/bf16[768,1536]{1,0:T(8,128)(2,1)}) custom-call(s32[1]{0:T(128)S(6)} %copy.35.length_ref, f32[768,384]{1,0:T(8,128)} %get-tuple-element.76.gg_ref, ...), custom_call_target="tpu_custom_call" | custom-call | flops 14000000000 | bytes 50000000 | tf_op jit(solution)/shard_map/pallas_call | solution.py:1210
  275.8 0.0 copy-start.1
  275.8 0.0 copy-start.2
  275.8 97.0 %shard_map.276 = (f32[768,1536]{1,0:T(8,128)}, f32[48,384]{1,0:T(8,128)}, f32[48,1536]{1,0:T(8,128)}, f32[16,1536]{1,0:T(8,128)}) custom-call(f32[768,1536]{1,0:T(8,128)} %get-tuple-element.87.x_ref, bf16[768,1536]{1,0:T(8,128)(2,1)} %bitcast.26, f32[192,1536]{1,0:T(8,128)} %get-tuple-element.85.own_ref.base_ref, bf16[1,1536]{1,0:T(2,128)(2,1)} %broadcast_in_dim.18.gain_ref, ...), custom_call_target="tpu_custom_call" | custom-call | tf_op jit(solution)/shard_map/pallas_call | solution.py:523
  372.9 0.9 multiply_bitcast_fusion
  373.7 0.6 fusion
  374.3 0.0 copy-done.1
  374.4 2.3 copy-done
  376.7 1.0 copy-done.3
  377.7 0.9 copy-done.4
  378.5 3.8 shard_map.277
  382.4 0.9 copy.34
  383.2 0.7 copy.33
  384.0 1.4 dynamic-slice_bitcast_fusion
  385.3 1.4 dynamic-slice_bitcast_fusion.1
  386.7 1.2 slice_bitcast_fusion
  (8 shorter events, 0.0 us)
Async XLA Ops:
  4.3 64.8 %copy-start.6 = (bf16[1536]{0:T(1024)(128)(2,1)S(1)}, bf16[1536]{0:T(1024)(128)(2,1)}, u32[]{:S(2)}) copy-start(bf16[1536]{0:T(1024)(128)(2,1)} %param.28) | copy-start | bytes 9220
  95.3 51.3 %copy-start.5 = (f32[2,1536]{1,0:T(2,128)S(1)}, f32[2,1536]{1,0:T(2,128)}, u32[]{:S(2)}) copy-start(f32[2,1536]{1,0:T(2,128)} %get-tuple-element.90) | copy-start | bytes 36868
  275.8 98.5 %copy-start.1 = (bf16[768,1536]{1,0:T(8,128)(2,1)S(1)}, bf16[768,1536]{1,0:T(8,128)(2,1)}, u32[]{:S(2)}) copy-start(bf16[768,1536]{1,0:T(8,128)(2,1)} %get-tuple-element.96.layer_in) | copy-start | bytes 7077892
  275.8 98.5 %copy-start.2 = (f32[48,3072]{1,0:T(8,128)S(1)}, f32[48,3072]{1,0:T(8,128)}, u32[]{:S(2)}) copy-start(f32[48,3072]{1,0:T(8,128)} %get-tuple-element.99.mlp_in) | copy-start | bytes 1769476
  374.3 2.3 copy-start
  376.7 1.0 copy-start.3
  377.6 0.9 copy-start.4

commit v4 on v3

--- a/solution.py
+++ b/solution.py
@@ -17,6 +17,8 @@
 F32 = jnp.float32
 Y = 4
 STEP = 512
+HBM = pl.BlockSpec(memory_space=pl.ANY)
+VMEM = pl.BlockSpec(memory_space=pltpu.VMEM)
 STEPS = ("oR", "oL", "iR", "iL", "dR", "dL", "gRa", "gRb", "gLa", "gLb", "fR", "fL")
 
 
@@ -331,8 +333,8 @@
     ]
 
 
-def scatter_sources(refs, step):
-    return [(ref, start, step) for ref in refs for start in range(0, ref.shape[1], step)]
+def scatter_sources(refs, pieces):
+    return [(refs[which], at * STEP, STEP) for which, at in pieces]
 
 
 def norm_back(value, source, base, gain):
@@ -350,12 +352,12 @@
     return copy
 
 
-def middle_kernel(count, x_ref, source_ref, base_ref, gain_ref, w_ref, *refs):
+def middle_kernel(pieces, count, x_ref, source_ref, base_ref, gain_ref, w_ref, *refs):
     ins, refs = refs[:count], refs[count:]
     grad_ref, gg_ref, share_ref, sums_ref = refs[:4]
     source_s, base_s, w_s, opp, nbr, held, blocks, csem, *sem = refs[4:16]
     here, ring = Place(), YRing(x_ref.shape[0], *sem[0:2])
-    total = ScatterSum(here, scatter_sources(ins, STEP), *refs[16:])
+    total = ScatterSum(here, scatter_sources(ins, pieces), *refs[16:])
     n = total.n
     far = (ring.dp, ring.far)
     meet(ring.neighbours() + [far] + here.peers())
@@ -410,13 +412,13 @@
     each(0, n, total.sent)
 
 
-def reduce_middle(partial, source, base, gain, w_full, grads, call_id):
-    n = sum(g.shape[1] for g in grads) // STEP
+def reduce_middle(partial, source, base, gain, w_full, grads, pieces, call_id):
+    n = len(pieces)
     hbm, vmem = pl.BlockSpec(memory_space=pl.ANY), pl.BlockSpec(memory_space=pltpu.VMEM)
     rows, columns = partial.shape
     quarter, inner = rows // Y, w_full.shape[0] // Y
     return pl.pallas_call(
-        functools.partial(middle_kernel, len(grads)),
+        functools.partial(middle_kernel, pieces, len(grads)),
         out_shape=[
             jax.ShapeDtypeStruct((quarter, columns), F32),
             jax.ShapeDtypeStruct((rows, inner), F32),
@@ -440,15 +442,18 @@
     )(partial, source, base, gain, w_full, *grads)
 
 
-def input_kernel(count, x_ref, source_ref, base_ref, gain_ref, other_ref, fall_ref, misc_ref, bias_ref, *refs):
+def input_kernel(
+    pieces, count, x_ref, source_ref, base_ref, gain_ref, other_ref, fall_ref, square_ref, more_ref,
+    bias_ref, length_ref, bucket_ref, *refs
+):
     ins, refs = refs[:count], refs[count:]
     out_ref, out_share_ref, share_ref, sums_ref = refs[:4]
     source_s, opp, nbr, held, wide_s, landed, csem, *sem = refs[4:15]
     bufs, arrived, asem, bsem = refs[15:19]
     here, ring = Place(), YRing(x_ref.shape[0], *sem[0:2])
-    total = ScatterSum(here, scatter_sources(ins, STEP), *refs[19:])
+    total = ScatterSum(here, scatter_sources(ins, pieces), *refs[19:])
     tiny = SmallSum(here, bufs, arrived, asem, bsem)
-    n, first = total.n, ins[0].shape[1] // STEP
+    n, first = total.n, wide_s.shape[1] // STEP
     meet(ring.neighbours() + here.peers() + tiny.far)
     ring.start(x_ref, opp, nbr)
     q, h = ring.quarter, ring.half
@@ -474,13 +479,19 @@
     bufs[0, 1:2, :] = other_ref[...]
     bufs[0, 8:16, :] = jnp.zeros_like(bufs[0, 8:16, :])
     bufs[0, 2:3, :] = jnp.zeros((1, sums_ref.shape[1]), F32)
-    bufs[0, 2:3, 0:PAIR] = misc_ref[1:2, :]
     bufs[0, 3:9, :] = fall_ref[0:6, :]
-    bufs[0, 9:10, 0:PAIR] = misc_ref[0:1, :]
+    lane = lax.broadcasted_iota(jnp.int32, (1, PAIR), 1)
+    both = jnp.sum(square_ref[...], axis=1, keepdims=True)
+    total_of = lambda at, value: jnp.where(lane == bucket_ref[0] + at * NBUCKET, value, 0.0)
+    bufs[0, 2:3, 0:PAIR] = total_of(0, jnp.sum(more_ref[...], axis=1, keepdims=True))
+    bufs[0, 9:10, 0:PAIR] = (
+        total_of(0, both[0:1]) + total_of(1, both[1:2]) + total_of(2, length_ref[0].astype(F32))
+    )
     bufs[0, 10:11, 0:PAIR] = bias_ref[...]
     tiny.send(0)
     each(n - 2, n, total.first_relay)
     each(0, n, total.second)
+    ring.forward(block)
     tiny.take(0)
     tiny.send(1)
     each(0, n, total.second_relay)
@@ -494,7 +505,6 @@
         columns = pl.ds(pl.multiple_of(to * inner, 128), inner)
         swaps.append(push(wide_s.at[:, columns], landed.at[j], *sem[2:4], j, (ring.dp, to)))
     each(first, n, lambda k: total.result(k, share_ref, k - first))
-    ring.forward(block)
     tiny.take(2)
     tiny.send(3)
     own = wide_s[:, pl.ds(pl.multiple_of(ring.me * inner, 128), inner)]
@@ -513,22 +523,23 @@
     each(0, n, total.sent)
 
 
-def reduce_input(partial, source, base, gain, small, grads, call_id):
-    n = sum(g.shape[1] for g in grads) // STEP
+def reduce_input(partial, source, base, gain, small, grads, pieces, call_id):
+    n = len(pieces)
+    smem = pl.BlockSpec(memory_space=pltpu.SMEM)
     hbm, vmem = pl.BlockSpec(memory_space=pl.ANY), pl.BlockSpec(memory_space=pltpu.VMEM)
     rows, columns = partial.shape
     quarter, inner = rows // Y, grads[0].shape[1] // Y
     wide = grads[0].shape[1]
-    shares = sum(g.shape[1] for g in grads[1:])
+    shares = n * STEP - wide
     return pl.pallas_call(
-        functools.partial(input_kernel, len(grads)),
+        functools.partial(input_kernel, pieces, len(grads)),
         out_shape=[
             jax.ShapeDtypeStruct(partial.shape, F32),
             jax.ShapeDtypeStruct((48, inner), F32),
             jax.ShapeDtypeStruct((48, shares), F32),
             jax.ShapeDtypeStruct((16, columns), F32),
         ],
-        in_specs=[vmem, hbm, vmem, vmem] + [vmem] * 4 + [hbm] * len(grads),
+        in_specs=[vmem, hbm, vmem, vmem] + [vmem] * 5 + [smem] * 2 + [hbm] * len(grads),
         out_specs=[vmem] * 4,
         scratch_shapes=[pltpu.VMEM((quarter, columns), source.dtype)]
         + ring_scratch(quarter, columns)
@@ -635,8 +646,8 @@
 
 def forward_kernel(
     length_ref, x_ref, gain_ref, wq_ref, wk_ref, wv_ref, wo_ref, wf_ref, bf_ref, w_ref,
-    low_ref, qn_ref, kn_ref, v_ref, sig_ref, att_ref, stat_ref, decay_ref, gated_ref, full_ref,
-    top_s, row_s, q_s, k_s, w_s, pre_s, gs, ws, wf_s, bf_s, *sem,
+    low_out, qn_ref, kn_ref, v_ref, sig_ref, att_ref, stat_ref, decay_ref, gated_out, full_out,
+    top_s, row_s, q_s, k_s, w_s, pre_s, gs, ws, wf_s, bf_s, low_ref, gated_ref, full_ref, osem, *sem,
 ):
     step = pl.program_id(0)
     seq = x_ref.shape[0]
@@ -670,6 +681,10 @@
         )[j]
         piece = gs.at[pair, owner, part * half : part * half + half]
         return link(piece, piece, *sem[0:2], pair * 6 + j, (here.dp, to))
+
+    def flush(j):
+        src, dst = ((low_ref, low_out), (full_ref, full_out), (gated_ref, gated_out))[j]
+        return pltpu.make_async_copy(src, dst, osem.at[j])
 
     def pass_on(make):
         make(0).wait_recv()
@@ -703,12 +718,13 @@
             return carry
 
         lax.fori_loop(0, seq // 128, norm, 0)
-        heads = wf_ref.shape[1]
+        flush(0).start()
+        heads = wf_ref.shape[0]
         wf_s[...] = jnp.zeros_like(wf_s)
-        wf_s[:, 0:heads] = wf_ref[...]
+        wf_s[0:heads, :] = wf_ref[...]
         bf_s[...] = jnp.zeros_like(bf_s)
         bf_s[0:1, 0:heads] = bf_ref[...].astype(F32)
-        pre = mm(low_ref[...], wf_s[...]) + bf_s[0:1, :]
+        pre = mm_t(low_ref[...], wf_s[...]) + bf_s[0:1, :]
         fall = jnp.minimum(pre, 0.0) - jnp.log1p(jnp.exp(-jnp.abs(pre)))
         decay = running_sum(fall)
         row = lax.broadcasted_iota(jnp.int32, decay.shape, 0)
@@ -820,13 +836,16 @@
             return carry
 
         lax.fori_loop(0, 8 * Y, turn, 0)
+        flush(1).start()
         pairs = gs.shape[0]
         for pair in range(pairs):
             arrived(lambda j: gate(pair, j))
             for y in range(Y):
                 lane = (y * pairs + pair) * PAIR
                 gated_ref[:, lane : lane + PAIR] = gs[pair, y].astype(jnp.bfloat16)
+        flush(2).start()
         for j in range(3):
+            flush(j).wait()
             plane(j).wait_send()
         for stage in (0, 1):
             for j in range(6):
@@ -848,7 +867,7 @@
         forward_kernel,
         heads // PAIR,
         [whole((seq, width)), whole((1, width))] + [weights] * 4 + [whole(wf.shape), whole(bf.shape), whole(w_out.shape)],
-        [whole((seq, width))] + [lanes] * 6 + [whole((2, seq, PAIR)), whole((seq, width)), whole((width, width))],
+        [HBM] + [lanes] * 6 + [whole((2, seq, PAIR)), HBM, HBM],
         [
             struct(seq, width, t=low), struct(seq, heads), struct(seq, heads), struct(seq, heads, t=low),
             struct(seq, heads), struct(seq, heads), struct(seq, heads),
@@ -863,83 +882,131 @@
             pltpu.VMEM((seq, 4 * PAIR), F32),
             pltpu.VMEM((heads // PAIR, Y, seq, PAIR), F32),
             pltpu.VMEM((2, 4, 4, Y, heads // 16, width // 2), F32),
-            pltpu.VMEM((width, PAIR), low),
+            pltpu.VMEM((PAIR, width), low),
             pltpu.VMEM((8, PAIR), F32),
+            pltpu.VMEM((seq, width), low),
+            pltpu.VMEM((seq, width), low),
+            pltpu.VMEM((heads * Y, width), low),
+            pltpu.SemaphoreType.DMA((3,)),
         ]
         + sems(6 * (heads // PAIR), 3, 6, 6, 4),
         56, 6, 20, call_id,
     )(length, tokens, gain, wq, wk, wv, wo, wf, bf, w_out)
 
 
+def copier(sem):
+    count = iter(range(sem.shape[0]))
+
+    def copy(src, dst):
+        return load(src, dst, sem.at[next(count)])
+
+    return copy
+
+
 def mlp_forward_kernel(
-    length_ref, x_ref, cot_ref, gated_ref, gain_ref, wo_ref, wg_ref, wu_ref, wd_ref,
-    mid_ref, low_ref, grad_ref, gate_ref, up_ref, hid_ref, out_ref, sums_ref,
-    all_s,
+    length_ref, x_in, cot_in, gated_in, gain_ref, wo_in, wg_in, wu_in, wd_in,
+    mid_out, low_out, grad_out, gate_out, up_out, hid_out, out_out, sums_ref,
+    x_ref, cot_ref, gated_ref, wo_ref, wg_ref, wu_ref, wd_ref,
+    mid_ref, low_ref, grad_ref, gate_ref, up_ref, hid_ref, out_ref, sem,
 ):
-    step = pl.program_id(0)
-    seq = x_ref.shape[0]
+    seq, width = x_ref.shape
     length = length_ref[0]
-    tile, units = wo_ref.shape[1], wg_ref.shape[1]
-
-    @pl.when(step < 2)
-    def _():
-        at = pl.ds(pl.multiple_of(step * tile, tile), tile)
-        branch = mm(gated_ref[...], wo_ref[...])
+    tile, units = wo_ref.shape[2], hid_ref.shape[1] // 2
+    copy = copier(sem)
+    columns = lambda j, size: pl.ds(pl.multiple_of(j * size, size), size)
+    outer = lambda j: pltpu.make_async_copy(
+        wo_in.at[:, columns(j, tile)], wo_ref.at[j], sem.at[sem.shape[0] - 2 + j]
+    )
+    need = copy(gated_in, gated_ref)
+    outer(0).start()
+    need_x = copy(x_in, x_ref)
+    need.wait()
+    outer(1).start()
+    need_cot = copy(cot_in, cot_ref)
+    weights = [copy(wg_in, wg_ref), copy(wu_in, wu_ref), copy(wd_in, wd_ref)]
+    kept = lax.broadcasted_iota(jnp.int32, (seq, 1), 0) < length
+    flushes = []
+
+    def project(j):
+        at = columns(j, tile)
+        outer(j).wait()
+        branch = mm(gated_ref[...], wo_ref[j])
         x = x_ref[:, at].astype(F32)
         mid_ref[:, at] = x + branch
-        kept = lax.broadcasted_iota(jnp.int32, (seq, 1), 0) < length
-        grad_ref[:, at] = jnp.where(kept, cot_ref[:, at].astype(F32), 0.0).astype(jnp.bfloat16)
         sums_ref[0:1, at] = jnp.sum(jnp.where(kept, x * x, 0.0), axis=0, keepdims=True)
         sums_ref[1:2, at] = jnp.sum(jnp.where(kept, branch * branch, 0.0), axis=0, keepdims=True)
 
-    @pl.when(step == 2)
-    def _():
-        def norm(i, carry):
-            at = rows_at(i, 128)
-            mid = mid_ref[at, :]
-            r = lax.rsqrt(jnp.mean(mid * mid, axis=1, keepdims=True) + EPSILON)
-            low_ref[at, :] = (mid * r * gain_ref[...].astype(F32)).astype(jnp.bfloat16)
-            return carry
-
-        lax.fori_loop(0, seq // 128, norm, 0)
-
-    @pl.when((step == 2) | (step == 3))
-    def _():
-        at = pl.ds(pl.multiple_of((step - 2) * units, units), units)
-        gate_ref[...] = mm(low_ref[...], wg_ref[...])
-        up_ref[...] = mm(low_ref[...], wu_ref[...])
-        gate = gate_ref[...]
-        hid = (gate * jax.nn.sigmoid(gate) * up_ref[...]).astype(jnp.bfloat16)
-        hid_ref[...] = hid
-        all_s[:, at] = hid
-
-    @pl.when(step > 3)
-    def _():
-        out_ref[...] = mm(all_s[...], wd_ref[...])
+    need_x.wait()
+    each(0, 2, project)
+    flushes.append(copy(mid_ref, mid_out))
+
+    def norm(i, carry):
+        at = rows_at(i, 128)
+        mid = mid_ref[at, :]
+        r = lax.rsqrt(jnp.mean(mid * mid, axis=1, keepdims=True) + EPSILON)
+        low_ref[at, :] = (mid * r * gain_ref[...].astype(F32)).astype(jnp.bfloat16)
+        return carry
+
+    lax.fori_loop(0, seq // 128, norm, 0)
+    flushes.append(copy(low_ref, low_out))
+    weights[0].wait()
+    weights[1].wait()
+
+    def hidden(j):
+        at = columns(j, units)
+        gate_ref[:, at] = mm(low_ref[...], wg_ref[:, at])
+        up_ref[:, at] = mm(low_ref[...], wu_ref[:, at])
+        gate = gate_ref[:, at]
+        hid_ref[:, at] = (gate * jax.nn.sigmoid(gate) * up_ref[:, at]).astype(jnp.bfloat16)
+
+    each(0, 2, hidden)
+    for src, dst in ((gate_ref, gate_out), (up_ref, up_out), (hid_ref, hid_out)):
+        flushes.append(copy(src, dst))
+    need_cot.wait()
+    grad_ref[...] = jnp.where(kept, cot_ref[...].astype(F32), 0.0).astype(jnp.bfloat16)
+    flushes.append(copy(grad_ref, grad_out))
+    weights[2].wait()
+    result = lambda j: pltpu.make_async_copy(
+        out_ref.at[:, columns(j, tile)], out_out.at[:, columns(j, tile)], sem.at[sem.shape[0] - 4 + j]
+    )
+
+    def project_out(j):
+        at = columns(j, tile)
+        out_ref[:, at] = mm(hid_ref[...], wd_ref[:, at])
+        result(j).start()
+
+    each(0, 2, project_out)
+    flushes += [result(0), result(1)]
+    for c in flushes:
+        c.wait()
 
 
 def mlp_forward(tokens, cotangent, length, gated, gain, wo, wg, wu, wd):
     seq, width = tokens.shape
     hidden = wg.shape[1]
-    tile, units = width // 2, hidden // 2
     low = jnp.bfloat16
-    stage = lambda first: (lambda i, _: (0, jnp.clip(i - first, 0, 1)))
-    columns = pl.BlockSpec((width, units), stage(2))
-    values = pl.BlockSpec((seq, units), stage(2))
-    full = whole((seq, width))
-    return local_call(
+    smem = pl.BlockSpec(memory_space=pltpu.SMEM)
+    outs = [
+        struct(seq, width), struct(seq, width, t=low), struct(seq, width, t=low),
+        struct(seq, hidden), struct(seq, hidden), struct(seq, hidden, t=low), struct(seq, width),
+    ]
+    return pl.pallas_call(
         mlp_forward_kernel,
-        6,
-        [full, full, full, whole((1, width)), pl.BlockSpec((width, tile), stage(0)), columns, columns]
-        + [pl.BlockSpec((hidden, tile), stage(4))],
-        [full, full, full, values, values, values, pl.BlockSpec((seq, tile), stage(4)), whole((2, width))],
-        [
-            struct(seq, width), struct(seq, width, t=low), struct(seq, width, t=low),
-            struct(seq, hidden), struct(seq, hidden),
-            struct(seq, hidden, t=low), struct(seq, width), struct(2, width),
-        ],
-        [pltpu.VMEM((seq, hidden), low)],
-        56, 11, 40,
+        in_specs=[smem, HBM, HBM, HBM, VMEM] + [HBM] * 4,
+        out_specs=[HBM] * 7 + [VMEM],
+        out_shape=outs + [struct(2, width)],
+        scratch_shapes=[
+            pltpu.VMEM((seq, width), low),
+            pltpu.VMEM((seq, width), low),
+            pltpu.VMEM((seq, width), low),
+            pltpu.VMEM((2, width, width // 2), low),
+            pltpu.VMEM((width, hidden), low),
+            pltpu.VMEM((width, hidden), low),
+            pltpu.VMEM((hidden, width), low),
+        ]
+        + [pltpu.VMEM(out.shape, out.dtype) for out in outs]
+        + [pltpu.SemaphoreType.DMA((18,))],
+        compiler_params=pltpu.CompilerParams(vmem_limit_bytes=58 << 20),
     )(length, tokens, cotangent, gated, gain, wo, wg, wu, wd)
 
 
@@ -963,115 +1030,160 @@
 
 
 def mlp_backward_kernel(
-    length_ref, grad_ref, low_ref, gate_ref, up_ref, hid_ref, wd_ref, wg_ref, wu_ref, x_ref, mid_ref,
-    back_ref, gd_ref, gg_ref, gu_ref, layer_ref, square_ref,
-    dg_s, du_s, opp, nbr, held, own_s, mid_s, csem, *sem,
+    length_ref, grad_in, low_in, gate_in, up_in, hid_in, wd_in, wg_in, wu_in, x_ref, mid_ref,
+    back_out, gd_out, gg_out, gu_out, layer_ref, square_ref,
+    grad_ref, low_ref, gate_ref, up_ref, hid_ref, wd_ref, wg_ref, wu_ref,
+    dg_s, du_s, back_s, bufs, opp, nbr, held, own_s, mid_s, csem, *sem,
 ):
-    step = pl.program_id(0)
-    seq = grad_ref.shape[0]
-    units = wd_ref.shape[0]
+    seq, width = grad_ref.shape
+    units = wd_ref.shape[0] // 2
     low16 = jnp.bfloat16
     message, me, right, left, peers = reduce_links(seq, x_ref, opp, nbr, held, sem)
-    q = seq // Y
-    h = q // 2
-
-    def fetch(j):
-        src, dst = (
-            (rows_of(x_ref, right * q, h), held.at[0]),
-            (rows_of(x_ref, left * q + h, h), held.at[1]),
-            (rows_of(x_ref, me * q, q), own_s),
-            (rows_of(mid_ref, me * q, q), mid_s),
-        )[j]
-        return pltpu.make_async_copy(src, dst, csem.at[j])
-
-    @pl.when(step == 0)
-    def _():
-        meet(peers)
-        for name in STEPS[:4]:
-            message(name).start()
-        for j in range(4):
-            fetch(j).start()
-
-    @pl.when(step == 2)
-    def _():
-        for j, (come, go) in enumerate((("oR", "dR"), ("oL", "dL"))):
-            message(come).wait_recv()
-            fetch(j).wait()
-            held[j] = held[j] + opp[j]
-            message(go).start()
-
-    @pl.when(step < 2)
-    def _():
-        at = pl.ds(pl.multiple_of(step * units, units), units)
-        grad = mm_t(grad_ref[...], wd_ref[...])
-        gate = gate_ref[...]
+    q, h = seq // Y, seq // Y // 2
+    copy = copier(csem)
+    need = [
+        copy(grad_in, grad_ref),
+        copy(wd_in.at[0:units], wd_ref.at[0:units]),
+        copy(gate_in.at[:, 0:units], gate_ref.at[:, 0:units]),
+        copy(up_in.at[:, 0:units], up_ref.at[:, 0:units]),
+    ]
+    meet(peers)
+    for name in STEPS[:4]:
+        message(name).start()
+    for c in need[0:2]:
+        c.wait()
+    next_low, next_hid = copy(low_in, low_ref), copy(hid_in, hid_ref)
+    more = [
+        copy(wd_in.at[units:], wd_ref.at[units:]),
+        copy(gate_in.at[:, units:], gate_ref.at[:, units:]),
+        copy(up_in.at[:, units:], up_ref.at[:, units:]),
+    ]
+    weights = [copy(wg_in, wg_ref), copy(wu_in, wu_ref)]
+    adds = [
+        copy(rows_of(x_ref, right * q, h), held.at[0]),
+        copy(rows_of(x_ref, left * q + h, h), held.at[1]),
+        copy(rows_of(x_ref, me * q, q), own_s),
+        copy(rows_of(mid_ref, me * q, q), mid_s),
+    ]
+    spots = (gd_out, gg_out, gu_out)
+    columns = lambda j: pl.ds(pl.multiple_of(j * units, units), units)
+    flush = lambda j, which: pltpu.make_async_copy(
+        bufs.at[which, j], spots[which].at[:, columns(j)], csem.at[csem.shape[0] - 6 + which * 2 + j]
+    )
+
+    def write(which, left_of, right_of, j):
+        slot, at = bufs.at[which, j], columns(j)
+
+        def rows(i, carry):
+            part = rows_at(i, 768)
+            slot[part, :] = t_mm(left_of[:, part], right_of[:, at])
+            return carry
+
+        lax.fori_loop(0, width // 768, rows, 0)
+        flush(j, which).start()
+
+    def tile(j):
+        at = columns(j)
+
+        @pl.when(j == 1)
+        def _():
+            for c in more:
+                c.wait()
+
+        grad = mm_t(grad_ref[...], wd_ref[at, :])
+
+        @pl.when(j == 0)
+        def _():
+            for c in need[2:4]:
+                c.wait()
+
+        gate = gate_ref[:, at]
         sig = jax.nn.sigmoid(gate)
-        dg_s[:, at] = (grad * up_ref[...] * (sig * (1.0 + gate * (1.0 - sig)))).astype(low16)
+        dg_s[:, at] = (grad * up_ref[:, at] * (sig * (1.0 + gate * (1.0 - sig)))).astype(low16)
         du_s[:, at] = (grad * (gate * sig)).astype(low16)
 
-        def grads(k, carry):
-            rows = rows_at(k, 768)
-            gd_ref[rows, :] = t_mm(grad_ref[:, rows], hid_ref[...])
-            gg_ref[rows, :] = t_mm(low_ref[:, rows], dg_s[:, at])
-            gu_ref[rows, :] = t_mm(low_ref[:, rows], du_s[:, at])
-            return carry
-
-        lax.fori_loop(0, gd_ref.shape[0] // 768, grads, 0)
-
-    @pl.when(step >= 2)
-    def _():
-        back_ref[...] = mm_t(dg_s[...], wg_ref[...])
-        back_ref[...] = back_ref[...] + mm_t(du_s[...], wu_ref[...])
-
-    @pl.when(step == 3)
-    def _():
-        fetch(2).wait()
-        fetch(3).wait()
-        sums = 0.0
-        for part, names in enumerate((("dR", "iL"), ("iR", "dL"))):
-            for name in names:
-                message(name).wait_recv()
-            at = slice(part * h, part * h + h)
-            branch = own_s[at, :] + nbr[0, at] + nbr[1, at]
-            layer_ref[at, :] = (mid_s[at, :] + branch).astype(low16).astype(F32)
-            row = lax.broadcasted_iota(jnp.int32, (h, 1), 0) + (me * q + part * h)
-            kept = jnp.where(row < length_ref[0], branch * branch, 0.0)
-            sums = sums + jnp.sum(kept, axis=0, keepdims=True)
-        square_ref[...] = sums
-        for name in STEPS[:6]:
-            message(name).wait_send()
+        @pl.when(j == 0)
+        def _():
+            next_low.wait()
+            next_hid.wait()
+
+        write(0, grad_ref, hid_ref, j)
+        write(1, low_ref, dg_s, j)
+
+        @pl.when(j == 1)
+        def _():
+            for part, (come, go) in enumerate((("oR", "dR"), ("oL", "dL"))):
+                message(come).wait_recv()
+                adds[part].wait()
+                held[part] = held[part] + opp[part]
+                message(go).start()
+
+        write(2, low_ref, du_s, j)
+
+    each(0, 2, tile)
+    for c in weights:
+        c.wait()
+
+    def back(i, carry):
+        rows = rows_at(i, 768)
+        back_s[:, rows] = mm_t(dg_s[...], wg_ref[rows, :])
+        back_s[:, rows] = back_s[:, rows] + mm_t(du_s[...], wu_ref[rows, :])
+        return carry
+
+    lax.fori_loop(0, width // 768, back, 0)
+    last = copy(back_s, back_out)
+    adds[2].wait()
+    adds[3].wait()
+    sums = 0.0
+    for part, names in enumerate((("dR", "iL"), ("iR", "dL"))):
+        for name in names:
+            message(name).wait_recv()
+        at = slice(part * h, part * h + h)
+        branch = own_s[at, :] + nbr[0, at] + nbr[1, at]
+        layer_ref[at, :] = (mid_s[at, :] + branch).astype(low16).astype(F32)
+        row = lax.broadcasted_iota(jnp.int32, (h, 1), 0) + (me * q + part * h)
+        kept = jnp.where(row < length_ref[0], branch * branch, 0.0)
+        sums = sums + jnp.sum(kept, axis=0, keepdims=True)
+    square_ref[...] = sums
+    last.wait()
+    for j in (0, 1):
+        for which in range(3):
+            flush(j, which).wait()
+    for name in STEPS[:6]:
+        message(name).wait_send()
 
 
 def mlp_backward(length, grad, low, gate, up, hid, wg, wu, wd, branch, mid, call_id):
     seq, width = low.shape
     hidden = wg.shape[1]
-    tile, units, quarter = width // 2, hidden // 2, seq // Y
-    stage = lambda first: (lambda i, _: (0, jnp.clip(i - first, 0, 1)))
-    down = lambda first: (lambda i, _: (jnp.clip(i - first, 0, 1), 0))
-    values = pl.BlockSpec((seq, units), stage(0))
-    grads = pl.BlockSpec((width, units), stage(0))
-    weights = pl.BlockSpec((tile, hidden), down(2))
-    full, hbm = whole((seq, width)), pl.BlockSpec(memory_space=pl.ANY)
-    return local_call(
+    quarter = seq // Y
+    low16 = jnp.bfloat16
+    smem = pl.BlockSpec(memory_space=pltpu.SMEM)
+    inputs = (grad, low, gate, up, hid, wd, wg, wu)
+    return pl.pallas_call(
         mlp_backward_kernel,
-        4,
-        [full, full, values, values, values, pl.BlockSpec((units, width), down(0)), weights, weights, hbm, hbm],
-        [pl.BlockSpec((seq, tile), stage(2)), grads, grads, grads, whole((quarter, width)), whole((1, width))],
-        [struct(seq, width)] + [struct(width, hidden)] * 3 + [struct(quarter, width), struct(1, width)],
-        [pltpu.VMEM((seq, hidden), jnp.bfloat16)] * 2
+        in_specs=[smem] + [HBM] * 10,
+        out_specs=[HBM] * 4 + [VMEM] * 2,
+        out_shape=[struct(seq, width)] + [struct(width, hidden)] * 3
+        + [struct(quarter, width), struct(1, width)],
+        scratch_shapes=[pltpu.VMEM(a.shape, a.dtype) for a in inputs]
+        + [pltpu.VMEM((seq, hidden), low16)] * 2
+        + [pltpu.VMEM((seq, width), F32), pltpu.VMEM((3, 2, width, hidden // 2), F32)]
         + ring_scratch(quarter, width)
         + [pltpu.VMEM((quarter, width), F32)] * 2
-        + [pltpu.SemaphoreType.DMA((4,))]
+        + [pltpu.SemaphoreType.DMA((22,))]
         + sems(6),
-        62, 13, 60, call_id,
-    )(length, grad, low, gate, up, hid, wd, wg, wu, branch, mid)
+        compiler_params=pltpu.CompilerParams(
+            vmem_limit_bytes=62 << 20, collective_id=call_id, has_side_effects=True
+        ),
+    )(length, *inputs, branch, mid)
 
 
 def backward_kernel(
     length_ref, gg_ref, low_ref, qn_ref, kn_ref, v_ref, sig_ref, att_ref, stat_ref,
     decay_ref, wq_ref, wk_ref, wv_ref, wo_ref, wf_ref, own_ref, gated_ref, layer_ref,
-    back_ref, four_ref, gout_ref, gf_ref, bias_ref, out_ref,
-    k_s, do_s, line_s, dq_s, dk_s, dv_s, all_s, fall_s, w_s, wf_s, lay_s, *sem,
+    back_out, four_out, gout_out, gf_ref, bias_ref, out_ref,
+    k_s, do_s, line_s, dq_s, dk_s, dv_s, all_s, fall_s, w_s, wf_s, lay_s, back_ref, wide_s, osem, *sem,
 ):
     step = pl.program_id(0)
     seq, width = low_ref.shape
@@ -1105,9 +1217,9 @@
 
     @pl.when(step == 0)
     def _():
-        heads = wf_ref.shape[1]
+        heads = wf_ref.shape[0]
         wf_s[...] = jnp.zeros_like(wf_s)
-        wf_s[:, 0:heads] = wf_ref[...]
+        wf_s[0:heads, :] = wf_ref[...]
         decay = decay_ref[0]
         row = lax.broadcasted_iota(jnp.int32, decay.shape, 0)
         final = jnp.sum(jnp.where(row == length - 1, decay, 0.0), axis=0, keepdims=True)
@@ -1169,14 +1281,27 @@
         r = jnp.where(first, stat[:, col : col + 1], stat[:, col + 1 : col + 2])
         all_s[:, part(to)] = (r * (e - n * jnp.where(first, a, b))).astype(low16)
     all_s[:, part(2)] = dv_s[...].astype(low16)
+    slot = lax.rem(step, 2)
+
+    def flush(j, at, step):
+        columns = pl.ds(pl.multiple_of(step * wide, wide), wide)
+        out = (four_out, gout_out)[j].at[:, columns]
+        return pltpu.make_async_copy(wide_s.at[at, j], out, osem.at[at * 2 + j])
+
+    @pl.when(step == 2)
+    def _():
+        for j in (0, 1):
+            flush(j, 0, 0).wait()
 
     def grads(k, carry):
         rows = rows_at(k, 768)
-        four_ref[rows, :] = t_mm(low_ref[:, rows], all_s[:, pl.ds(base, wide)])
-        gout_ref[rows, :] = t_mm(own_ref[:, rows].astype(low16), gated_ref[...])
+        wide_s[slot, 0, rows, :] = t_mm(low_ref[:, rows], all_s[:, pl.ds(base, wide)])
+        wide_s[slot, 1, rows, :] = t_mm(own_ref[:, rows].astype(low16), gated_ref[...])
         return carry
 
     lax.fori_loop(0, width // 768, grads, 0)
+    for j in (0, 1):
+        flush(j, slot, step).start()
 
     @pl.when(step == pl.num_programs(0) - 1)
     def _():
@@ -1188,13 +1313,18 @@
         def tail(k, carry):
             rows = rows_at(k, 768)
             back_ref[:, rows] = mm_t(all_s[...], w_s[rows, :])
-            back_ref[:, rows] = back_ref[:, rows] + mm_t(fall, wf_s[rows, :])
+            back_ref[:, rows] = back_ref[:, rows] + mm(fall, wf_s[:, rows])
             return carry
 
         lax.fori_loop(0, width // 768, tail, 0)
+        last = load(back_ref, back_out, osem.at[4])
         for j in (1, 2, 4, 5):
             spread(j).wait_recv()
         out_ref[...] = lay_s[...].astype(low16)
+        for at, done in ((1, 1), (0, 2)):
+            for j in (0, 1):
+                flush(j, at, done).wait()
+        last.wait()
         for j in range(6):
             spread(j).wait_send()
 
@@ -1204,7 +1334,6 @@
     heads = wq.shape[1]
     weights = pl.BlockSpec((width, PAIR), lambda i, _: (0, i))
     lanes = pl.BlockSpec((seq, PAIR), lambda i, _: (0, i))
-    wide = pl.BlockSpec((width, 4 * PAIR), lambda i, _: (0, i))
     full = whole((seq, width))
     low16 = jnp.bfloat16
     return local_call(
@@ -1213,7 +1342,7 @@
         [lanes, full] + [lanes] * 6 + [whole((2, seq, PAIR))] + [weights] * 4
         + [whole(wf.shape), whole(own.shape)]
         + [pl.BlockSpec((own.shape[0], 4 * PAIR), lambda i, _: (lax.axis_index("mp"), i)), whole(layer.shape)],
-        [full, wide, wide, whole((8, width)), whole((1, PAIR)), full],
+        [HBM, HBM, HBM, whole((8, width)), whole((1, PAIR)), full],
         [
             struct(seq, width), struct(width, 4 * heads), struct(width, width), struct(8, width),
             struct(1, PAIR), struct(seq, width, t=low16),
@@ -1228,17 +1357,21 @@
             pltpu.VMEM((seq, 4 * heads), low16),
             pltpu.VMEM((seq, PAIR), F32),
             pltpu.VMEM((width, 4 * heads), low16),
-            pltpu.VMEM((width, PAIR), low16),
+            pltpu.VMEM((PAIR, width), low16),
             pltpu.VMEM((seq, width), F32),
+            pltpu.VMEM((seq, width), F32),
+            pltpu.VMEM((2, 2, width, 4 * PAIR), F32),
+            pltpu.SemaphoreType.DMA((5,)),
         ]
         + sems(6),
-        60, 14, 50, call_id,
+        62, 14, 50, call_id,
     )(place, gg, low, qn, kn, v, sig, att, stat, decay, wq, wk, wv, wo, wf, own, gated, layer)
 
 
 def finish_kernel(
-    grad_in, layer_in, wout_in, four_in, mlp_in,
+    grad_in, layer_in, wout_in, four_in, mlp_in, sums_in,
     grad_ref, layer_ref, wout_ref, q_ref, k_ref, v_ref, o_ref, gate_ref, up_ref, down_ref,
+    gain_ref, gain2_ref, fall_ref,
     sem,
 ):
     rows = grad_in.shape[0] // 4
@@ -1248,33 +1381,45 @@
             part = slice(j * rows, j * rows + rows)
             copies.append(load(src.at[part], dst.at[part], sem.at[at]))
     wout_ref[...] = wout_in[...].T
+    inner = q_ref.shape[1]
     for j, ref in enumerate((q_ref, k_ref, v_ref, o_ref)):
-        for pair in range(q_ref.shape[1] // PAIR):
+        for pair in range(inner // PAIR):
             lane = (pair * 4 + j) * PAIR
             ref[:, pair * PAIR : pair * PAIR + PAIR] = four_in[:, lane : lane + PAIR]
     units = gate_ref.shape[1]
     down_ref[...] = mlp_in[:, 0:units].T
     gate_ref[...] = mlp_in[:, units : 2 * units]
-    up_ref[...] = mlp_in[:, 2 * units : 3 * units]
+    up_ref[:, 0:STEP] = mlp_in[:, 2 * units : 2 * units + STEP]
+    up_ref[:, STEP:] = four_in[:, 4 * inner : 4 * inner + STEP]
+    share, width = gain_ref.shape[1], sums_in.shape[1]
+    row = lax.broadcasted_iota(jnp.int32, (width, share), 0)
+    lane = lax.broadcasted_iota(jnp.int32, (width, share), 1)
+    pick = jnp.where(row == lane + lax.axis_index("dp") * share, 1.0, 0.0)
+    own = jnp.dot(
+        sums_in[...], pick, precision=lax.Precision.HIGHEST, preferred_element_type=F32
+    )
+    gain_ref[...] = own[0:1]
+    gain2_ref[...] = own[1:2]
+    fall_ref[...] = own[3 : 3 + fall_ref.shape[1]].T
     for copy in copies:
         copy.wait()
 
 
-def finish(grad, layer, out_share, share, mlp_share):
+def finish(grad, layer, out_share, share, mlp_share, sums, heads):
     rows, inner = out_share.shape
-    units = mlp_share.shape[1] // 3
-    hbm, vmem = pl.BlockSpec(memory_space=pl.ANY), pl.BlockSpec(memory_space=pltpu.VMEM)
+    units = mlp_share.shape[1] * 2 // 5
     return pl.pallas_call(
         finish_kernel,
         out_shape=[
             struct(*grad.shape), struct(*layer.shape, t=layer.dtype), struct(inner, rows),
             *[struct(rows, inner)] * 4, struct(rows, units), struct(rows, units), struct(units, rows),
+            struct(1, rows), struct(1, rows), struct(rows, heads),
         ],
-        in_specs=[hbm, hbm, vmem, vmem, vmem],
-        out_specs=[hbm, hbm] + [vmem] * 8,
+        in_specs=[HBM, HBM] + [VMEM] * 4,
+        out_specs=[HBM, HBM] + [VMEM] * 11,
         scratch_shapes=[pltpu.SemaphoreType.DMA((8,))],
         compiler_params=pltpu.CompilerParams(vmem_limit_bytes=16 << 20),
-    )(grad, layer, out_share, share, mlp_share)
+    )(grad, layer, out_share, share, mlp_share, sums)
 
 
 def per_device(
@@ -1285,7 +1430,7 @@
     model_width = x.shape[1]
     heads = w_forget.shape[1]
     gain_in, gain_mid = gain_attn[None], gain_mlp[None]
-    weights = (w_query, w_key, w_value, w_outgate, w_forget)
+    weights = (w_query, w_key, w_value, w_outgate, w_forget.T)
     low, qn, kn, value, sig, attended, stat, decay, gated, w_full = forward_attention(
         x, lengths, gain_in, *weights, b_forget[None], w_out, 0
     )
@@ -1296,40 +1441,36 @@
         lengths, grad_rows, mid_low, gate, up, hidden, w_gate, w_up, w_down, mlp_local, middle, 1
     )
     grad_own, gg, mlp_share, mlp_gain = reduce_middle(
-        mid_local, middle, grad_rows, gain_mid, w_full, [g_down, g_gate, g_up], 2
+        mid_local, middle, grad_rows, gain_mid, w_full, [g_down, g_gate, g_up],
+        ((0, 0), (0, 1), (1, 0), (1, 1), (2, 0)), 2,
     )
     in_local, g_four, g_out, g_fall, bias, layer_out = backward_attention(
         lengths, gg, low, qn, kn, value, sig, attended, stat, decay, *weights, grad_own, gated,
         layer_own, 3,
     )
-    bucket_hot = (buckets[0] == jnp.arange(NBUCKET)).astype(F32)
-    square_sums = jnp.concatenate([squares, mlp_square]).sum(axis=1)
-    misc = jnp.stack([square_sums[0], square_sums[1], lengths[0].astype(F32), square_sums[2]])
-    misc = misc[:, None] * bucket_hot[None, :]
-    misc = jnp.stack([misc[:3].reshape(-1), jnp.pad(misc[3], (0, 2 * NBUCKET))])
-    misc = jnp.pad(misc, ((0, 0), (0, PAIR - 3 * NBUCKET)))
+    small = (mlp_gain, g_fall, squares, mlp_square, bias, lengths, buckets)
     input_grad, out_share, share, sums = reduce_input(
-        in_local, x, grad_own, gain_in, (mlp_gain, g_fall, misc, bias), [g_out, g_four], 4
-    )
-    input_grad, layer_out, g_out, g_query, g_key, g_value, g_outgate, g_gate, g_up, g_down = finish(
-        input_grad, layer_out, out_share, share, mlp_share
-    )
+        in_local, x, grad_own, gain_in, small, [g_out, g_four, g_up],
+        ((0, 0), (0, 1), (0, 2), (1, 0), (1, 1), (1, 2), (2, 1)), 4,
+    )
+    (
+        input_grad, layer_out, g_out, g_query, g_key, g_value, g_outgate, g_gate, g_up, g_down,
+        g_gain, g_gain_mid, g_fall,
+    ) = finish(input_grad, layer_out, out_share, share, mlp_share, sums, heads)
     totals = jnp.stack([sums[9, :NBUCKET], sums[9, NBUCKET : 2 * NBUCKET], sums[2, :NBUCKET]])
     rms = jnp.sqrt(totals / (sums[9, 2 * NBUCKET : 3 * NBUCKET] * model_width)[None, :])
-    rows = model_width // lax.axis_size("dp")
-    mine = lax.dynamic_slice_in_dim(sums[:9], lax.axis_index("dp") * rows, rows, axis=1)
     return (
         layer_out[None],
         input_grad[None],
-        mine[0],
+        g_gain[0],
         g_query,
         g_key,
         g_value,
         g_outgate,
-        mine[3 : 3 + heads].T,
+        g_fall,
         sums[10, :heads],
         g_out,
-        mine[1],
+        g_gain_mid[0],
         g_gate,
         g_up,
         g_down,

time: 388 us -> 365 us (0.941)
  Pallas kernels: 368 us -> 350 us
    pallas_call x4, Pallas kernels: 242 us -> 228 us  [the longest x1 98.5 us: reduce_input(): pl.pallas_call(functools.partial(input_kernel, pieces, len(grads)), out_s...]
where the time goes in v4:
time: 365 us; the launch traced here: 364 us
  Pallas kernels  350 us (96%)
  local copies, waits for them, and re-layouts  10.5 us (3%)
    pallas_call x1, Pallas kernels, reduce_input(): pl.pallas_call(functools.partial(input_kernel, pieces, len(grads)), out_s...  98.5 us
    pallas_call x1, Pallas kernels, reduce_middle(): pl.pallas_call(functools.partial(middle_kernel, pieces, len(grads)), out_...  67.8 us
    pallas_call x1, Pallas kernels, forward_attention(): local_call(forward_kernel, heads // PAIR, [whole((seq, width)), whole((1,...  63.3 us
    pallas_call x1, Pallas kernels, backward_attention(): local_call(backward_kernel, heads // PAIR, [lanes, full] + [lanes] * 6 +...  54.9 us
    pallas_call x1, Pallas kernels, mlp_backward(): pl.pallas_call(mlp_backward_kernel, in_specs=[smem] + [HBM] * 10, out_spe...  41.7 us
    pallas_call x1, Pallas kernels, mlp_forward(): pl.pallas_call(mlp_forward_kernel, in_specs=[smem, HBM, HBM, HBM, VMEM] +...  19.9 us
    unnamed x17, local copies, waits for them, and re-layouts  7.39 us

profile of v4, /device:TPU:0, one launch (start us, length us, event | category | flops | bytes accessed | tf_op | source)
XLA Modules:
  0.0 364.3 jit_solution(15694293047204698467)
XLA Ops:
  1.3 1.3 broadcast_in_dim.16.gain_ref
  2.6 0.0 copy-start.6
  2.6 63.3 %shard_map.271 = (bf16[768,1536]{1,0:T(8,128)(2,1)}, f32[768,384]{1,0:T(8,128)}, f32[768,384]{1,0:T(8,128)}, bf16[768,384]{1,0:T(8,128)(2,1)}, f32[768,384]{1,0:...) custom-call(s32[1]{0:T(128)S(6)} %copy.34.length_ref, ...), custom_call_target="tpu_custom_call" | custom-call | flops 6000000000 | bytes 20000000 | tf_op jit(solution)/shard_map/pallas_call | solution.py:866
  65.9 0.0 copy-done.6
  65.9 0.6 broadcast_in_dim.18.gain_ref
  66.5 19.9 %shard_map.272 = (f32[768,1536]{1,0:T(8,128)}, bf16[768,1536]{1,0:T(8,128)(2,1)}, bf16[768,1536]{1,0:T(8,128)(2,1)}, f32[768,1024]{1,0:T(8,128)}, f32[768,1024]{...) custom-call(s32[1]{0:T(128)S(6)} %copy.34.length_ref, ...), custom_call_target="tpu_custom_call" | custom-call | tf_op jit(solution)/shard_map/pallas_call | solution.py:993
  86.4 41.7 %shard_map.273 = (f32[768,1536]{1,0:T(8,128)}, f32[1536,1024]{1,0:T(8,128)}, f32[1536,1024]{1,0:T(8,128)}, f32[1536,1024]{1,0:T(8,128)}, f32[192,1536]{1,0:T(8,128)}, /*index=5*/f32[1,1536]{1,0:T(1,128)}) custom-call(s32[1]{0:T(128)S(6)} %copy.34.length_ref, bf16[768,1536]{1,0:T(8,128)(2,1)} %get-tuple-element.68.grad_in.base_ref, ...), custom_call_target="tpu_custom_call" | custom-call | tf_op jit(solution)/shard_map/pallas_call | solution.py:1163
  128.2 67.8 %shard_map.274 = (f32[192,1536]{1,0:T(8,128)}, f32[768,384]{1,0:T(8,128)}, f32[48,2560]{1,0:T(8,128)}, f32[1,1536]{1,0:T(1,128)}) custom-call(f32[768,1536]{1,0:T(8,128)} %get-tuple-element.75.x_ref, f32[768,1536]{1,0:T(8,128)} %get-tuple-element.74.mid_ref.source_ref, bf16[768,1536]{1,0:T(8,128)(2,1)} %get-tuple-element.68.grad_in.base_ref, ...), custom_call_target="tpu_custom_call" | custom-call | tf_op jit(solution)/shard_map/pallas_call | solution.py:420
  196.0 54.9 %shard_map.275 = (f32[768,1536]{1,0:T(8,128)}, f32[1536,1536]{1,0:T(8,128)}, f32[1536,1536]{1,0:T(8,128)}, f32[8,1536]{1,0:T(8,128)}, f32[1,128]{1,0:T(1,128)}, /*index=5*/bf16[768,1536]{1,0:T(8,128)(2,1)}) custom-call(s32[1]{0:T(128)S(6)} %copy.34.length_ref, f32[768,384]{1,0:T(8,128)} %get-tuple-element.79.gg_ref, ...), custom_call_target="tpu_custom_call" | custom-call | flops 14000000000 | bytes 50000000 | tf_op jit(solution)/shard_map/pallas_call | solution.py:1339
  251.5 0.0 copy-start.1
  251.5 0.0 copy-start.2
  251.5 98.5 %shard_map.276 = (f32[768,1536]{1,0:T(8,128)}, f32[48,384]{1,0:T(8,128)}, f32[48,2048]{1,0:T(8,128)}, f32[16,1536]{1,0:T(8,128)}) custom-call(f32[768,1536]{1,0:T(8,128)} %get-tuple-element.90.x_ref, bf16[768,1536]{1,0:T(8,128)(2,1)} %bitcast.14, f32[192,1536]{1,0:T(8,128)} %get-tuple-element.88.own_ref.base_ref, bf16[1,1536]{1,0:T(2,128)(2,1)} %broadcast_in_dim.16.gain_ref, ...), custom_call_target="tpu_custom_call" | custom-call | tf_op jit(solution)/shard_map/pallas_call | solution.py:534
  350.0 0.9 multiply_bitcast_fusion
  350.9 0.6 fusion
  351.5 0.0 copy-done.1
  351.5 0.0 copy-done.2
  351.5 0.0 copy-start
  351.5 2.3 copy-done
  353.8 0.0 copy-start.3
  353.8 1.0 copy-done.3
  354.8 0.0 copy-start.4
  354.8 0.9 copy-done.4
  355.7 0.0 copy-start.5
  355.7 0.9 copy-done.5
  356.6 4.2 %shard_map.277 = (f32[768,1536]{1,0:T(8,128)}, bf16[768,1536]{1,0:T(8,128)(2,1)}, f32[384,48]{1,0:T(8,128)S(1)}, f32[48,384]{1,0:T(8,128)}, f32[48,384]{1,0:T(8,...) custom-call(f32[768,1536]{1,0:T(8,128)S(1)} %copy-done, ...), custom_call_target="tpu_custom_call" | custom-call | tf_op jit(solution)/shard_map/pallas_call | solution.py:1411
  360.9 0.9 copy.33
  361.7 0.7 copy.32
  362.5 0.7 copy.31
  363.1 1.2 slice_bitcast_fusion
Async XLA Ops:
  2.6 63.3 %copy-start.6 = (bf16[1536]{0:T(1024)(128)(2,1)S(1)}, bf16[1536]{0:T(1024)(128)(2,1)}, u32[]{:S(2)}) copy-start(bf16[1536]{0:T(1024)(128)(2,1)} %param.28) | copy-start | bytes 9220
  251.5 100.0 %copy-start.1 = (bf16[768,1536]{1,0:T(8,128)(2,1)S(1)}, bf16[768,1536]{1,0:T(8,128)(2,1)}, u32[]{:S(2)}) copy-start(bf16[768,1536]{1,0:T(8,128)(2,1)} %get-tuple-element.99.layer_in) | copy-start | bytes 7077892
  251.5 100.0 %copy-start.2 = (f32[48,2560]{1,0:T(8,128)S(1)}, f32[48,2560]{1,0:T(8,128)}, u32[]{:S(2)}) copy-start(f32[48,2560]{1,0:T(8,128)} %get-tuple-element.102.mlp_in) | copy-start | bytes 1474564
  351.5 2.3 copy-start
  353.8 1.0 copy-start.3
  354.8 0.9 copy-start.4
  355.7 0.9 copy-start.5

commit v5 on v4

--- a/solution.py
+++ b/solution.py
@@ -51,57 +51,76 @@
 
 
 class YRing:
-    def __init__(self, rows, ssem, rsem):
+    def __init__(self, rows, waves, ssem, rsem):
         self.sems = (ssem, rsem)
         self.dp, self.me = lax.axis_index("dp"), lax.axis_index("mp")
         self.right, self.left = lax.rem(self.me + 1, Y), lax.rem(self.me + 3, Y)
         self.far = lax.rem(self.me + 2, Y)
         self.quarter, self.half = rows // Y, rows // Y // 2
+        self.tall = self.half // waves
         self.sent = {}
 
     def neighbours(self):
         return [(self.dp, self.right), (self.dp, self.left)]
 
-    def send(self, name, src, dst, to):
-        self.sent[name] = push(src, dst, *self.sems, STEPS.index(name), (self.dp, to))
-
-    def start(self, x, opp, nbr):
-        q, h = self.quarter, self.half
-        self.send("oR", rows_of(x, self.far * q, h), opp.at[0], self.right)
-        self.send("oL", rows_of(x, self.far * q + h, h), opp.at[1], self.left)
-        self.send("iR", rows_of(x, self.right * q + h, h), nbr.at[0, h:q], self.right)
-        self.send("iL", rows_of(x, self.left * q, h), nbr.at[1, 0:h], self.left)
-
-    def relay(self, x, opp, nbr, held):
-        q, h = self.quarter, self.half
-        self.sent["oR"].wait_recv()
-        held[0] = rows_of(x, self.right * q, h)[...] + opp[0]
-        self.send("dR", held.at[0], nbr.at[0, 0:h], self.right)
-        self.sent["oL"].wait_recv()
-        held[1] = rows_of(x, self.left * q + h, h)[...] + opp[1]
-        self.send("dL", held.at[1], nbr.at[1, h:q], self.left)
-
-    def collect(self, x, nbr, part):
-        h = self.half
+    def send(self, name, wave, src, dst, to):
+        at = wave * 6 + STEPS.index(name)
+        self.sent[name, wave] = push(src, dst, *self.sems, at, (self.dp, to))
+
+    def rows(self, x, owner, part, wave):
+        return rows_of(x, owner * self.quarter + part * self.half + wave * self.tall, self.tall)
+
+    def fetch(self, x, held, own, sem):
+        self.loads = [
+            load(rows_of(x, self.right * self.quarter, self.half), held.at[0], sem.at[0]),
+            load(rows_of(x, self.left * self.quarter + self.half, self.half), held.at[1], sem.at[1]),
+            load(rows_of(x, self.me * self.quarter, self.quarter), own, sem.at[2]),
+        ]
+
+    def start(self, x, opp, nbr, wave):
+        w = slice(wave * self.tall, wave * self.tall + self.tall)
+        low = slice(self.half + wave * self.tall, self.half + wave * self.tall + self.tall)
+        self.send("oR", wave, self.rows(x, self.far, 0, wave), opp.at[0, w], self.right)
+        self.send("oL", wave, self.rows(x, self.far, 1, wave), opp.at[1, w], self.left)
+        self.send("iR", wave, self.rows(x, self.right, 1, wave), nbr.at[0, low], self.right)
+        self.send("iL", wave, self.rows(x, self.left, 0, wave), nbr.at[1, w], self.left)
+
+    def relay(self, opp, nbr, held, wave):
+        w = slice(wave * self.tall, wave * self.tall + self.tall)
+        low = slice(self.half + wave * self.tall, self.half + wave * self.tall + self.tall)
+        for part, (come, go, into, to) in enumerate(
+            (("oR", "dR", nbr.at[0, w], self.right), ("oL", "dL", nbr.at[1, low], self.left))
+        ):
+            self.sent[come, wave].wait_recv()
+            if wave == 0:
+                self.loads[part].wait()
+            held[part, w] = held[part, w] + opp[part, w]
+            self.send(go, wave, held.at[part, w], into, to)
+
+    def collect(self, own, nbr, part, wave):
+        if part == 0 and wave == 0:
+            self.loads[2].wait()
         for name in (("dR", "iL"), ("iR", "dL"))[part]:
-            self.sent[name].wait_recv()
-        at = slice(part * h, part * h + h)
-        return rows_of(x, self.me * self.quarter + part * h, h)[...] + nbr[0, at] + nbr[1, at]
-
-    def spread(self, part, block):
-        own, tag = block(self.me, part), "ab"[part]
-        self.send("gR" + tag, own, own, self.right)
-        self.send("gL" + tag, own, own, self.left)
+            self.sent[name, wave].wait_recv()
+        start = part * self.half + wave * self.tall
+        at = slice(start, start + self.tall)
+        return at, own[at, :] + nbr[0, at] + nbr[1, at]
+
+    def spread(self, part, own, block):
+        into, tag = block(self.me, part), "ab"[part]
+        mine = own.at[part * self.half : part * self.half + self.half]
+        self.send("gR" + tag, 0, mine, into, self.right)
+        self.send("gL" + tag, 0, mine, into, self.left)
 
     def forward(self, block):
-        self.sent["gRa"].wait_recv()
-        self.send("fR", block(self.left, 0), block(self.left, 0), self.right)
-        self.sent["gLb"].wait_recv()
-        self.send("fL", block(self.right, 1), block(self.right, 1), self.left)
+        self.sent["gRa", 0].wait_recv()
+        self.send("fR", 0, block(self.left, 0), block(self.left, 0), self.right)
+        self.sent["gLb", 0].wait_recv()
+        self.send("fL", 0, block(self.right, 1), block(self.right, 1), self.left)
 
     def arrive(self):
         for name in ("gRb", "gLa", "fR", "fL"):
-            self.sent[name].wait_recv()
+            self.sent[name, 0].wait_recv()
 
     def finish(self):
         for copy in self.sent.values():
@@ -355,57 +374,62 @@
 def middle_kernel(pieces, count, x_ref, source_ref, base_ref, gain_ref, w_ref, *refs):
     ins, refs = refs[:count], refs[count:]
     grad_ref, gg_ref, share_ref, sums_ref = refs[:4]
-    source_s, base_s, w_s, opp, nbr, held, blocks, csem, *sem = refs[4:16]
-    here, ring = Place(), YRing(x_ref.shape[0], *sem[0:2])
-    total = ScatterSum(here, scatter_sources(ins, pieces), *refs[16:])
+    source_s, base_s, w_s, opp, nbr, held, own_s, blocks, csem, *sem = refs[4:17]
+    here, ring = Place(), YRing(x_ref.shape[0], 2, *sem[0:2])
+    total = ScatterSum(here, scatter_sources(ins, pieces), *refs[17:])
     n = total.n
     far = (ring.dp, ring.far)
     meet(ring.neighbours() + [far] + here.peers())
-    ring.start(x_ref, opp, nbr)
+    ring.start(x_ref, opp, nbr, 0)
     q, h = ring.quarter, ring.half
-    loads = [
-        load(rows_of(source_ref, ring.me * q, q), source_s, csem.at[0]),
-        load(rows_of(base_ref, ring.me * q, q), base_s, csem.at[1]),
-        load(w_ref, w_s, csem.at[2]),
-    ]
+    ring.fetch(x_ref, held, own_s, csem)
     for k in range(n):
         total.exchange(k)
-    each(0, n // 2, total.first)
-    ring.relay(x_ref, opp, nbr, held)
-    each(n // 2, n, total.first)
+    loads = [
+        load(rows_of(source_ref, ring.me * q, q), source_s, csem.at[3]),
+        load(rows_of(base_ref, ring.me * q, q), base_s, csem.at[4]),
+        load(w_ref, w_s, csem.at[5]),
+    ]
+    ring.relay(opp, nbr, held, 0)
+    ring.start(x_ref, opp, nbr, 1)
+    each(0, n, total.first)
     each(0, n - 2, total.first_relay)
+    ring.relay(opp, nbr, held, 1)
     for copy in loads:
         copy.wait()
-    sums = 0.0
-    for part in (0, 1):
-        at = slice(part * h, part * h + h)
-        value, more = norm_back(
-            ring.collect(x_ref, nbr, part), source_s[at, :], base_s[at, :], gain_ref[...]
-        )
-        grad_ref[at, :] = value
-        sums = sums + more
+    sums, swaps, keeps = 0.0, [], []
+    inner = gg_ref.shape[1]
+    for wave in (0, 1):
+        for part in (0, 1):
+            at, value = ring.collect(own_s, nbr, part, wave)
+            value, more = norm_back(value, source_s[at, :], base_s[at, :], gain_ref[...])
+            grad_ref[at, :] = value
+            sums = sums + more
+        tall = ring.tall
+        low = jnp.concatenate(
+            [grad_ref[part * h + wave * tall : part * h + wave * tall + tall, :] for part in (0, 1)], axis=0
+        ).astype(jnp.bfloat16)
+        for j, by in enumerate((2, 1, 3, 0)):
+            to = lax.rem(ring.me + by, Y)
+            blocks[wave, j] = mm_t(low, rows_of(w_s, to * inner, inner)[...])
+            for part in (0, 1):
+                src = blocks.at[wave, j, part * tall : part * tall + tall]
+                into = rows_of(gg_ref, ring.me * q + part * h + wave * tall, tall)
+                if by:
+                    at = (wave * 3 + j) * 2 + part
+                    swaps.append(push(src, into, *sem[2:4], at, (ring.dp, to)))
+                else:
+                    keeps.append(load(src, into, csem.at[6 + wave * 2 + part]))
+        if wave == 0:
+            each(n - 2, n, total.first_relay)
     sums_ref[...] = sums
-    low = grad_ref[...].astype(jnp.bfloat16)
-    inner = gg_ref.shape[1]
-    swaps = []
-    for j, by in enumerate((2, 1, 3, 0)):
-        to = lax.rem(ring.me + by, Y)
-        block = lax.dot_general(
-            low, rows_of(w_s, to * inner, inner)[...], (((1,), (1,)), ((), ())),
-            preferred_element_type=F32,
-        )
-        place = rows_of(gg_ref, ring.me * q, q)
-        if by:
-            blocks[j] = block
-            swaps.append(push(blocks.at[j], place, *sem[2:4], j, (ring.dp, to)))
-        else:
-            place[...] = block
-    each(n - 2, n, total.first_relay)
     each(0, n, total.second)
     each(0, n, total.second_relay)
     each(0, n, lambda k: total.result(k, share_ref, k))
     for copy in swaps:
         copy.wait_recv()
+    for copy in keeps:
+        copy.wait()
     for copy in swaps:
         copy.wait_send()
     ring.finish()
@@ -425,16 +449,20 @@
             jax.ShapeDtypeStruct((48, n * STEP), F32),
             jax.ShapeDtypeStruct((1, columns), F32),
         ],
-        in_specs=[vmem, hbm, hbm, vmem, hbm] + [hbm] * len(grads),
-        out_specs=[vmem] * 4,
+        in_specs=[hbm, hbm, hbm, vmem, hbm] + [hbm] * len(grads),
+        out_specs=[vmem, hbm, vmem, vmem],
         scratch_shapes=[
             pltpu.VMEM((quarter, columns), source.dtype),
             pltpu.VMEM((quarter, columns), base.dtype),
             pltpu.VMEM(w_full.shape, w_full.dtype),
         ]
         + ring_scratch(quarter, columns)
-        + [pltpu.VMEM((3, quarter, inner), F32), pltpu.SemaphoreType.DMA((3,))]
-        + sems(12, 3)
+        + [
+            pltpu.VMEM((quarter, columns), F32),
+            pltpu.VMEM((2, 4, quarter // 2, inner), F32),
+            pltpu.SemaphoreType.DMA((10,)),
+        ]
+        + sems(12, 12)
         + scatter_scratch(n, STEP),
         compiler_params=pltpu.CompilerParams(
             collective_id=call_id, has_side_effects=True, vmem_limit_bytes=56 << 20
@@ -448,33 +476,33 @@
 ):
     ins, refs = refs[:count], refs[count:]
     out_ref, out_share_ref, share_ref, sums_ref = refs[:4]
-    source_s, opp, nbr, held, wide_s, landed, csem, *sem = refs[4:15]
-    bufs, arrived, asem, bsem = refs[15:19]
-    here, ring = Place(), YRing(x_ref.shape[0], *sem[0:2])
-    total = ScatterSum(here, scatter_sources(ins, pieces), *refs[19:])
+    source_s, opp, nbr, held, own_s, mine_s, wide_s, landed, csem, *sem = refs[4:17]
+    bufs, arrived, asem, bsem = refs[17:21]
+    here, ring = Place(), YRing(x_ref.shape[0], 1, *sem[0:2])
+    total = ScatterSum(here, scatter_sources(ins, pieces), *refs[21:])
     tiny = SmallSum(here, bufs, arrived, asem, bsem)
     n, first = total.n, wide_s.shape[1] // STEP
     meet(ring.neighbours() + here.peers() + tiny.far)
-    ring.start(x_ref, opp, nbr)
+    ring.start(x_ref, opp, nbr, 0)
     q, h = ring.quarter, ring.half
-    copy = load(rows_of(source_ref, ring.me * q, q), source_s, csem.at[0])
+    ring.fetch(x_ref, held, own_s, csem)
+    copy = load(rows_of(source_ref, ring.me * q, q), source_s, csem.at[3])
     for k in range(n):
         total.exchange(k)
     each(0, n // 2, total.first)
-    ring.relay(x_ref, opp, nbr, held)
+    ring.relay(opp, nbr, held, 0)
     each(n // 2, n, total.first)
     each(0, n - 2, total.first_relay)
     copy.wait()
     block = lambda owner, part: rows_of(out_ref, owner * q + part * h, h)
     sums = 0.0
     for part in (0, 1):
-        at = slice(part * h, part * h + h)
-        value, more = norm_back(
-            ring.collect(x_ref, nbr, part), source_s[at, :], base_ref[at, :], gain_ref[...]
-        )
-        block(ring.me, part)[...] = value
-        ring.spread(part, block)
+        at, value = ring.collect(own_s, nbr, part, 0)
+        value, more = norm_back(value, source_s[at, :], base_ref[at, :], gain_ref[...])
+        mine_s[at, :] = value
+        ring.spread(part, mine_s, block)
         sums = sums + more
+    kept = load(mine_s, rows_of(out_ref, ring.me * q, q), csem.at[4])
     bufs[0, 0:1, :] = sums
     bufs[0, 1:2, :] = other_ref[...]
     bufs[0, 8:16, :] = jnp.zeros_like(bufs[0, 8:16, :])
@@ -482,11 +510,10 @@
     bufs[0, 3:9, :] = fall_ref[0:6, :]
     lane = lax.broadcasted_iota(jnp.int32, (1, PAIR), 1)
     both = jnp.sum(square_ref[...], axis=1, keepdims=True)
-    total_of = lambda at, value: jnp.where(lane == bucket_ref[0] + at * NBUCKET, value, 0.0)
-    bufs[0, 2:3, 0:PAIR] = total_of(0, jnp.sum(more_ref[...], axis=1, keepdims=True))
-    bufs[0, 9:10, 0:PAIR] = (
-        total_of(0, both[0:1]) + total_of(1, both[1:2]) + total_of(2, length_ref[0].astype(F32))
-    )
+    in_bucket = lambda value: jnp.where(lane == bucket_ref[0], value, 0.0)
+    bufs[0, 2:3, 0:PAIR] = in_bucket(jnp.sum(more_ref[...], axis=1, keepdims=True))
+    for at, value in enumerate((both[0:1], both[1:2], length_ref[0].astype(F32))):
+        bufs[0, 9:10, at * PAIR : at * PAIR + PAIR] = in_bucket(value)
     bufs[0, 10:11, 0:PAIR] = bias_ref[...]
     tiny.send(0)
     each(n - 2, n, total.first_relay)
@@ -516,6 +543,7 @@
     rows = lax.broadcasted_iota(jnp.int32, sums_ref.shape, 0)
     sums_ref[...] = jnp.where(rows < 3, bufs[4], bufs[3])
     ring.arrive()
+    kept.wait()
     for copy in swaps:
         copy.wait_send()
     tiny.finish()
@@ -539,14 +567,16 @@
             jax.ShapeDtypeStruct((48, shares), F32),
             jax.ShapeDtypeStruct((16, columns), F32),
         ],
-        in_specs=[vmem, hbm, vmem, vmem] + [vmem] * 5 + [smem] * 2 + [hbm] * len(grads),
-        out_specs=[vmem] * 4,
+        in_specs=[hbm, hbm, vmem, vmem] + [vmem] * 5 + [smem] * 2 + [hbm] * len(grads),
+        out_specs=[hbm] + [vmem] * 3,
         scratch_shapes=[pltpu.VMEM((quarter, columns), source.dtype)]
         + ring_scratch(quarter, columns)
         + [
+            pltpu.VMEM((quarter, columns), F32),
+            pltpu.VMEM((quarter, columns), F32),
             pltpu.VMEM((48, wide), F32),
             pltpu.VMEM((3, 48, inner), F32),
-            pltpu.SemaphoreType.DMA((1,)),
+            pltpu.SemaphoreType.DMA((5,)),
         ]
         + sems(12, 3)
         + [pltpu.VMEM((5, 16, columns), F32), pltpu.VMEM((10, 16, columns), F32)]
@@ -798,8 +828,9 @@
         out = jnp.where(first, both[0], both[1])
         att_ref[at, :] = out
         gs[step, me, at, :] = (out * sig_ref[at, :]).astype(jnp.bfloat16).astype(F32)
-    for j in range(4):
-        gate(step, j).start()
+        if n % half == 0:
+            gate(step, n // half - 1).start()
+            gate(step, n // half + 1).start()
 
     @pl.when(step == 0)
     def _():
@@ -1180,10 +1211,11 @@
 
 
 def backward_kernel(
-    length_ref, gg_ref, low_ref, qn_ref, kn_ref, v_ref, sig_ref, att_ref, stat_ref,
+    length_ref, gg_ref, low_in, qn_ref, kn_ref, v_ref, sig_ref, att_ref, stat_ref,
     decay_ref, wq_ref, wk_ref, wv_ref, wo_ref, wf_ref, own_ref, gated_ref, layer_ref,
     back_out, four_out, gout_out, gf_ref, bias_ref, out_ref,
-    k_s, do_s, line_s, dq_s, dk_s, dv_s, all_s, fall_s, w_s, wf_s, lay_s, back_ref, wide_s, osem, *sem,
+    k_s, do_s, line_s, dq_s, dk_s, dv_s, all_s, fall_s, w_s, wf_s, lay_s, back_ref, wide_s, low_ref, osem,
+    *sem,
 ):
     step = pl.program_id(0)
     seq, width = low_ref.shape
@@ -1199,14 +1231,20 @@
             (me, 0, right), (me, 1, right), (me, 0, left), (me, 1, left), (left, 0, right), (right, 1, left)
         )[j]
         piece = rows_of(lay_s, owner * q + part * h, h)
-        return link(piece, piece, *sem, j, (dp, to))
+        source = layer_ref.at[part * h : part * h + h] if j < 4 else piece
+        return link(source, piece, *sem, j, (dp, to))
+
+    def fetch(j):
+        pair = ((layer_ref, rows_of(lay_s, me * q, q)), (low_in, low_ref))[j]
+        return pltpu.make_async_copy(*pair, osem.at[5 + j])
 
     @pl.when(step == 0)
     def _():
-        rows_of(lay_s, me * q, q)[...] = layer_ref[...]
         meet([(dp, right), (dp, left)])
         for j in range(4):
             spread(j).start()
+        for j in (0, 1):
+            fetch(j).start()
 
     @pl.when(step == 1)
     def _():
@@ -1283,6 +1321,11 @@
     all_s[:, part(2)] = dv_s[...].astype(low16)
     slot = lax.rem(step, 2)
 
+    @pl.when(step == 0)
+    def _():
+        for j in (0, 1):
+            fetch(j).wait()
+
     def flush(j, at, step):
         columns = pl.ds(pl.multiple_of(step * wide, wide), wide)
         out = (four_out, gout_out)[j].at[:, columns]
@@ -1339,9 +1382,9 @@
     return local_call(
         backward_kernel,
         heads // PAIR,
-        [lanes, full] + [lanes] * 6 + [whole((2, seq, PAIR))] + [weights] * 4
+        [lanes, HBM] + [lanes] * 6 + [whole((2, seq, PAIR))] + [weights] * 4
         + [whole(wf.shape), whole(own.shape)]
-        + [pl.BlockSpec((own.shape[0], 4 * PAIR), lambda i, _: (lax.axis_index("mp"), i)), whole(layer.shape)],
+        + [pl.BlockSpec((own.shape[0], 4 * PAIR), lambda i, _: (lax.axis_index("mp"), i)), HBM],
         [HBM, HBM, HBM, whole((8, width)), whole((1, PAIR)), full],
         [
             struct(seq, width), struct(width, 4 * heads), struct(width, width), struct(8, width),
@@ -1361,7 +1404,8 @@
             pltpu.VMEM((seq, width), F32),
             pltpu.VMEM((seq, width), F32),
             pltpu.VMEM((2, 2, width, 4 * PAIR), F32),
-            pltpu.SemaphoreType.DMA((5,)),
+            pltpu.VMEM((seq, width), low16),
+            pltpu.SemaphoreType.DMA((7,)),
         ]
         + sems(6),
         62, 14, 50, call_id,
@@ -1371,7 +1415,7 @@
 def finish_kernel(
     grad_in, layer_in, wout_in, four_in, mlp_in, sums_in,
     grad_ref, layer_ref, wout_ref, q_ref, k_ref, v_ref, o_ref, gate_ref, up_ref, down_ref,
-    gain_ref, gain2_ref, fall_ref,
+    gain_ref, gain2_ref, fall_ref, rms_ref, bias_ref,
     sem,
 ):
     rows = grad_in.shape[0] // 4
@@ -1380,14 +1424,14 @@
         for src, dst, at in ((grad_in, grad_ref, j), (layer_in, layer_ref, 4 + j)):
             part = slice(j * rows, j * rows + rows)
             copies.append(load(src.at[part], dst.at[part], sem.at[at]))
-    wout_ref[...] = wout_in[...].T
+    wout_ref[...] = wout_in[...]
     inner = q_ref.shape[1]
     for j, ref in enumerate((q_ref, k_ref, v_ref, o_ref)):
         for pair in range(inner // PAIR):
             lane = (pair * 4 + j) * PAIR
             ref[:, pair * PAIR : pair * PAIR + PAIR] = four_in[:, lane : lane + PAIR]
     units = gate_ref.shape[1]
-    down_ref[...] = mlp_in[:, 0:units].T
+    down_ref[...] = mlp_in[:, 0:units]
     gate_ref[...] = mlp_in[:, units : 2 * units]
     up_ref[:, 0:STEP] = mlp_in[:, 2 * units : 2 * units + STEP]
     up_ref[:, STEP:] = four_in[:, 4 * inner : 4 * inner + STEP]
@@ -1400,7 +1444,11 @@
     )
     gain_ref[...] = own[0:1]
     gain2_ref[...] = own[1:2]
-    fall_ref[...] = own[3 : 3 + fall_ref.shape[1]].T
+    fall_ref[...] = own[3 : 3 + fall_ref.shape[0]]
+    square = lambda row, at: sums_in[row : row + 1, at * PAIR : at * PAIR + NBUCKET]
+    squares = jnp.concatenate([square(9, 0), square(9, 1), square(2, 0)], axis=0)
+    rms_ref[...] = jnp.sqrt(squares / (square(9, 2) * width))
+    bias_ref[...] = sums_in[10:11, 0 : bias_ref.shape[1]]
     for copy in copies:
         copy.wait()
 
@@ -1411,14 +1459,14 @@
     return pl.pallas_call(
         finish_kernel,
         out_shape=[
-            struct(*grad.shape), struct(*layer.shape, t=layer.dtype), struct(inner, rows),
-            *[struct(rows, inner)] * 4, struct(rows, units), struct(rows, units), struct(units, rows),
-            struct(1, rows), struct(1, rows), struct(rows, heads),
+            struct(*grad.shape), struct(*layer.shape, t=layer.dtype), *[struct(rows, inner)] * 5,
+            *[struct(rows, units)] * 3, struct(1, rows), struct(1, rows), struct(heads, rows),
+            struct(3, NBUCKET), struct(1, heads),
         ],
         in_specs=[HBM, HBM] + [VMEM] * 4,
-        out_specs=[HBM, HBM] + [VMEM] * 11,
+        out_specs=[HBM, HBM] + [VMEM] * 13,
         scratch_shapes=[pltpu.SemaphoreType.DMA((8,))],
-        compiler_params=pltpu.CompilerParams(vmem_limit_bytes=16 << 20),
+        compiler_params=pltpu.CompilerParams(vmem_limit_bytes=60 << 20),
     )(grad, layer, out_share, share, mlp_share, sums)
 
 
@@ -1427,7 +1475,6 @@
     w_forget, b_forget, w_out, gain_mlp, w_gate, w_up, w_down,
 ):
     x, cotangent = tokens[0], out_cotangent[0]
-    model_width = x.shape[1]
     heads = w_forget.shape[1]
     gain_in, gain_mid = gain_attn[None], gain_mlp[None]
     weights = (w_query, w_key, w_value, w_outgate, w_forget.T)
@@ -1455,10 +1502,8 @@
     )
     (
         input_grad, layer_out, g_out, g_query, g_key, g_value, g_outgate, g_gate, g_up, g_down,
-        g_gain, g_gain_mid, g_fall,
+        g_gain, g_gain_mid, g_fall, rms, bias,
     ) = finish(input_grad, layer_out, out_share, share, mlp_share, sums, heads)
-    totals = jnp.stack([sums[9, :NBUCKET], sums[9, NBUCKET : 2 * NBUCKET], sums[2, :NBUCKET]])
-    rms = jnp.sqrt(totals / (sums[9, 2 * NBUCKET : 3 * NBUCKET] * model_width)[None, :])
     return (
         layer_out[None],
         input_grad[None],
@@ -1467,13 +1512,13 @@
         g_key,
         g_value,
         g_outgate,
-        g_fall,
-        sums[10, :heads],
-        g_out,
+        g_fall.T,
+        bias[0],
+        g_out.T,
         g_gain_mid[0],
         g_gate,
         g_up,
-        g_down,
+        g_down.T,
         rms,
     )
 

time: 365 us -> 559 us (1.53)
  Pallas kernels: 350 us -> 554 us
  local copies, waits for them, and re-layouts: 10.5 us -> 1.89 us
    pallas_call x1, Pallas kernels: 4.25 us -> 218 us  [finish(): pl.pallas_call(finish_kernel, out_shape=[struct(*grad.shape), struct(*lay...]
    unnamed x17 -> x2, local copies, waits for them, and re-layouts: 7.39 us -> 0.01 us
where the time goes in v5:
time: 559 us; the launch traced here: 558 us
  Pallas kernels  554 us (99%)
    pallas_call x1, Pallas kernels, finish(): pl.pallas_call(finish_kernel, out_shape=[struct(*grad.shape), struct(*lay...  218 us
    pallas_call x1, Pallas kernels, reduce_input(): pl.pallas_call(functools.partial(input_kernel, pieces, len(grads)), out_s...  93.1 us
    pallas_call x1, Pallas kernels, reduce_middle(): pl.pallas_call(functools.partial(middle_kernel, pieces, len(grads)), out_...  65.4 us
    pallas_call x1, Pallas kernels, forward_attention(): local_call(forward_kernel, heads // PAIR, [whole((seq, width)), whole((1,...  61.3 us
    pallas_call x1, Pallas kernels, backward_attention(): local_call(backward_kernel, heads // PAIR, [lanes, HBM] + [lanes] * 6 + [...  55.2 us
    pallas_call x1, Pallas kernels, mlp_backward(): pl.pallas_call(mlp_backward_kernel, in_specs=[smem] + [HBM] * 10, out_spe...  41.7 us
    pallas_call x1, Pallas kernels, mlp_forward(): pl.pallas_call(mlp_forward_kernel, in_specs=[smem, HBM, HBM, HBM, VMEM] +...  19.9 us

profile of v5, /device:TPU:0, one launch (start us, length us, event | category | flops | bytes accessed | tf_op | source)
XLA Modules:
  0.0 558.5 jit_solution(3849899495373764083)
XLA Ops:
  1.3 1.3 broadcast_in_dim.15.gain_ref
  2.6 0.0 copy-start
  2.6 61.3 %shard_map.271 = (bf16[768,1536]{1,0:T(8,128)(2,1)}, f32[768,384]{1,0:T(8,128)}, f32[768,384]{1,0:T(8,128)}, bf16[768,384]{1,0:T(8,128)(2,1)}, f32[768,384]{1,0:...) custom-call(s32[1]{0:T(128)S(6)} %copy.31.length_ref, ...), custom_call_target="tpu_custom_call" | custom-call | flops 6000000000 | bytes 20000000 | tf_op jit(solution)/shard_map/pallas_call | solution.py:897
  63.9 0.0 copy-done
  63.9 0.6 broadcast_in_dim.17.gain_ref
  64.5 19.9 %shard_map.272 = (f32[768,1536]{1,0:T(8,128)}, bf16[768,1536]{1,0:T(8,128)(2,1)}, bf16[768,1536]{1,0:T(8,128)(2,1)}, f32[768,1024]{1,0:T(8,128)}, f32[768,1024]{...) custom-call(s32[1]{0:T(128)S(6)} %copy.31.length_ref, ...), custom_call_target="tpu_custom_call" | custom-call | tf_op jit(solution)/shard_map/pallas_call | solution.py:1024
  84.4 41.7 %shard_map.273 = (f32[768,1536]{1,0:T(8,128)}, f32[1536,1024]{1,0:T(8,128)}, f32[1536,1024]{1,0:T(8,128)}, f32[1536,1024]{1,0:T(8,128)}, f32[192,1536]{1,0:T(8,128)}, /*index=5*/f32[1,1536]{1,0:T(1,128)}) custom-call(s32[1]{0:T(128)S(6)} %copy.31.length_ref, bf16[768,1536]{1,0:T(8,128)(2,1)} %get-tuple-element.70.grad_in.base_ref, ...), custom_call_target="tpu_custom_call" | custom-call | tf_op jit(solution)/shard_map/pallas_call | solution.py:1194
  126.2 65.4 %shard_map.274 = (f32[192,1536]{1,0:T(8,128)}, f32[768,384]{1,0:T(8,128)}, f32[48,2560]{1,0:T(8,128)}, f32[1,1536]{1,0:T(1,128)}) custom-call(f32[768,1536]{1,0:T(8,128)} %get-tuple-element.77.x_ref, f32[768,1536]{1,0:T(8,128)} %get-tuple-element.76.mid_ref.source_ref, bf16[768,1536]{1,0:T(8,128)(2,1)} %get-tuple-element.70.grad_in.base_ref, ...), custom_call_target="tpu_custom_call" | custom-call | tf_op jit(solution)/shard_map/pallas_call | solution.py:444
  191.6 55.2 %shard_map.275 = (f32[768,1536]{1,0:T(8,128)}, f32[1536,1536]{1,0:T(8,128)}, f32[1536,1536]{1,0:T(8,128)}, f32[8,1536]{1,0:T(8,128)}, f32[1,128]{1,0:T(1,128)}, /*index=5*/bf16[768,1536]{1,0:T(8,128)(2,1)}) custom-call(s32[1]{0:T(128)S(6)} %copy.31.length_ref, f32[768,384]{1,0:T(8,128)} %get-tuple-element.81.gg_ref, ...), custom_call_target="tpu_custom_call" | custom-call | flops 14000000000 | bytes 50000000 | tf_op jit(solution)/shard_map/pallas_call | solution.py:1382
  247.4 93.1 %shard_map.276 = (f32[768,1536]{1,0:T(8,128)}, f32[48,384]{1,0:T(8,128)}, f32[48,2048]{1,0:T(8,128)}, f32[16,1536]{1,0:T(8,128)}) custom-call(f32[768,1536]{1,0:T(8,128)} %get-tuple-element.92.x_ref, bf16[768,1536]{1,0:T(8,128)(2,1)} %bitcast.14, f32[192,1536]{1,0:T(8,128)} %get-tuple-element.90.own_ref.base_ref, bf16[1,1536]{1,0:T(2,128)(2,1)} %broadcast_in_dim.15.gain_ref, ...), custom_call_target="tpu_custom_call" | custom-call | tf_op jit(solution)/shard_map/pallas_call | solution.py:562
  340.5 217.8 %shard_map.277 = (f32[768,1536]{1,0:T(8,128)}, bf16[768,1536]{1,0:T(8,128)(2,1)}, f32[48,384]{1,0:T(8,128)}, f32[48,384]{1,0:T(8,128)}, f32[48,384]{1,0:T(8,128)...) custom-call(f32[768,1536]{1,0:T(8,128)} %get-tuple-element.100.grad_, ...), custom_call_target="tpu_custom_call" | custom-call | tf_op jit(solution)/shard_map/pallas_call | solution.py:1459
Async XLA Ops:
  2.6 61.4 %copy-start = (bf16[1536]{0:T(1024)(128)(2,1)S(1)}, bf16[1536]{0:T(1024)(128)(2,1)}, u32[]{:S(2)}) copy-start(bf16[1536]{0:T(1024)(128)(2,1)} %param.28) | copy-start | bytes 9220

commit v6 on v5

--- a/solution.py
+++ b/solution.py
@@ -1416,14 +1416,14 @@
     grad_in, layer_in, wout_in, four_in, mlp_in, sums_in,
     grad_ref, layer_ref, wout_ref, q_ref, k_ref, v_ref, o_ref, gate_ref, up_ref, down_ref,
     gain_ref, gain2_ref, fall_ref, rms_ref, bias_ref,
-    sem,
+    grad_s, layer_s, sem,
 ):
     rows = grad_in.shape[0] // 4
-    copies = []
-    for j in range(4):
-        for src, dst, at in ((grad_in, grad_ref, j), (layer_in, layer_ref, 4 + j)):
-            part = slice(j * rows, j * rows + rows)
-            copies.append(load(src.at[part], dst.at[part], sem.at[at]))
+    parts = [slice(j * rows, j * rows + rows) for j in range(4)]
+    come, copies = [], []
+    for src, mid, dst in ((grad_in, grad_s, grad_ref), (layer_in, layer_s, layer_ref)):
+        for part in parts:
+            come.append((load(src.at[part], mid.at[part], sem.at[len(come)]), mid.at[part], dst.at[part]))
     wout_ref[...] = wout_in[...]
     inner = q_ref.shape[1]
     for j, ref in enumerate((q_ref, k_ref, v_ref, o_ref)):
@@ -1449,6 +1449,9 @@
     squares = jnp.concatenate([square(9, 0), square(9, 1), square(2, 0)], axis=0)
     rms_ref[...] = jnp.sqrt(squares / (square(9, 2) * width))
     bias_ref[...] = sums_in[10:11, 0 : bias_ref.shape[1]]
+    for arrived, mid, dst in come:
+        arrived.wait()
+        copies.append(load(mid, dst, sem.at[8 + len(copies)]))
     for copy in copies:
         copy.wait()
 
@@ -1465,7 +1468,11 @@
         ],
         in_specs=[HBM, HBM] + [VMEM] * 4,
         out_specs=[HBM, HBM] + [VMEM] * 13,
-        scratch_shapes=[pltpu.SemaphoreType.DMA((8,))],
+        scratch_shapes=[
+            pltpu.VMEM(grad.shape, grad.dtype),
+            pltpu.VMEM(layer.shape, layer.dtype),
+            pltpu.SemaphoreType.DMA((16,)),
+        ],
         compiler_params=pltpu.CompilerParams(vmem_limit_bytes=60 << 20),
     )(grad, layer, out_share, share, mlp_share, sums)
 

time: 559 us -> 349 us (0.62)
  Pallas kernels: 554 us -> 345 us
    pallas_call x1, Pallas kernels: 218 us -> 8.17 us  [finish(): pl.pallas_call(finish_kernel, out_shape=[struct(*grad.shape), struct(*lay...]
where the time goes in v6:
time: 349 us
  Pallas kernels  345 us (99%)
    pallas_call x1, Pallas kernels, reduce_input(): pl.pallas_call(functools.partial(input_kernel, pieces, len(grads)), out_s...  93.1 us
    pallas_call x1, Pallas kernels, reduce_middle(): pl.pallas_call(functools.partial(middle_kernel, pieces, len(grads)), out_...  65.4 us
    pallas_call x1, Pallas kernels, forward_attention(): local_call(forward_kernel, heads // PAIR, [whole((seq, width)), whole((1,...  61.3 us
    pallas_call x1, Pallas kernels, backward_attention(): local_call(backward_kernel, heads // PAIR, [lanes, HBM] + [lanes] * 6 + [...  55.2 us
    pallas_call x1, Pallas kernels, mlp_backward(): pl.pallas_call(mlp_backward_kernel, in_specs=[smem] + [HBM] * 10, out_spe...  41.7 us
    pallas_call x1, Pallas kernels, mlp_forward(): pl.pallas_call(mlp_forward_kernel, in_specs=[smem, HBM, HBM, HBM, VMEM] +...  19.9 us
    pallas_call x1, Pallas kernels, finish(): pl.pallas_call(finish_kernel, out_shape=[struct(*grad.shape), struct(*lay...  8.17 us

profile of v6, /device:TPU:0, one launch (start us, length us, event | category | flops | bytes accessed | tf_op | source)
XLA Modules:
  0.0 348.9 jit_solution(1107608114032986152)
XLA Ops:
  1.3 1.3 broadcast_in_dim.15.gain_ref
  2.6 0.0 copy-start
  2.6 61.3 %shard_map.271 = (bf16[768,1536]{1,0:T(8,128)(2,1)}, f32[768,384]{1,0:T(8,128)}, f32[768,384]{1,0:T(8,128)}, bf16[768,384]{1,0:T(8,128)(2,1)}, f32[768,384]{1,0:...) custom-call(s32[1]{0:T(128)S(6)} %copy.31.length_ref, ...), custom_call_target="tpu_custom_call" | custom-call | flops 6000000000 | bytes 20000000 | tf_op jit(solution)/shard_map/pallas_call | solution.py:897
  63.9 0.0 copy-done
  63.9 0.6 broadcast_in_dim.17.gain_ref
  64.5 19.9 %shard_map.272 = (f32[768,1536]{1,0:T(8,128)}, bf16[768,1536]{1,0:T(8,128)(2,1)}, bf16[768,1536]{1,0:T(8,128)(2,1)}, f32[768,1024]{1,0:T(8,128)}, f32[768,1024]{...) custom-call(s32[1]{0:T(128)S(6)} %copy.31.length_ref, ...), custom_call_target="tpu_custom_call" | custom-call | tf_op jit(solution)/shard_map/pallas_call | solution.py:1024
  84.4 41.7 %shard_map.273 = (f32[768,1536]{1,0:T(8,128)}, f32[1536,1024]{1,0:T(8,128)}, f32[1536,1024]{1,0:T(8,128)}, f32[1536,1024]{1,0:T(8,128)}, f32[192,1536]{1,0:T(8,128)}, /*index=5*/f32[1,1536]{1,0:T(1,128)}) custom-call(s32[1]{0:T(128)S(6)} %copy.31.length_ref, bf16[768,1536]{1,0:T(8,128)(2,1)} %get-tuple-element.70.grad_in.base_ref, ...), custom_call_target="tpu_custom_call" | custom-call | tf_op jit(solution)/shard_map/pallas_call | solution.py:1194
  126.2 65.4 %shard_map.274 = (f32[192,1536]{1,0:T(8,128)}, f32[768,384]{1,0:T(8,128)}, f32[48,2560]{1,0:T(8,128)}, f32[1,1536]{1,0:T(1,128)}) custom-call(f32[768,1536]{1,0:T(8,128)} %get-tuple-element.77.x_ref, f32[768,1536]{1,0:T(8,128)} %get-tuple-element.76.mid_ref.source_ref, bf16[768,1536]{1,0:T(8,128)(2,1)} %get-tuple-element.70.grad_in.base_ref, ...), custom_call_target="tpu_custom_call" | custom-call | tf_op jit(solution)/shard_map/pallas_call | solution.py:444
  191.6 55.2 %shard_map.275 = (f32[768,1536]{1,0:T(8,128)}, f32[1536,1536]{1,0:T(8,128)}, f32[1536,1536]{1,0:T(8,128)}, f32[8,1536]{1,0:T(8,128)}, f32[1,128]{1,0:T(1,128)}, /*index=5*/bf16[768,1536]{1,0:T(8,128)(2,1)}) custom-call(s32[1]{0:T(128)S(6)} %copy.31.length_ref, f32[768,384]{1,0:T(8,128)} %get-tuple-element.81.gg_ref, ...), custom_call_target="tpu_custom_call" | custom-call | flops 14000000000 | bytes 50000000 | tf_op jit(solution)/shard_map/pallas_call | solution.py:1382
  247.4 93.1 %shard_map.276 = (f32[768,1536]{1,0:T(8,128)}, f32[48,384]{1,0:T(8,128)}, f32[48,2048]{1,0:T(8,128)}, f32[16,1536]{1,0:T(8,128)}) custom-call(f32[768,1536]{1,0:T(8,128)} %get-tuple-element.92.x_ref, bf16[768,1536]{1,0:T(8,128)(2,1)} %bitcast.14, f32[192,1536]{1,0:T(8,128)} %get-tuple-element.90.own_ref.base_ref, bf16[1,1536]{1,0:T(2,128)(2,1)} %broadcast_in_dim.15.gain_ref, ...), custom_call_target="tpu_custom_call" | custom-call | tf_op jit(solution)/shard_map/pallas_call | solution.py:562
  340.5 8.2 %shard_map.277 = (f32[768,1536]{1,0:T(8,128)}, bf16[768,1536]{1,0:T(8,128)(2,1)}, f32[48,384]{1,0:T(8,128)}, f32[48,384]{1,0:T(8,128)}, f32[48,384]{1,0:T(8,128)...) custom-call(f32[768,1536]{1,0:T(8,128)} %get-tuple-element.100.grad_, ...), custom_call_target="tpu_custom_call" | custom-call | tf_op jit(solution)/shard_map/pallas_call | solution.py:1462
Async XLA Ops:
  2.6 61.4 %copy-start = (bf16[1536]{0:T(1024)(128)(2,1)S(1)}, bf16[1536]{0:T(1024)(128)(2,1)}, u32[]{:S(2)}) copy-start(bf16[1536]{0:T(1024)(128)(2,1)} %param.28) | copy-start | bytes 9220

commit v7 on v5

--- a/solution.py
+++ b/solution.py
@@ -64,7 +64,8 @@
         return [(self.dp, self.right), (self.dp, self.left)]
 
     def send(self, name, wave, src, dst, to):
-        at = wave * 6 + STEPS.index(name)
+        kind, index = divmod(STEPS.index(name), 6)
+        at = kind * 12 + wave * 6 + index
         self.sent[name, wave] = push(src, dst, *self.sems, at, (self.dp, to))
 
     def rows(self, x, owner, part, wave):
@@ -106,21 +107,25 @@
         at = slice(start, start + self.tall)
         return at, own[at, :] + nbr[0, at] + nbr[1, at]
 
-    def spread(self, part, own, block):
-        into, tag = block(self.me, part), "ab"[part]
-        mine = own.at[part * self.half : part * self.half + self.half]
-        self.send("gR" + tag, 0, mine, into, self.right)
-        self.send("gL" + tag, 0, mine, into, self.left)
-
-    def forward(self, block):
-        self.sent["gRa", 0].wait_recv()
-        self.send("fR", 0, block(self.left, 0), block(self.left, 0), self.right)
-        self.sent["gLb", 0].wait_recv()
-        self.send("fL", 0, block(self.right, 1), block(self.right, 1), self.left)
-
-    def arrive(self):
+    def spread(self, part, wave, own, out):
+        tag, into = "ab"[part], self.rows(out, self.me, part, wave)
+        start = part * self.half + wave * self.tall
+        mine = own.at[start : start + self.tall]
+        self.send("gR" + tag, wave, mine, into, self.right)
+        self.send("gL" + tag, wave, mine, into, self.left)
+
+    def forward(self, wave, out):
+        for come, go, owner, part, to in (
+            ("gRa", "fR", self.left, 0, self.right),
+            ("gLb", "fL", self.right, 1, self.left),
+        ):
+            self.sent[come, wave].wait_recv()
+            block = self.rows(out, owner, part, wave)
+            self.send(go, wave, block, block, to)
+
+    def arrive(self, wave):
         for name in ("gRb", "gLa", "fR", "fL"):
-            self.sent[name, 0].wait_recv()
+            self.sent[name, wave].wait_recv()
 
     def finish(self):
         for copy in self.sent.values():
@@ -478,7 +483,7 @@
     out_ref, out_share_ref, share_ref, sums_ref = refs[:4]
     source_s, opp, nbr, held, own_s, mine_s, wide_s, landed, csem, *sem = refs[4:17]
     bufs, arrived, asem, bsem = refs[17:21]
-    here, ring = Place(), YRing(x_ref.shape[0], 1, *sem[0:2])
+    here, ring = Place(), YRing(x_ref.shape[0], 2, *sem[0:2])
     total = ScatterSum(here, scatter_sources(ins, pieces), *refs[21:])
     tiny = SmallSum(here, bufs, arrived, asem, bsem)
     n, first = total.n, wide_s.shape[1] // STEP
@@ -489,19 +494,20 @@
     copy = load(rows_of(source_ref, ring.me * q, q), source_s, csem.at[3])
     for k in range(n):
         total.exchange(k)
-    each(0, n // 2, total.first)
     ring.relay(opp, nbr, held, 0)
-    each(n // 2, n, total.first)
+    ring.start(x_ref, opp, nbr, 1)
+    each(0, n, total.first)
+    ring.relay(opp, nbr, held, 1)
     each(0, n - 2, total.first_relay)
     copy.wait()
-    block = lambda owner, part: rows_of(out_ref, owner * q + part * h, h)
     sums = 0.0
-    for part in (0, 1):
-        at, value = ring.collect(own_s, nbr, part, 0)
-        value, more = norm_back(value, source_s[at, :], base_ref[at, :], gain_ref[...])
-        mine_s[at, :] = value
-        ring.spread(part, mine_s, block)
-        sums = sums + more
+    for wave in (0, 1):
+        for part in (0, 1):
+            at, value = ring.collect(own_s, nbr, part, wave)
+            value, more = norm_back(value, source_s[at, :], base_ref[at, :], gain_ref[...])
+            mine_s[at, :] = value
+            ring.spread(part, wave, mine_s, out_ref)
+            sums = sums + more
     kept = load(mine_s, rows_of(out_ref, ring.me * q, q), csem.at[4])
     bufs[0, 0:1, :] = sums
     bufs[0, 1:2, :] = other_ref[...]
@@ -514,11 +520,15 @@
     bufs[0, 2:3, 0:PAIR] = in_bucket(jnp.sum(more_ref[...], axis=1, keepdims=True))
     for at, value in enumerate((both[0:1], both[1:2], length_ref[0].astype(F32))):
         bufs[0, 9:10, at * PAIR : at * PAIR + PAIR] = in_bucket(value)
-    bufs[0, 10:11, 0:PAIR] = bias_ref[...]
+    diagonal = lax.broadcasted_iota(jnp.int32, bias_ref.shape, 0) == lax.broadcasted_iota(
+        jnp.int32, bias_ref.shape, 1
+    )
+    bufs[0, 10:11, 0:PAIR] = jnp.sum(jnp.where(diagonal, bias_ref[...], 0.0), axis=0, keepdims=True)
     tiny.send(0)
     each(n - 2, n, total.first_relay)
+    ring.forward(0, out_ref)
     each(0, n, total.second)
-    ring.forward(block)
+    ring.forward(1, out_ref)
     tiny.take(0)
     tiny.send(1)
     each(0, n, total.second_relay)
@@ -542,7 +552,8 @@
     tiny.take(3)
     rows = lax.broadcasted_iota(jnp.int32, sums_ref.shape, 0)
     sums_ref[...] = jnp.where(rows < 3, bufs[4], bufs[3])
-    ring.arrive()
+    ring.arrive(0)
+    ring.arrive(1)
     kept.wait()
     for copy in swaps:
         copy.wait_send()
@@ -578,7 +589,7 @@
             pltpu.VMEM((3, 48, inner), F32),
             pltpu.SemaphoreType.DMA((5,)),
         ]
-        + sems(12, 3)
+        + sems(24, 3)
         + [pltpu.VMEM((5, 16, columns), F32), pltpu.VMEM((10, 16, columns), F32)]
         + sems(10)
         + scatter_scratch(n, STEP),
@@ -619,14 +630,14 @@
 
 
 def running_sum(values, backward=False):
-    count = values.shape[0]
-    row = lax.broadcasted_iota(jnp.int32, values.shape, 0)
+    count = values.shape[1]
+    at = lax.broadcasted_iota(jnp.int32, values.shape, 1)
     shift = 1
     while shift < count:
         if backward:
-            moved = jnp.where(row < count - shift, pltpu.roll(values, count - shift, 0), 0.0)
+            moved = jnp.where(at < count - shift, pltpu.roll(values, count - shift, 1), 0.0)
         else:
-            moved = jnp.where(row >= shift, pltpu.roll(values, shift, 0), 0.0)
+            moved = jnp.where(at >= shift, pltpu.roll(values, shift, 1), 0.0)
         values = values + moved
         shift *= 2
     return values
@@ -753,16 +764,17 @@
         wf_s[...] = jnp.zeros_like(wf_s)
         wf_s[0:heads, :] = wf_ref[...]
         bf_s[...] = jnp.zeros_like(bf_s)
-        bf_s[0:1, 0:heads] = bf_ref[...].astype(F32)
-        pre = mm_t(low_ref[...], wf_s[...]) + bf_s[0:1, :]
+        bf_s[:, 0:heads] = bf_ref[...].astype(F32)
+        pre = mm_t(wf_s[...], low_ref[...])[0:8] + jnp.broadcast_to(bf_s[...], (PAIR, PAIR)).T[0:8, 0:1]
         fall = jnp.minimum(pre, 0.0) - jnp.log1p(jnp.exp(-jnp.abs(pre)))
         decay = running_sum(fall)
-        row = lax.broadcasted_iota(jnp.int32, decay.shape, 0)
-        final = jnp.sum(jnp.where(row == length - 1, decay, 0.0), axis=0, keepdims=True)
+        column = lax.broadcasted_iota(jnp.int32, decay.shape, 1)
         decay_ref[0] = decay
         decay_ref[1] = jax.nn.sigmoid(-pre)
-        top_s[...] = jnp.where(row < length, decay, final)
-        row_s[...] = jnp.where(row < length, decay, -NEG).T[0:8]
+        row_s[...] = jnp.where(column < length, decay, -NEG)
+        final = jnp.sum(jnp.where(column == length - 1, decay, 0.0), axis=1, keepdims=True)
+        top = jnp.where(column < length, decay, final)
+        top_s[...] = jnp.concatenate([top, jnp.zeros((PAIR - 8, seq), F32)], axis=0).T
 
     for j, ref in enumerate((wq_ref, wk_ref, wv_ref, wo_ref)):
         w_s[:, j * PAIR : j * PAIR + PAIR] = ref[...]
@@ -898,11 +910,11 @@
         forward_kernel,
         heads // PAIR,
         [whole((seq, width)), whole((1, width))] + [weights] * 4 + [whole(wf.shape), whole(bf.shape), whole(w_out.shape)],
-        [HBM] + [lanes] * 6 + [whole((2, seq, PAIR)), HBM, HBM],
+        [HBM] + [lanes] * 6 + [whole((2, 8, seq)), HBM, HBM],
         [
             struct(seq, width, t=low), struct(seq, heads), struct(seq, heads), struct(seq, heads, t=low),
             struct(seq, heads), struct(seq, heads), struct(seq, heads),
-            struct(2, seq, PAIR), struct(seq, heads * Y, t=low), struct(heads * Y, width, t=low),
+            struct(2, 8, seq), struct(seq, heads * Y, t=low), struct(heads * Y, width, t=low),
         ],
         [
             pltpu.VMEM((seq, PAIR), F32),
@@ -913,8 +925,8 @@
             pltpu.VMEM((seq, 4 * PAIR), F32),
             pltpu.VMEM((heads // PAIR, Y, seq, PAIR), F32),
             pltpu.VMEM((2, 4, 4, Y, heads // 16, width // 2), F32),
-            pltpu.VMEM((PAIR, width), low),
-            pltpu.VMEM((8, PAIR), F32),
+            pltpu.VMEM((16, width), low),
+            pltpu.VMEM((1, PAIR), F32),
             pltpu.VMEM((seq, width), low),
             pltpu.VMEM((seq, width), low),
             pltpu.VMEM((heads * Y, width), low),
@@ -1214,7 +1226,7 @@
     length_ref, gg_ref, low_in, qn_ref, kn_ref, v_ref, sig_ref, att_ref, stat_ref,
     decay_ref, wq_ref, wk_ref, wv_ref, wo_ref, wf_ref, own_ref, gated_ref, layer_ref,
     back_out, four_out, gout_out, gf_ref, bias_ref, out_ref,
-    k_s, do_s, line_s, dq_s, dk_s, dv_s, all_s, fall_s, w_s, wf_s, lay_s, back_ref, wide_s, low_ref, osem,
+    k_s, do_s, line_s, top_s, dq_s, dk_s, dv_s, all_s, fall_s, w_s, wf_s, lay_s, back_ref, wide_s, low_ref, osem,
     *sem,
 ):
     step = pl.program_id(0)
@@ -1246,7 +1258,7 @@
         for j in (0, 1):
             fetch(j).start()
 
-    @pl.when(step == 1)
+    @pl.when(step == 2)
     def _():
         spread(0).wait_recv()
         spread(4).start()
@@ -1259,9 +1271,11 @@
         wf_s[...] = jnp.zeros_like(wf_s)
         wf_s[0:heads, :] = wf_ref[...]
         decay = decay_ref[0]
-        row = lax.broadcasted_iota(jnp.int32, decay.shape, 0)
-        final = jnp.sum(jnp.where(row == length - 1, decay, 0.0), axis=0, keepdims=True)
-        line_s[...] = jnp.where(row < length, decay, final).T[0:8]
+        column = lax.broadcasted_iota(jnp.int32, decay.shape, 1)
+        final = jnp.sum(jnp.where(column == length - 1, decay, 0.0), axis=1, keepdims=True)
+        line_s[...] = jnp.where(column < length, decay, final)
+        masked = jnp.where(column < length, decay, -NEG)
+        top_s[...] = jnp.concatenate([masked, jnp.zeros((PAIR - 8, seq), F32)], axis=0).T
         fall_s[...] = jnp.zeros_like(fall_s)
 
     base = pl.multiple_of(step * wide, wide)
@@ -1275,13 +1289,12 @@
     k_s[...] = kn_ref[...].astype(low16)
     dk_s[...] = jnp.zeros_like(dk_s)
     dv_s[...] = jnp.zeros_like(dv_s)
-    row = lax.broadcasted_iota(jnp.int32, (seq, PAIR), 0)
     columns, lines = [], [one_row(line_s, 2 * step + head) for head in (0, 1)]
     for head in (0, 1):
         column = jnp.sum(
-            jnp.where(lane_is((seq, PAIR), 2 * step + head), decay_ref[0], 0.0), axis=1, keepdims=True
+            jnp.where(lane_is((seq, PAIR), 2 * step + head), top_s[...], 0.0), axis=1, keepdims=True
         )
-        columns.append(jnp.where(row[:, 0:1] < length, column, -NEG))
+        columns.append(column)
     block = first_head((128, PAIR))
     zero = jnp.zeros((128, PAIR), low16)
     lower = lax.broadcasted_iota(jnp.int32, (128, 128), 0) > lax.broadcasted_iota(
@@ -1348,15 +1361,16 @@
 
     @pl.when(step == pl.num_programs(0) - 1)
     def _():
-        fall = running_sum(fall_s[...], backward=True) * decay_ref[1]
-        fall = fall.astype(low16)
-        bias_ref[...] = jnp.sum(fall.astype(F32), axis=0, keepdims=True)
-        gf_ref[...] = t_mm(fall, low_ref[...])[0:8]
+        fall = running_sum(fall_s[...].T[0:8], backward=True) * decay_ref[1]
+        fall = jnp.concatenate([fall, jnp.zeros_like(fall)], axis=0).astype(low16)
+        bias = jnp.sum(fall.astype(F32), axis=1, keepdims=True)
+        bias_ref[...] = jnp.broadcast_to(bias[0:8], (8, PAIR))
+        gf_ref[...] = mm(fall, low_ref[...])[0:8]
 
         def tail(k, carry):
             rows = rows_at(k, 768)
             back_ref[:, rows] = mm_t(all_s[...], w_s[rows, :])
-            back_ref[:, rows] = back_ref[:, rows] + mm(fall, wf_s[:, rows])
+            back_ref[:, rows] = back_ref[:, rows] + t_mm(fall, wf_s[:, rows])
             return carry
 
         lax.fori_loop(0, width // 768, tail, 0)
@@ -1382,25 +1396,26 @@
     return local_call(
         backward_kernel,
         heads // PAIR,
-        [lanes, HBM] + [lanes] * 6 + [whole((2, seq, PAIR))] + [weights] * 4
+        [lanes, HBM] + [lanes] * 6 + [whole((2, 8, seq))] + [weights] * 4
         + [whole(wf.shape), whole(own.shape)]
         + [pl.BlockSpec((own.shape[0], 4 * PAIR), lambda i, _: (lax.axis_index("mp"), i)), HBM],
-        [HBM, HBM, HBM, whole((8, width)), whole((1, PAIR)), full],
+        [HBM, HBM, HBM, whole((8, width)), whole((8, PAIR)), full],
         [
             struct(seq, width), struct(width, 4 * heads), struct(width, width), struct(8, width),
-            struct(1, PAIR), struct(seq, width, t=low16),
+            struct(8, PAIR), struct(seq, width, t=low16),
         ],
         [
             pltpu.VMEM((seq, PAIR), low16),
             pltpu.VMEM((seq, PAIR), low16),
             pltpu.VMEM((8, seq), F32),
             pltpu.VMEM((seq, PAIR), F32),
+            pltpu.VMEM((seq, PAIR), F32),
             pltpu.VMEM((seq, 2 * PAIR), F32),
             pltpu.VMEM((seq, PAIR), F32),
             pltpu.VMEM((seq, 4 * heads), low16),
             pltpu.VMEM((seq, PAIR), F32),
             pltpu.VMEM((width, 4 * heads), low16),
-            pltpu.VMEM((PAIR, width), low16),
+            pltpu.VMEM((16, width), low16),
             pltpu.VMEM((seq, width), F32),
             pltpu.VMEM((seq, width), F32),
             pltpu.VMEM((2, 2, width, 4 * PAIR), F32),
@@ -1413,18 +1428,27 @@
 
 
 def finish_kernel(
-    grad_in, layer_in, wout_in, four_in, mlp_in, sums_in,
+    grad_in, layer_in, wout_hbm, four_hbm, mlp_hbm, sums_hbm,
     grad_ref, layer_ref, wout_ref, q_ref, k_ref, v_ref, o_ref, gate_ref, up_ref, down_ref,
     gain_ref, gain2_ref, fall_ref, rms_ref, bias_ref,
-    sem,
+    grad_s, layer_s, four_in, mlp_in, sums_in, sem,
 ):
+    copy = copier(sem)
     rows = grad_in.shape[0] // 4
+    parts = [slice(j * rows, j * rows + rows) for j in range(4)]
+    come = [(copy(grad_in.at[p], grad_s.at[p]), grad_s.at[p], grad_ref.at[p]) for p in parts]
+    small = [copy(wout_hbm, wout_ref), copy(four_hbm, four_in), copy(mlp_hbm, mlp_in), copy(sums_hbm, sums_in)]
+    come += [(copy(layer_in.at[p], layer_s.at[p]), layer_s.at[p], layer_ref.at[p]) for p in parts]
     copies = []
-    for j in range(4):
-        for src, dst, at in ((grad_in, grad_ref, j), (layer_in, layer_ref, 4 + j)):
-            part = slice(j * rows, j * rows + rows)
-            copies.append(load(src.at[part], dst.at[part], sem.at[at]))
-    wout_ref[...] = wout_in[...]
+
+    def leave(some):
+        for arrived, mid, dst in some:
+            arrived.wait()
+            copies.append(copy(mid, dst))
+
+    leave(come[0:4])
+    for c in small:
+        c.wait()
     inner = q_ref.shape[1]
     for j, ref in enumerate((q_ref, k_ref, v_ref, o_ref)):
         for pair in range(inner // PAIR):
@@ -1433,8 +1457,8 @@
     units = gate_ref.shape[1]
     down_ref[...] = mlp_in[:, 0:units]
     gate_ref[...] = mlp_in[:, units : 2 * units]
-    up_ref[:, 0:STEP] = mlp_in[:, 2 * units : 2 * units + STEP]
-    up_ref[:, STEP:] = four_in[:, 4 * inner : 4 * inner + STEP]
+    up_ref[...] = four_in[:, 4 * inner : 4 * inner + units]
+    leave(come[4:8])
     share, width = gain_ref.shape[1], sums_in.shape[1]
     row = lax.broadcasted_iota(jnp.int32, (width, share), 0)
     lane = lax.broadcasted_iota(jnp.int32, (width, share), 1)
@@ -1449,13 +1473,13 @@
     squares = jnp.concatenate([square(9, 0), square(9, 1), square(2, 0)], axis=0)
     rms_ref[...] = jnp.sqrt(squares / (square(9, 2) * width))
     bias_ref[...] = sums_in[10:11, 0 : bias_ref.shape[1]]
-    for copy in copies:
-        copy.wait()
+    for c in copies:
+        c.wait()
 
 
 def finish(grad, layer, out_share, share, mlp_share, sums, heads):
     rows, inner = out_share.shape
-    units = mlp_share.shape[1] * 2 // 5
+    units = mlp_share.shape[1] // 2
     return pl.pallas_call(
         finish_kernel,
         out_shape=[
@@ -1463,9 +1487,10 @@
             *[struct(rows, units)] * 3, struct(1, rows), struct(1, rows), struct(heads, rows),
             struct(3, NBUCKET), struct(1, heads),
         ],
-        in_specs=[HBM, HBM] + [VMEM] * 4,
+        in_specs=[HBM] * 6,
         out_specs=[HBM, HBM] + [VMEM] * 13,
-        scratch_shapes=[pltpu.SemaphoreType.DMA((8,))],
+        scratch_shapes=[pltpu.VMEM(a.shape, a.dtype) for a in (grad, layer, share, mlp_share, sums)]
+        + [pltpu.SemaphoreType.DMA((20,))],
         compiler_params=pltpu.CompilerParams(vmem_limit_bytes=60 << 20),
     )(grad, layer, out_share, share, mlp_share, sums)
 
@@ -1488,8 +1513,8 @@
         lengths, grad_rows, mid_low, gate, up, hidden, w_gate, w_up, w_down, mlp_local, middle, 1
     )
     grad_own, gg, mlp_share, mlp_gain = reduce_middle(
-        mid_local, middle, grad_rows, gain_mid, w_full, [g_down, g_gate, g_up],
-        ((0, 0), (0, 1), (1, 0), (1, 1), (2, 0)), 2,
+        mid_local, middle, grad_rows, gain_mid, w_full, [g_down, g_gate],
+        ((0, 0), (0, 1), (1, 0), (1, 1)), 2,
     )
     in_local, g_four, g_out, g_fall, bias, layer_out = backward_attention(
         lengths, gg, low, qn, kn, value, sig, attended, stat, decay, *weights, grad_own, gated,
@@ -1498,7 +1523,7 @@
     small = (mlp_gain, g_fall, squares, mlp_square, bias, lengths, buckets)
     input_grad, out_share, share, sums = reduce_input(
         in_local, x, grad_own, gain_in, small, [g_out, g_four, g_up],
-        ((0, 0), (0, 1), (0, 2), (1, 0), (1, 1), (1, 2), (2, 1)), 4,
+        ((0, 0), (0, 1), (0, 2), (1, 0), (1, 1), (1, 2), (2, 0), (2, 1)), 4,
     )
     (
         input_grad, layer_out, g_out, g_query, g_key, g_value, g_outgate, g_gate, g_up, g_down,

time: 559 us -> 349 us (0.62)
  Pallas kernels: 554 us -> 345 us
    pallas_call x1, Pallas kernels: 218 us -> 7 us  [finish(): pl.pallas_call(finish_kernel, out_shape=[struct(*grad.shape), struct(*lay...]
    pallas_call x1, Pallas kernels: 93.1 us -> 107 us  [reduce_input(): pl.pallas_call(functools.partial(input_kernel, pieces, len(grads)), out_s...]
    pallas_call x1, Pallas kernels: 55.2 us -> 44.5 us  [backward_attention(): local_call(backward_kernel, heads // PAIR, [lanes, HBM] + [lanes] * 6 + [...]
where the time goes in v7:
time: 349 us
  Pallas kernels  345 us (99%)
    pallas_call x1, Pallas kernels, reduce_input(): pl.pallas_call(functools.partial(input_kernel, pieces, len(grads)), out_s...  107 us
    pallas_call x1, Pallas kernels, reduce_middle(): pl.pallas_call(functools.partial(middle_kernel, pieces, len(grads)), out_...  63.6 us
    pallas_call x1, Pallas kernels, forward_attention(): local_call(forward_kernel, heads // PAIR, [whole((seq, width)), whole((1,...  61.4 us
    pallas_call x1, Pallas kernels, backward_attention(): local_call(backward_kernel, heads // PAIR, [lanes, HBM] + [lanes] * 6 + [...  44.5 us
    pallas_call x1, Pallas kernels, mlp_backward(): pl.pallas_call(mlp_backward_kernel, in_specs=[smem] + [HBM] * 10, out_spe...  41.9 us
    pallas_call x1, Pallas kernels, mlp_forward(): pl.pallas_call(mlp_forward_kernel, in_specs=[smem, HBM, HBM, HBM, VMEM] +...  19.9 us
    pallas_call x1, Pallas kernels, finish(): pl.pallas_call(finish_kernel, out_shape=[struct(*grad.shape), struct(*lay...  7 us

profile of v7, /device:TPU:0, one launch (start us, length us, event | category | flops | bytes accessed | tf_op | source)
XLA Modules:
  0.0 349.2 jit_solution(16330867330739939702)
XLA Ops:
  1.3 1.3 broadcast_in_dim.15.gain_ref
  2.6 0.0 copy-start
  2.6 61.4 %shard_map.271 = (bf16[768,1536]{1,0:T(8,128)(2,1)}, f32[768,384]{1,0:T(8,128)}, f32[768,384]{1,0:T(8,128)}, bf16[768,384]{1,0:T(8,128)(2,1)}, f32[768,384]{1,0:...) custom-call(s32[1]{0:T(128)S(6)} %copy.31.length_ref, ...), custom_call_target="tpu_custom_call" | custom-call | flops 6000000000 | bytes 20000000 | tf_op jit(solution)/shard_map/pallas_call | solution.py:909
  64.0 0.0 copy-done
  64.0 0.6 broadcast_in_dim.17.gain_ref
  64.6 19.9 %shard_map.272 = (f32[768,1536]{1,0:T(8,128)}, bf16[768,1536]{1,0:T(8,128)(2,1)}, bf16[768,1536]{1,0:T(8,128)(2,1)}, f32[768,1024]{1,0:T(8,128)}, f32[768,1024]{...) custom-call(s32[1]{0:T(128)S(6)} %copy.31.length_ref, ...), custom_call_target="tpu_custom_call" | custom-call | tf_op jit(solution)/shard_map/pallas_call | solution.py:1036
  84.5 41.9 %shard_map.273 = (f32[768,1536]{1,0:T(8,128)}, f32[1536,1024]{1,0:T(8,128)}, f32[1536,1024]{1,0:T(8,128)}, f32[1536,1024]{1,0:T(8,128)}, f32[192,1536]{1,0:T(8,128)}, /*index=5*/f32[1,1536]{1,0:T(1,128)}) custom-call(s32[1]{0:T(128)S(6)} %copy.31.length_ref, bf16[768,1536]{1,0:T(8,128)(2,1)} %get-tuple-element.70.grad_in.base_ref, ...), custom_call_target="tpu_custom_call" | custom-call | tf_op jit(solution)/shard_map/pallas_call | solution.py:1206
  126.4 63.6 %shard_map.274 = (f32[192,1536]{1,0:T(8,128)}, f32[768,384]{1,0:T(8,128)}, f32[48,2048]{1,0:T(8,128)}, f32[1,1536]{1,0:T(1,128)}) custom-call(f32[768,1536]{1,0:T(8,128)} %get-tuple-element.77.x_ref, f32[768,1536]{1,0:T(8,128)} %get-tuple-element.76.mid_ref.source_ref, bf16[768,1536]{1,0:T(8,128)(2,1)} %get-tuple-element.70.grad_in.base_ref, ...), custom_call_target="tpu_custom_call" | custom-call | tf_op jit(solution)/shard_map/pallas_call | solution.py:449
  189.9 44.5 %shard_map.275 = (f32[768,1536]{1,0:T(8,128)}, f32[1536,1536]{1,0:T(8,128)}, f32[1536,1536]{1,0:T(8,128)}, f32[8,1536]{1,0:T(8,128)}, f32[8,128]{1,0:T(8,128)}, /*index=5*/bf16[768,1536]{1,0:T(8,128)(2,1)}) custom-call(s32[1]{0:T(128)S(6)} %copy.31.length_ref, f32[768,384]{1,0:T(8,128)} %get-tuple-element.80.gg_ref, ...), custom_call_target="tpu_custom_call" | custom-call | flops 14000000000 | bytes 50000000 | tf_op jit(solution)/shard_map/pallas_call | solution.py:1396
  235.1 106.9 %shard_map.276 = (f32[768,1536]{1,0:T(8,128)}, f32[48,384]{1,0:T(8,128)}, f32[48,2560]{1,0:T(8,128)}, f32[16,1536]{1,0:T(8,128)}) custom-call(f32[768,1536]{1,0:T(8,128)} %get-tuple-element.91.x_ref, bf16[768,1536]{1,0:T(8,128)(2,1)} %bitcast.14, f32[192,1536]{1,0:T(8,128)} %get-tuple-element.89.own_ref.base_ref, bf16[1,1536]{1,0:T(2,128)(2,1)} %broadcast_in_dim.15.gain_ref, ...), custom_call_target="tpu_custom_call" | custom-call | tf_op jit(solution)/shard_map/pallas_call | solution.py:573
  342.0 7.0 %shard_map.277 = (f32[768,1536]{1,0:T(8,128)}, bf16[768,1536]{1,0:T(8,128)(2,1)}, f32[48,384]{1,0:T(8,128)}, f32[48,384]{1,0:T(8,128)}, f32[48,384]{1,0:T(8,128)...) custom-call(f32[768,1536]{1,0:T(8,128)} %get-tuple-element.100.grad_, ...), custom_call_target="tpu_custom_call" | custom-call | tf_op jit(solution)/shard_map/pallas_call | solution.py:1483
Async XLA Ops:
  2.6 61.4 %copy-start = (bf16[1536]{0:T(1024)(128)(2,1)S(1)}, bf16[1536]{0:T(1024)(128)(2,1)}, u32[]{:S(2)}) copy-start(bf16[1536]{0:T(1024)(128)(2,1)} %param.28) | copy-start | bytes 9220

commit v8 on v7

--- a/solution.py
+++ b/solution.py
@@ -483,7 +483,7 @@
     out_ref, out_share_ref, share_ref, sums_ref = refs[:4]
     source_s, opp, nbr, held, own_s, mine_s, wide_s, landed, csem, *sem = refs[4:17]
     bufs, arrived, asem, bsem = refs[17:21]
-    here, ring = Place(), YRing(x_ref.shape[0], 2, *sem[0:2])
+    here, ring = Place(), YRing(x_ref.shape[0], 1, *sem[0:2])
     total = ScatterSum(here, scatter_sources(ins, pieces), *refs[21:])
     tiny = SmallSum(here, bufs, arrived, asem, bsem)
     n, first = total.n, wide_s.shape[1] // STEP
@@ -494,14 +494,13 @@
     copy = load(rows_of(source_ref, ring.me * q, q), source_s, csem.at[3])
     for k in range(n):
         total.exchange(k)
+    each(0, n // 2, total.first)
     ring.relay(opp, nbr, held, 0)
-    ring.start(x_ref, opp, nbr, 1)
-    each(0, n, total.first)
-    ring.relay(opp, nbr, held, 1)
+    each(n // 2, n, total.first)
     each(0, n - 2, total.first_relay)
     copy.wait()
     sums = 0.0
-    for wave in (0, 1):
+    for wave in (0,):
         for part in (0, 1):
             at, value = ring.collect(own_s, nbr, part, wave)
             value, more = norm_back(value, source_s[at, :], base_ref[at, :], gain_ref[...])
@@ -526,9 +525,8 @@
     bufs[0, 10:11, 0:PAIR] = jnp.sum(jnp.where(diagonal, bias_ref[...], 0.0), axis=0, keepdims=True)
     tiny.send(0)
     each(n - 2, n, total.first_relay)
+    each(0, n, total.second)
     ring.forward(0, out_ref)
-    each(0, n, total.second)
-    ring.forward(1, out_ref)
     tiny.take(0)
     tiny.send(1)
     each(0, n, total.second_relay)
@@ -553,7 +551,6 @@
     rows = lax.broadcasted_iota(jnp.int32, sums_ref.shape, 0)
     sums_ref[...] = jnp.where(rows < 3, bufs[4], bufs[3])
     ring.arrive(0)
-    ring.arrive(1)
     kept.wait()
     for copy in swaps:
         copy.wait_send()

time: 349 us -> 340 us (0.974)
  Pallas kernels: 345 us -> 336 us
    pallas_call x1, Pallas kernels: 107 us -> 97.6 us  [reduce_input(): pl.pallas_call(functools.partial(input_kernel, pieces, len(grads)), out_s...]
where the time goes in v8:
time: 340 us
  Pallas kernels  336 us (99%)
    pallas_call x1, Pallas kernels, reduce_input(): pl.pallas_call(functools.partial(input_kernel, pieces, len(grads)), out_s...  97.6 us
    pallas_call x1, Pallas kernels, reduce_middle(): pl.pallas_call(functools.partial(middle_kernel, pieces, len(grads)), out_...  63.6 us
    pallas_call x1, Pallas kernels, forward_attention(): local_call(forward_kernel, heads // PAIR, [whole((seq, width)), whole((1,...  61.4 us
    pallas_call x1, Pallas kernels, backward_attention(): local_call(backward_kernel, heads // PAIR, [lanes, HBM] + [lanes] * 6 + [...  44.5 us
    pallas_call x1, Pallas kernels, mlp_backward(): pl.pallas_call(mlp_backward_kernel, in_specs=[smem] + [HBM] * 10, out_spe...  41.9 us
    pallas_call x1, Pallas kernels, mlp_forward(): pl.pallas_call(mlp_forward_kernel, in_specs=[smem, HBM, HBM, HBM, VMEM] +...  19.9 us
    pallas_call x1, Pallas kernels, finish(): pl.pallas_call(finish_kernel, out_shape=[struct(*grad.shape), struct(*lay...  7 us

profile of v8, /device:TPU:0, one launch (start us, length us, event | category | flops | bytes accessed | tf_op | source)
XLA Modules:
  0.0 339.9 jit_solution(7336343374182335120)
XLA Ops:
  1.3 1.3 broadcast_in_dim.15.gain_ref
  2.6 0.0 copy-start
  2.6 61.4 %shard_map.271 = (bf16[768,1536]{1,0:T(8,128)(2,1)}, f32[768,384]{1,0:T(8,128)}, f32[768,384]{1,0:T(8,128)}, bf16[768,384]{1,0:T(8,128)(2,1)}, f32[768,384]{1,0:...) custom-call(s32[1]{0:T(128)S(6)} %copy.31.length_ref, ...), custom_call_target="tpu_custom_call" | custom-call | flops 6000000000 | bytes 20000000 | tf_op jit(solution)/shard_map/pallas_call | solution.py:906
  64.0 0.0 copy-done
  64.0 0.6 broadcast_in_dim.17.gain_ref
  64.6 19.9 %shard_map.272 = (f32[768,1536]{1,0:T(8,128)}, bf16[768,1536]{1,0:T(8,128)(2,1)}, bf16[768,1536]{1,0:T(8,128)(2,1)}, f32[768,1024]{1,0:T(8,128)}, f32[768,1024]{...) custom-call(s32[1]{0:T(128)S(6)} %copy.31.length_ref, ...), custom_call_target="tpu_custom_call" | custom-call | tf_op jit(solution)/shard_map/pallas_call | solution.py:1033
  84.5 41.9 %shard_map.273 = (f32[768,1536]{1,0:T(8,128)}, f32[1536,1024]{1,0:T(8,128)}, f32[1536,1024]{1,0:T(8,128)}, f32[1536,1024]{1,0:T(8,128)}, f32[192,1536]{1,0:T(8,128)}, /*index=5*/f32[1,1536]{1,0:T(1,128)}) custom-call(s32[1]{0:T(128)S(6)} %copy.31.length_ref, bf16[768,1536]{1,0:T(8,128)(2,1)} %get-tuple-element.70.grad_in.base_ref, ...), custom_call_target="tpu_custom_call" | custom-call | tf_op jit(solution)/shard_map/pallas_call | solution.py:1203
  126.4 63.6 %shard_map.274 = (f32[192,1536]{1,0:T(8,128)}, f32[768,384]{1,0:T(8,128)}, f32[48,2048]{1,0:T(8,128)}, f32[1,1536]{1,0:T(1,128)}) custom-call(f32[768,1536]{1,0:T(8,128)} %get-tuple-element.77.x_ref, f32[768,1536]{1,0:T(8,128)} %get-tuple-element.76.mid_ref.source_ref, bf16[768,1536]{1,0:T(8,128)(2,1)} %get-tuple-element.70.grad_in.base_ref, ...), custom_call_target="tpu_custom_call" | custom-call | tf_op jit(solution)/shard_map/pallas_call | solution.py:449
  189.9 44.5 %shard_map.275 = (f32[768,1536]{1,0:T(8,128)}, f32[1536,1536]{1,0:T(8,128)}, f32[1536,1536]{1,0:T(8,128)}, f32[8,1536]{1,0:T(8,128)}, f32[8,128]{1,0:T(8,128)}, /*index=5*/bf16[768,1536]{1,0:T(8,128)(2,1)}) custom-call(s32[1]{0:T(128)S(6)} %copy.31.length_ref, f32[768,384]{1,0:T(8,128)} %get-tuple-element.80.gg_ref, ...), custom_call_target="tpu_custom_call" | custom-call | flops 14000000000 | bytes 50000000 | tf_op jit(solution)/shard_map/pallas_call | solution.py:1393
  235.1 97.6 %shard_map.276 = (f32[768,1536]{1,0:T(8,128)}, f32[48,384]{1,0:T(8,128)}, f32[48,2560]{1,0:T(8,128)}, f32[16,1536]{1,0:T(8,128)}) custom-call(f32[768,1536]{1,0:T(8,128)} %get-tuple-element.91.x_ref, bf16[768,1536]{1,0:T(8,128)(2,1)} %bitcast.14, f32[192,1536]{1,0:T(8,128)} %get-tuple-element.89.own_ref.base_ref, bf16[1,1536]{1,0:T(2,128)(2,1)} %broadcast_in_dim.15.gain_ref, ...), custom_call_target="tpu_custom_call" | custom-call | tf_op jit(solution)/shard_map/pallas_call | solution.py:570
  332.7 7.0 %shard_map.277 = (f32[768,1536]{1,0:T(8,128)}, bf16[768,1536]{1,0:T(8,128)(2,1)}, f32[48,384]{1,0:T(8,128)}, f32[48,384]{1,0:T(8,128)}, f32[48,384]{1,0:T(8,128)...) custom-call(f32[768,1536]{1,0:T(8,128)} %get-tuple-element.100.grad_, ...), custom_call_target="tpu_custom_call" | custom-call | tf_op jit(solution)/shard_map/pallas_call | solution.py:1480
Async XLA Ops:
  2.6 61.4 %copy-start = (bf16[1536]{0:T(1024)(128)(2,1)S(1)}, bf16[1536]{0:T(1024)(128)(2,1)}, u32[]{:S(2)}) copy-start(bf16[1536]{0:T(1024)(128)(2,1)} %param.28) | copy-start | bytes 9220

commit v9 on v8

--- a/solution.py
+++ b/solution.py
@@ -684,8 +684,11 @@
 
 def forward_kernel(
     length_ref, x_ref, gain_ref, wq_ref, wk_ref, wv_ref, wo_ref, wf_ref, bf_ref, w_ref,
+    gain2_ref, cot_in, wg_in, wu_in, wd_in,
     low_out, qn_ref, kn_ref, v_ref, sig_ref, att_ref, stat_ref, decay_ref, gated_out, full_out,
-    top_s, row_s, q_s, k_s, w_s, pre_s, gs, ws, wf_s, bf_s, low_ref, gated_ref, full_ref, osem, *sem,
+    mid_out, normed_out, grad_out, gate_out, up_out, hid_out, mlp_out, sums_ref,
+    top_s, row_s, q_s, k_s, w_s, pre_s, gs, ws, wf_s, bf_s, low_ref, gated_ref, full_ref,
+    wg_s, wu_s, wd_s, cot_s, mid_s, normed_s, grad_s, gate_s, up_s, hid_s, mlp_s, osem, *sem,
 ):
     step = pl.program_id(0)
     seq = x_ref.shape[0]
@@ -693,7 +696,7 @@
     here = Place()
     me, right, left, far = (lax.rem(here.my + by, Y) for by in (0, 1, 3, 2))
     sibling, right1, left1, right2, left2 = here.peers()
-    c, p1, p2, half = here.c, here.p1, here.p2, seq // 2
+    c, p1, p2, half, quarter = here.c, here.p1, here.p2, seq // 2, seq // Y
     mine = ws.at[c, p2, p1, me]
     cross_order = (p2, here.l2, here.r2, here.o2)
 
@@ -713,16 +716,38 @@
         piece = ws.at[c, cross_order[j]]
         return link(piece, piece, *sem[8:10], j, sibling)
 
-    def gate(pair, j):
+    def gate(pair, chunk, j):
         owner, part, to = (
             (me, 0, right), (me, 1, right), (me, 0, left), (me, 1, left), (left, 0, right), (right, 1, left)
         )[j]
-        piece = gs.at[pair, owner, part * half : part * half + half]
-        return link(piece, piece, *sem[0:2], pair * 6 + j, (here.dp, to))
+        start = pl.multiple_of(chunk * half + part * quarter, quarter)
+        piece = gs.at[pair, owner, pl.ds(start, quarter)]
+        return link(piece, piece, *sem[0:2], (pair * 2 + chunk) * 6 + j, (here.dp, to))
+
+    def offer(pair, chunk):
+        for j in range(4):
+            gate(pair, chunk, j).start()
 
     def flush(j):
-        src, dst = ((low_ref, low_out), (full_ref, full_out), (gated_ref, gated_out))[j]
+        src, dst = (
+            (low_ref, low_out),
+            (full_ref, full_out),
+            (rows_of(gated_ref, me * quarter, quarter), gated_out),
+            (wg_in, wg_s),
+            (wu_in, wu_s),
+            (wd_in, wd_s),
+        )[j]
         return pltpu.make_async_copy(src, dst, osem.at[j])
+
+    def leave(j, chunk):
+        src, dst = (
+            (mid_s, mid_out), (normed_s, normed_out), (grad_s, grad_out), (gate_s, gate_out),
+            (up_s, up_out), (hid_s, hid_out), (mlp_s, mlp_out),
+        )[j]
+        return pltpu.make_async_copy(src, dst.at[rows_at(chunk, half)], osem.at[6 + j])
+
+    def come(chunk):
+        return pltpu.make_async_copy(cot_in.at[rows_at(chunk, half)], cot_s, osem.at[13])
 
     def pass_on(make):
         make(0).wait_recv()
@@ -807,6 +832,9 @@
         for j in range(4):
             torus(1, j).start()
         cross(0).start()
+        for j in (3, 4, 5):
+            flush(j).start()
+        come(0).start()
 
     @pl.when(step == 2)
     def _():
@@ -837,17 +865,17 @@
         out = jnp.where(first, both[0], both[1])
         att_ref[at, :] = out
         gs[step, me, at, :] = (out * sig_ref[at, :]).astype(jnp.bfloat16).astype(F32)
-        if n % half == 0:
-            gate(step, n // half - 1).start()
-            gate(step, n // half + 1).start()
+        if n == half:
+            offer(step, 0)
 
     @pl.when(step == 0)
     def _():
+        offer(0, 1)
         pass_on(lambda j: torus(0, j))
 
     @pl.when(step > 0)
     def _():
-        pass_on(lambda j: gate(step - 1, j))
+        pass_on(lambda j: gate(step - 1, 0, j))
 
     @pl.when(step == pl.num_programs(0) - 1)
     def _():
@@ -858,7 +886,10 @@
         torus(1, 4).wait_recv()
         torus(1, 5).wait_recv()
         cross(3).start()
-        pass_on(lambda j: gate(step, j))
+        pass_on(lambda j: gate(step, 0, j))
+        pairs = gs.shape[0]
+        for pair in range(1, pairs):
+            offer(pair, 1)
         for j in range(4):
             cross(j).wait_recv()
         tall, wide, shard = ws.shape[4], ws.shape[5], w_ref.shape[0]
@@ -877,13 +908,87 @@
 
         lax.fori_loop(0, 8 * Y, turn, 0)
         flush(1).start()
-        pairs = gs.shape[0]
-        for pair in range(pairs):
-            arrived(lambda j: gate(pair, j))
-            for y in range(Y):
-                lane = (y * pairs + pair) * PAIR
-                gated_ref[:, lane : lane + PAIR] = gs[pair, y].astype(jnp.bfloat16)
-        flush(2).start()
+        for j in (3, 4, 5):
+            flush(j).wait()
+        outer, inner = full_ref.shape[1] // 2, wg_s.shape[1] // 2
+        columns = lambda k, size: pl.ds(pl.multiple_of(k * size, size), size)
+        sums_ref[...] = jnp.zeros_like(sums_ref)
+
+        def feed_forward(chunk):
+            rows = rows_at(chunk, half)
+            for pair in range(pairs):
+                arrived(lambda j: gate(pair, chunk, j))
+                for y in range(Y):
+                    lane = (y * pairs + pair) * PAIR
+                    gated_ref[rows, lane : lane + PAIR] = gs[pair, y, rows, :].astype(jnp.bfloat16)
+
+            @pl.when(chunk == 1)
+            def _():
+                flush(2).start()
+                for j in range(7):
+                    leave(j, 0).wait()
+                come(1).start()
+
+            kept = lax.broadcasted_iota(jnp.int32, (half, 1), 0) + chunk * half < length
+
+            def project(k):
+                at = columns(k, outer)
+                branch = mm(gated_ref[rows, :], full_ref[:, at])
+                x = x_ref[rows, at].astype(F32)
+                mid_s[:, at] = x + branch
+                for row, value in ((0, x), (1, branch)):
+                    value = jnp.where(kept, value * value, 0.0)
+                    sums_ref[row : row + 1, at] = sums_ref[row : row + 1, at] + jnp.sum(
+                        value, axis=0, keepdims=True
+                    )
+
+            each(0, 2, project)
+            leave(0, chunk).start()
+
+            def norm(i, carry):
+                at = rows_at(i, 128)
+                mid = mid_s[at, :]
+                r = lax.rsqrt(jnp.mean(mid * mid, axis=1, keepdims=True) + EPSILON)
+                normed_s[at, :] = (mid * r * gain2_ref[...].astype(F32)).astype(jnp.bfloat16)
+                return carry
+
+            lax.fori_loop(0, half // 128, norm, 0)
+            leave(1, chunk).start()
+
+            @pl.when(chunk == 0)
+            def _():
+                pass_on(lambda j: gate(0, 1, j))
+
+            def hidden(k):
+                at = columns(k, inner)
+                gate_s[:, at] = mm(normed_s[...], wg_s[:, at])
+                up_s[:, at] = mm(normed_s[...], wu_s[:, at])
+                pre = gate_s[:, at]
+                hid_s[:, at] = (pre * jax.nn.sigmoid(pre) * up_s[:, at]).astype(jnp.bfloat16)
+
+            each(0, 2, hidden)
+            for j in (3, 4, 5):
+                leave(j, chunk).start()
+
+            @pl.when(chunk == 0)
+            def _():
+                for pair in range(1, pairs):
+                    pass_on(lambda j: gate(pair, 1, j))
+
+            come(chunk).wait()
+            grad_s[...] = jnp.where(kept, cot_s[...].astype(F32), 0.0).astype(jnp.bfloat16)
+            leave(2, chunk).start()
+
+            def project_out(k):
+                at = columns(k, outer)
+                mlp_s[:, at] = mm(hid_s[...], wd_s[:, at])
+
+            each(0, 2, project_out)
+            leave(6, chunk).start()
+
+        each(0, 2, feed_forward)
+        for j in range(7):
+            leave(j, 1).wait()
         for j in range(3):
             flush(j).wait()
             plane(j).wait_send()
@@ -893,25 +998,33 @@
         for j in range(4):
             cross(j).wait_send()
         for pair in range(pairs):
-            for j in range(6):
-                gate(pair, j).wait_send()
-
-
-def forward_attention(tokens, length, gain, wq, wk, wv, wo, wf, bf, w_out, call_id):
+            for chunk in (0, 1):
+                for j in range(6):
+                    gate(pair, chunk, j).wait_send()
+
+
+def forward(
+    tokens, cotangent, length, gain, wq, wk, wv, wo, wf, bf, w_out, gain2, wg, wu, wd, call_id
+):
     seq, width = tokens.shape
-    heads = wq.shape[1]
+    heads, hidden, half = wq.shape[1], wg.shape[1], seq // 2
     weights = pl.BlockSpec((width, PAIR), lambda i, _: (0, i))
     lanes = pl.BlockSpec((seq, PAIR), lambda i, _: (0, i))
     low = jnp.bfloat16
+    half_rows = lambda w, t=F32: pltpu.VMEM((half, w), t)
     return local_call(
         forward_kernel,
         heads // PAIR,
-        [whole((seq, width)), whole((1, width))] + [weights] * 4 + [whole(wf.shape), whole(bf.shape), whole(w_out.shape)],
-        [HBM] + [lanes] * 6 + [whole((2, 8, seq)), HBM, HBM],
+        [whole((seq, width)), whole((1, width))] + [weights] * 4
+        + [whole(wf.shape), whole(bf.shape), whole(w_out.shape), whole((1, width))] + [HBM] * 4,
+        [HBM] + [lanes] * 6 + [whole((2, 8, seq))] + [HBM] * 9 + [whole((2, width))],
         [
             struct(seq, width, t=low), struct(seq, heads), struct(seq, heads), struct(seq, heads, t=low),
             struct(seq, heads), struct(seq, heads), struct(seq, heads),
-            struct(2, 8, seq), struct(seq, heads * Y, t=low), struct(heads * Y, width, t=low),
+            struct(2, 8, seq), struct(seq // Y, heads * Y, t=low), struct(heads * Y, width, t=low),
+            struct(seq, width), struct(seq, width, t=low), struct(seq, width, t=low),
+            struct(seq, hidden), struct(seq, hidden), struct(seq, hidden, t=low), struct(seq, width),
+            struct(2, width),
         ],
         [
             pltpu.VMEM((seq, PAIR), F32),
@@ -927,127 +1040,25 @@
             pltpu.VMEM((seq, width), low),
             pltpu.VMEM((seq, width), low),
             pltpu.VMEM((heads * Y, width), low),
-            pltpu.SemaphoreType.DMA((3,)),
-        ]
-        + sems(6 * (heads // PAIR), 3, 6, 6, 4),
-        56, 6, 20, call_id,
-    )(length, tokens, gain, wq, wk, wv, wo, wf, bf, w_out)
-
-
-def copier(sem):
-    count = iter(range(sem.shape[0]))
-
-    def copy(src, dst):
-        return load(src, dst, sem.at[next(count)])
-
-    return copy
-
-
-def mlp_forward_kernel(
-    length_ref, x_in, cot_in, gated_in, gain_ref, wo_in, wg_in, wu_in, wd_in,
-    mid_out, low_out, grad_out, gate_out, up_out, hid_out, out_out, sums_ref,
-    x_ref, cot_ref, gated_ref, wo_ref, wg_ref, wu_ref, wd_ref,
-    mid_ref, low_ref, grad_ref, gate_ref, up_ref, hid_ref, out_ref, sem,
-):
-    seq, width = x_ref.shape
-    length = length_ref[0]
-    tile, units = wo_ref.shape[2], hid_ref.shape[1] // 2
-    copy = copier(sem)
-    columns = lambda j, size: pl.ds(pl.multiple_of(j * size, size), size)
-    outer = lambda j: pltpu.make_async_copy(
-        wo_in.at[:, columns(j, tile)], wo_ref.at[j], sem.at[sem.shape[0] - 2 + j]
-    )
-    need = copy(gated_in, gated_ref)
-    outer(0).start()
-    need_x = copy(x_in, x_ref)
-    need.wait()
-    outer(1).start()
-    need_cot = copy(cot_in, cot_ref)
-    weights = [copy(wg_in, wg_ref), copy(wu_in, wu_ref), copy(wd_in, wd_ref)]
-    kept = lax.broadcasted_iota(jnp.int32, (seq, 1), 0) < length
-    flushes = []
-
-    def project(j):
-        at = columns(j, tile)
-        outer(j).wait()
-        branch = mm(gated_ref[...], wo_ref[j])
-        x = x_ref[:, at].astype(F32)
-        mid_ref[:, at] = x + branch
-        sums_ref[0:1, at] = jnp.sum(jnp.where(kept, x * x, 0.0), axis=0, keepdims=True)
-        sums_ref[1:2, at] = jnp.sum(jnp.where(kept, branch * branch, 0.0), axis=0, keepdims=True)
-
-    need_x.wait()
-    each(0, 2, project)
-    flushes.append(copy(mid_ref, mid_out))
-
-    def norm(i, carry):
-        at = rows_at(i, 128)
-        mid = mid_ref[at, :]
-        r = lax.rsqrt(jnp.mean(mid * mid, axis=1, keepdims=True) + EPSILON)
-        low_ref[at, :] = (mid * r * gain_ref[...].astype(F32)).astype(jnp.bfloat16)
-        return carry
-
-    lax.fori_loop(0, seq // 128, norm, 0)
-    flushes.append(copy(low_ref, low_out))
-    weights[0].wait()
-    weights[1].wait()
-
-    def hidden(j):
-        at = columns(j, units)
-        gate_ref[:, at] = mm(low_ref[...], wg_ref[:, at])
-        up_ref[:, at] = mm(low_ref[...], wu_ref[:, at])
-        gate = gate_ref[:, at]
-        hid_ref[:, at] = (gate * jax.nn.sigmoid(gate) * up_ref[:, at]).astype(jnp.bfloat16)
-
-    each(0, 2, hidden)
-    for src, dst in ((gate_ref, gate_out), (up_ref, up_out), (hid_ref, hid_out)):
-        flushes.append(copy(src, dst))
-    need_cot.wait()
-    grad_ref[...] = jnp.where(kept, cot_ref[...].astype(F32), 0.0).astype(jnp.bfloat16)
-    flushes.append(copy(grad_ref, grad_out))
-    weights[2].wait()
-    result = lambda j: pltpu.make_async_copy(
-        out_ref.at[:, columns(j, tile)], out_out.at[:, columns(j, tile)], sem.at[sem.shape[0] - 4 + j]
-    )
-
-    def project_out(j):
-        at = columns(j, tile)
-        out_ref[:, at] = mm(hid_ref[...], wd_ref[:, at])
-        result(j).start()
-
-    each(0, 2, project_out)
-    flushes += [result(0), result(1)]
-    for c in flushes:
-        c.wait()
-
-
-def mlp_forward(tokens, cotangent, length, gated, gain, wo, wg, wu, wd):
-    seq, width = tokens.shape
-    hidden = wg.shape[1]
-    low = jnp.bfloat16
-    smem = pl.BlockSpec(memory_space=pltpu.SMEM)
-    outs = [
-        struct(seq, width), struct(seq, width, t=low), struct(seq, width, t=low),
-        struct(seq, hidden), struct(seq, hidden), struct(seq, hidden, t=low), struct(seq, width),
-    ]
-    return pl.pallas_call(
-        mlp_forward_kernel,
-        in_specs=[smem, HBM, HBM, HBM, VMEM] + [HBM] * 4,
-        out_specs=[HBM] * 7 + [VMEM],
-        out_shape=outs + [struct(2, width)],
-        scratch_shapes=[
-            pltpu.VMEM((seq, width), low),
-            pltpu.VMEM((seq, width), low),
-            pltpu.VMEM((seq, width), low),
-            pltpu.VMEM((2, width, width // 2), low),
             pltpu.VMEM((width, hidden), low),
             pltpu.VMEM((width, hidden), low),
             pltpu.VMEM((hidden, width), low),
+            half_rows(width, low), half_rows(width), half_rows(width, low), half_rows(width, low),
+            half_rows(hidden), half_rows(hidden), half_rows(hidden, low), half_rows(width),
+            pltpu.SemaphoreType.DMA((14,)),
         ]
-        + [pltpu.VMEM(out.shape, out.dtype) for out in outs]
-        + [pltpu.SemaphoreType.DMA((18,))],
-        compiler_params=pltpu.CompilerParams(vmem_limit_bytes=58 << 20),
-    )(length, tokens, cotangent, gated, gain, wo, wg, wu, wd)
+        + sems(12 * (heads // PAIR), 3, 6, 6, 4),
+        63, 17, 60, call_id,
+    )(length, tokens, gain, wq, wk, wv, wo, wf, bf, w_out, gain2, cotangent, wg, wu, wd)
+
+
+def copier(sem):
+    count = iter(range(sem.shape[0]))
+
+    def copy(src, dst):
+        return load(src, dst, sem.at[next(count)])
+
+    return copy
 
 
 def reduce_links(rows, x, opp, nbr, held, sem):
@@ -1395,7 +1406,7 @@
         heads // PAIR,
         [lanes, HBM] + [lanes] * 6 + [whole((2, 8, seq))] + [weights] * 4
         + [whole(wf.shape), whole(own.shape)]
-        + [pl.BlockSpec((own.shape[0], 4 * PAIR), lambda i, _: (lax.axis_index("mp"), i)), HBM],
+        + [pl.BlockSpec((own.shape[0], 4 * PAIR), lambda i, _: (0, i)), HBM],
         [HBM, HBM, HBM, whole((8, width)), whole((8, PAIR)), full],
         [
             struct(seq, width), struct(width, 4 * heads), struct(width, width), struct(8, width),
@@ -1500,11 +1511,11 @@
     heads = w_forget.shape[1]
     gain_in, gain_mid = gain_attn[None], gain_mlp[None]
     weights = (w_query, w_key, w_value, w_outgate, w_forget.T)
-    low, qn, kn, value, sig, attended, stat, decay, gated, w_full = forward_attention(
-        x, lengths, gain_in, *weights, b_forget[None], w_out, 0
-    )
-    middle, mid_low, grad_rows, gate, up, hidden, mlp_local, squares = mlp_forward(
-        x, cotangent, lengths, gated, gain_mid, w_full, w_gate, w_up, w_down
+    (
+        low, qn, kn, value, sig, attended, stat, decay, gated, w_full,
+        middle, mid_low, grad_rows, gate, up, hidden, mlp_local, squares,
+    ) = forward(
+        x, cotangent, lengths, gain_in, *weights, b_forget[None], w_out, gain_mid, w_gate, w_up, w_down, 0
     )
     mid_local, g_down, g_gate, g_up, layer_own, mlp_square = mlp_backward(
         lengths, grad_rows, mid_low, gate, up, hidden, w_gate, w_up, w_down, mlp_local, middle, 1

time: 340 us -> 337 us (level)
  Pallas kernels: 336 us -> 332 us
    pallas_call x2 -> x1, Pallas kernels: 81.3 us -> 76.4 us  [forward(): local_call(forward_kernel, heads // PAIR, [whole((seq, width)), whole((1,...]
where the time goes in v9:
time: 337 us; the launch traced here: 336 us
  Pallas kernels  332 us (99%)
    pallas_call x1, Pallas kernels, reduce_input(): pl.pallas_call(functools.partial(input_kernel, pieces, len(grads)), out_s...  94.5 us
    pallas_call x1, Pallas kernels, forward(): local_call(forward_kernel, heads // PAIR, [whole((seq, width)), whole((1,...  76.4 us
    pallas_call x1, Pallas kernels, reduce_middle(): pl.pallas_call(functools.partial(middle_kernel, pieces, len(grads)), out_...  65.2 us
    pallas_call x1, Pallas kernels, backward_attention(): local_call(backward_kernel, heads // PAIR, [lanes, HBM] + [lanes] * 6 + [...  46.6 us
    pallas_call x1, Pallas kernels, mlp_backward(): pl.pallas_call(mlp_backward_kernel, in_specs=[smem] + [HBM] * 10, out_spe...  42.2 us
    pallas_call x1, Pallas kernels, finish(): pl.pallas_call(finish_kernel, out_shape=[struct(*grad.shape), struct(*lay...  7 us

profile of v9, /device:TPU:0, one launch (start us, length us, event | category | flops | bytes accessed | tf_op | source)
XLA Modules:
  0.0 336.5 jit_solution(17766456269153598198)
XLA Ops:
  1.3 1.3 broadcast_in_dim.15.gain_ref
  2.6 1.3 broadcast_in_dim.17.gain2_ref.gain_ref
  3.9 76.4 %shard_map.271 = (bf16[768,1536]{1,0:T(8,128)(2,1)}, f32[768,384]{1,0:T(8,128)}, f32[768,384]{1,0:T(8,128)}, bf16[768,384]{1,0:T(8,128)(2,1)}, f32[768,384]{1,0:...) custom-call(s32[1]{0:T(128)S(6)} %copy.31.length_ref, ...), custom_call_target="tpu_custom_call" | custom-call | flops 16999999488 | bytes 60000000 | tf_op jit(solution)/shard_map/pallas_call | solution.py:1015
  80.2 42.2 %shard_map.272 = (f32[768,1536]{1,0:T(8,128)}, f32[1536,1024]{1,0:T(8,128)}, f32[1536,1024]{1,0:T(8,128)}, f32[1536,1024]{1,0:T(8,128)}, f32[192,1536]{1,0:T(8,128)}, /*index=5*/f32[1,1536]{1,0:T(1,128)}) custom-call(s32[1]{0:T(128)S(6)} %copy.31.length_ref, bf16[768,1536]{1,0:T(8,128)(2,1)} %get-tuple-element.68.grad_in.base_ref, ...), custom_call_target="tpu_custom_call" | custom-call | tf_op jit(solution)/shard_map/pallas_call | solution.py:1214
  122.4 65.2 %shard_map.273 = (f32[192,1536]{1,0:T(8,128)}, f32[768,384]{1,0:T(8,128)}, f32[48,2048]{1,0:T(8,128)}, f32[1,1536]{1,0:T(1,128)}) custom-call(f32[768,1536]{1,0:T(8,128)} %get-tuple-element.75.x_ref, f32[768,1536]{1,0:T(8,128)} %get-tuple-element.74.mid_ref.source_ref, bf16[768,1536]{1,0:T(8,128)(2,1)} %get-tuple-element.68.grad_in.base_ref, ...), custom_call_target="tpu_custom_call" | custom-call | tf_op jit(solution)/shard_map/pallas_call | solution.py:449
  187.6 46.6 %shard_map.274 = (f32[768,1536]{1,0:T(8,128)}, f32[1536,1536]{1,0:T(8,128)}, f32[1536,1536]{1,0:T(8,128)}, f32[8,1536]{1,0:T(8,128)}, f32[8,128]{1,0:T(8,128)}, /*index=5*/bf16[768,1536]{1,0:T(8,128)(2,1)}) custom-call(s32[1]{0:T(128)S(6)} %copy.31.length_ref, f32[768,384]{1,0:T(8,128)} %get-tuple-element.79.gg_ref, ...), custom_call_target="tpu_custom_call" | custom-call | flops 14000000000 | bytes 50000000 | tf_op jit(solution)/shard_map/pallas_call | solution.py:1404
  234.8 94.5 %shard_map.275 = (f32[768,1536]{1,0:T(8,128)}, f32[48,384]{1,0:T(8,128)}, f32[48,2560]{1,0:T(8,128)}, f32[16,1536]{1,0:T(8,128)}) custom-call(f32[768,1536]{1,0:T(8,128)} %get-tuple-element.91.x_ref, bf16[768,1536]{1,0:T(8,128)(2,1)} %bitcast.13, f32[192,1536]{1,0:T(8,128)} %get-tuple-element.88.own_ref.base_ref, bf16[1,1536]{1,0:T(2,128)(2,1)} %broadcast_in_dim.15.gain_ref, ...), custom_call_target="tpu_custom_call" | custom-call | tf_op jit(solution)/shard_map/pallas_call | solution.py:570
  329.3 7.0 %shard_map.276 = (f32[768,1536]{1,0:T(8,128)}, bf16[768,1536]{1,0:T(8,128)(2,1)}, f32[48,384]{1,0:T(8,128)}, f32[48,384]{1,0:T(8,128)}, f32[48,384]{1,0:T(8,128)...) custom-call(f32[768,1536]{1,0:T(8,128)} %get-tuple-element.100.grad_, ...), custom_call_target="tpu_custom_call" | custom-call | tf_op jit(solution)/shard_map/pallas_call | solution.py:1491

commit v10 on v9

--- a/solution.py
+++ b/solution.py
@@ -716,17 +716,16 @@
         piece = ws.at[c, cross_order[j]]
         return link(piece, piece, *sem[8:10], j, sibling)
 
-    def gate(pair, chunk, j):
+    def gate(pair, j):
         owner, part, to = (
             (me, 0, right), (me, 1, right), (me, 0, left), (me, 1, left), (left, 0, right), (right, 1, left)
         )[j]
-        start = pl.multiple_of(chunk * half + part * quarter, quarter)
-        piece = gs.at[pair, owner, pl.ds(start, quarter)]
-        return link(piece, piece, *sem[0:2], (pair * 2 + chunk) * 6 + j, (here.dp, to))
-
-    def offer(pair, chunk):
-        for j in range(4):
-            gate(pair, chunk, j).start()
+        piece = gs.at[pair, owner, part * half : part * half + half]
+        return link(piece, piece, *sem[0:2], pair * 6 + j, (here.dp, to))
+
+    def hand_on(pair, come, go):
+        gate(pair, come).wait_recv()
+        gate(pair, go).start()
 
     def flush(j):
         src, dst = (
@@ -849,33 +848,41 @@
     for i in range(seq // 128):
         at, n = slice(i * 128, i * 128 + 128), i * 128 + 128
         q = q_s[at, :]
-        both = []
+        two = jnp.concatenate([jnp.where(first, q, zero), jnp.where(first, zero, q)], axis=0)
+        raw = mm_t(two, k_s[0:n, :]) * (HEAD ** (-0.5))
+        probs = []
         for head in (0, 1):
-            own = jnp.where(first, q, zero) if head == 0 else jnp.where(first, zero, q)
-            s = mm_t(own, k_s[0:n, :])
             column = jnp.sum(
                 jnp.where(lane_is((128, PAIR), 2 * step + head), top_s[at, :], 0.0), axis=1, keepdims=True
             )
-            s = s * (HEAD ** (-0.5)) + (column - lines[head][:, 0:n])
+            s = raw[head * 128 : head * 128 + 128] + (column - lines[head][:, 0:n])
             diagonal = jnp.where(upper, NEG, s[:, n - 128 :])
             s = diagonal if i == 0 else jnp.concatenate([s[:, : n - 128], diagonal], axis=1)
             p = jnp.exp(s)
-            p = p * (1.0 / jnp.sum(p, axis=1, keepdims=True))
-            both.append(mm(p.astype(jnp.bfloat16), v_ref[0:n, :]))
-        out = jnp.where(first, both[0], both[1])
+            probs.append((p * (1.0 / jnp.sum(p, axis=1, keepdims=True))).astype(jnp.bfloat16))
+        both = mm(jnp.concatenate(probs, axis=0), v_ref[0:n, :])
+        out = jnp.where(first, both[0:128], both[128:])
         att_ref[at, :] = out
         gs[step, me, at, :] = (out * sig_ref[at, :]).astype(jnp.bfloat16).astype(F32)
         if n == half:
-            offer(step, 0)
+            gate(step, 0).start()
+            gate(step, 2).start()
+
+            @pl.when(step > 0)
+            def _():
+                hand_on(step - 1, 0, 4)
+
+
+    gate(step, 3).start()
 
     @pl.when(step == 0)
     def _():
-        offer(0, 1)
+        gate(0, 1).start()
         pass_on(lambda j: torus(0, j))
 
     @pl.when(step > 0)
     def _():
-        pass_on(lambda j: gate(step - 1, 0, j))
+        hand_on(step - 1, 3, 5)
 
     @pl.when(step == pl.num_programs(0) - 1)
     def _():
@@ -886,10 +893,11 @@
         torus(1, 4).wait_recv()
         torus(1, 5).wait_recv()
         cross(3).start()
-        pass_on(lambda j: gate(step, 0, j))
+        hand_on(step, 0, 4)
         pairs = gs.shape[0]
         for pair in range(1, pairs):
-            offer(pair, 1)
+            gate(pair, 1).start()
+        hand_on(step, 3, 5)
         for j in range(4):
             cross(j).wait_recv()
         tall, wide, shard = ws.shape[4], ws.shape[5], w_ref.shape[0]
@@ -916,8 +924,15 @@
 
         def feed_forward(chunk):
             rows = rows_at(chunk, half)
+            for part, names in enumerate(((2, 4), (1, 5))):
+
+                @pl.when(chunk == part)
+                def _():
+                    for pair in range(pairs):
+                        for j in names:
+                            gate(pair, j).wait_recv()
+
             for pair in range(pairs):
-                arrived(lambda j: gate(pair, chunk, j))
                 for y in range(Y):
                     lane = (y * pairs + pair) * PAIR
                     gated_ref[rows, lane : lane + PAIR] = gs[pair, y, rows, :].astype(jnp.bfloat16)
@@ -955,10 +970,6 @@
             lax.fori_loop(0, half // 128, norm, 0)
             leave(1, chunk).start()
 
-            @pl.when(chunk == 0)
-            def _():
-                pass_on(lambda j: gate(0, 1, j))
-
             def hidden(k):
                 at = columns(k, inner)
                 gate_s[:, at] = mm(normed_s[...], wg_s[:, at])
@@ -969,11 +980,6 @@
             each(0, 2, hidden)
             for j in (3, 4, 5):
                 leave(j, chunk).start()
-
-            @pl.when(chunk == 0)
-            def _():
-                for pair in range(1, pairs):
-                    pass_on(lambda j: gate(pair, 1, j))
 
             come(chunk).wait()
             grad_s[...] = jnp.where(kept, cot_s[...].astype(F32), 0.0).astype(jnp.bfloat16)
@@ -998,9 +1004,8 @@
         for j in range(4):
             cross(j).wait_send()
         for pair in range(pairs):
-            for chunk in (0, 1):
-                for j in range(6):
-                    gate(pair, chunk, j).wait_send()
+            for j in range(6):
+                gate(pair, j).wait_send()
 
 
 def forward(
@@ -1047,7 +1052,7 @@
             half_rows(hidden), half_rows(hidden), half_rows(hidden, low), half_rows(width),
             pltpu.SemaphoreType.DMA((14,)),
         ]
-        + sems(12 * (heads // PAIR), 3, 6, 6, 4),
+        + sems(6 * (heads // PAIR), 3, 6, 6, 4),
         63, 17, 60, call_id,
     )(length, tokens, gain, wq, wk, wv, wo, wf, bf, w_out, gain2, cotangent, wg, wu, wd)
 
@@ -1234,7 +1239,7 @@
     length_ref, gg_ref, low_in, qn_ref, kn_ref, v_ref, sig_ref, att_ref, stat_ref,
     decay_ref, wq_ref, wk_ref, wv_ref, wo_ref, wf_ref, own_ref, gated_ref, layer_ref,
     back_out, four_out, gout_out, gf_ref, bias_ref, out_ref,
-    k_s, do_s, line_s, top_s, dq_s, dk_s, dv_s, all_s, fall_s, w_s, wf_s, lay_s, back_ref, wide_s, low_ref, osem,
+    k_s, do_s, line_s, top_s, both_s, dq_s, dk_s, dv_s, all_s, fall_s, w_s, wf_s, lay_s, back_ref, wide_s, low_ref, osem,
     *sem,
 ):
     step = pl.program_id(0)
@@ -1303,34 +1308,42 @@
             jnp.where(lane_is((seq, PAIR), 2 * step + head), top_s[...], 0.0), axis=1, keepdims=True
         )
         columns.append(column)
+    both_s[...] = jnp.concatenate([jnp.broadcast_to(column, (seq, PAIR)) for column in columns], axis=1)
+    ones = jnp.concatenate(
+        [jnp.where(lane_is((128, PAIR), 2 * step + head), 1.0, 0.0) for head in (0, 1)], axis=0
+    ).astype(low16)
+    lanes = lax.broadcasted_iota(jnp.int32, (seq, PAIR), 1)
+    marks = jnp.where(lanes // 2 == step, 1.0, 0.0).astype(low16)
     block = first_head((128, PAIR))
     zero = jnp.zeros((128, PAIR), low16)
-    lower = lax.broadcasted_iota(jnp.int32, (128, 128), 0) > lax.broadcasted_iota(
-        jnp.int32, (128, 128), 1
+    lower = lax.broadcasted_iota(jnp.int32, (128, 256), 0) > lax.rem(
+        lax.broadcasted_iota(jnp.int32, (128, 256), 1), 128
     )
     for i in range(seq // 128):
         at, n = slice(i * 128, i * 128 + 128), i * 128 + 128
         query = qn_ref[at, :].astype(low16)
         do = do_s[at, :]
-        pieces = []
-        for head in (0, 1):
-            pick = (lambda t: jnp.where(block, t, zero)) if head == 0 else (lambda t: jnp.where(block, zero, t))
-            own_q, own_do = pick(query), pick(do)
-            one = jnp.where(lane_is((128, PAIR), 2 * step + head), 1.0, 0.0).astype(low16)
-            s = mm_t(k_s[0:n, :], own_q)
-            s = s * (HEAD ** (-0.5)) + (lines[head][:, at] - columns[head][0:n])
-            diagonal = jnp.where(lower, NEG, s[n - 128 :, :])
-            s = diagonal if i == 0 else jnp.concatenate([s[: n - 128, :], diagonal], axis=0)
-            p = jnp.exp(s)
-            p = p * (1.0 / jnp.sum(p, axis=0, keepdims=True))
-            gp = mm_t(v_ref[0:n, :], own_do)
-            ds = (p * (gp - jnp.sum(p * gp, axis=0, keepdims=True))).astype(low16)
-            dv_s[0:n, :] = dv_s[0:n, :] + mm(p.astype(low16), own_do)
-            dk_s[0:n, :] = dk_s[0:n, :] + mm(ds, jnp.concatenate([own_q, one], axis=1))
-            mark = jnp.where(lane_is((n, PAIR), 2 * step + head), 1.0, 0.0).astype(low16)
-            pieces.append(t_mm(ds, jnp.concatenate([k_s[0:n, :], mark], axis=1)))
-        dq_s[at, :] = jnp.where(block, pieces[0][:, 0:PAIR], pieces[1][:, 0:PAIR])
-        fall_s[at, :] = fall_s[at, :] + pieces[0][:, PAIR:] + pieces[1][:, PAIR:]
+        two_q, two_do = (
+            jnp.concatenate([jnp.where(block, t, zero), jnp.where(block, zero, t)], axis=0)
+            for t in (query, do)
+        )
+        s = mm_t(k_s[0:n, :], two_q) * (HEAD ** (-0.5))
+        s = s + (jnp.concatenate([line[:, at] for line in lines], axis=1) - both_s[0:n, :])
+        diagonal = jnp.where(lower, NEG, s[n - 128 :, :])
+        s = diagonal if i == 0 else jnp.concatenate([s[: n - 128, :], diagonal], axis=0)
+        p = jnp.exp(s)
+        p = p * (1.0 / jnp.sum(p, axis=0, keepdims=True))
+        gp = mm_t(v_ref[0:n, :], two_do)
+        ds = (p * (gp - jnp.sum(p * gp, axis=0, keepdims=True))).astype(low16)
+        dv_s[0:n, :] = dv_s[0:n, :] + mm(p.astype(low16), two_do)
+        dk_s[0:n, :] = dk_s[0:n, :] + mm(ds, jnp.concatenate([two_q, ones], axis=1))
+        pieces = t_mm(ds, jnp.concatenate([k_s[0:n, :], marks[0:n]], axis=1))
+        one, two = pieces[0:128], pieces[128:]
+        dq_s[at, :] = jnp.where(block, one[:, 0:PAIR], two[:, 0:PAIR])
+        fall_s[at, :] = fall_s[at, :] + (
+            jnp.where(lane_is((128, PAIR), 2 * step), one[:, PAIR:], 0.0)
+            + jnp.where(lane_is((128, PAIR), 2 * step + 1), two[:, PAIR:], 0.0)
+        )
     fall_s[...] = fall_s[...] - dk_s[:, PAIR:]
     stat = stat_ref[...]
     for e, n_ref, col, to in ((dq_s, qn_ref, 0, 0), (dk_s, kn_ref, 2, 1)):
@@ -1417,6 +1430,7 @@
             pltpu.VMEM((seq, PAIR), low16),
             pltpu.VMEM((8, seq), F32),
             pltpu.VMEM((seq, PAIR), F32),
+            pltpu.VMEM((seq, 2 * PAIR), F32),
             pltpu.VMEM((seq, PAIR), F32),
             pltpu.VMEM((seq, 2 * PAIR), F32),
             pltpu.VMEM((seq, PAIR), F32),

time: 337 us -> 333 us (0.988)
  Pallas kernels: 332 us -> 328 us
where the time goes in v10:
time: 333 us
  Pallas kernels  328 us (98%)
    pallas_call x1, Pallas kernels, reduce_input(): pl.pallas_call(functools.partial(input_kernel, pieces, len(grads)), out_s...  97.1 us
    pallas_call x1, Pallas kernels, forward(): local_call(forward_kernel, heads // PAIR, [whole((seq, width)), whole((1,...  75.3 us
    pallas_call x1, Pallas kernels, reduce_middle(): pl.pallas_call(functools.partial(middle_kernel, pieces, len(grads)), out_...  64.3 us
    pallas_call x1, Pallas kernels, backward_attention(): local_call(backward_kernel, heads // PAIR, [lanes, HBM] + [lanes] * 6 + [...  44.5 us
    pallas_call x1, Pallas kernels, mlp_backward(): pl.pallas_call(mlp_backward_kernel, in_specs=[smem] + [HBM] * 10, out_spe...  40.1 us
    pallas_call x1, Pallas kernels, finish(): pl.pallas_call(finish_kernel, out_shape=[struct(*grad.shape), struct(*lay...  7 us

profile of v10, /device:TPU:0, one launch (start us, length us, event | category | flops | bytes accessed | tf_op | source)
XLA Modules:
  0.0 333.1 jit_solution(5354791751882397077)
XLA Ops:
  1.3 1.3 broadcast_in_dim.15.gain_ref
  2.6 1.3 broadcast_in_dim.17.gain2_ref.gain_ref
  3.9 75.3 %shard_map.271 = (bf16[768,1536]{1,0:T(8,128)(2,1)}, f32[768,384]{1,0:T(8,128)}, f32[768,384]{1,0:T(8,128)}, bf16[768,384]{1,0:T(8,128)(2,1)}, f32[768,384]{1,0:...) custom-call(s32[1]{0:T(128)S(6)} %copy.31.length_ref, ...), custom_call_target="tpu_custom_call" | custom-call | flops 16999999488 | bytes 60000000 | tf_op jit(solution)/shard_map/pallas_call | solution.py:1020
  79.2 40.1 %shard_map.272 = (f32[768,1536]{1,0:T(8,128)}, f32[1536,1024]{1,0:T(8,128)}, f32[1536,1024]{1,0:T(8,128)}, f32[1536,1024]{1,0:T(8,128)}, f32[192,1536]{1,0:T(8,128)}, /*index=5*/f32[1,1536]{1,0:T(1,128)}) custom-call(s32[1]{0:T(128)S(6)} %copy.31.length_ref, bf16[768,1536]{1,0:T(8,128)(2,1)} %get-tuple-element.68.grad_in.base_ref, ...), custom_call_target="tpu_custom_call" | custom-call | tf_op jit(solution)/shard_map/pallas_call | solution.py:1219
  119.3 64.3 %shard_map.273 = (f32[192,1536]{1,0:T(8,128)}, f32[768,384]{1,0:T(8,128)}, f32[48,2048]{1,0:T(8,128)}, f32[1,1536]{1,0:T(1,128)}) custom-call(f32[768,1536]{1,0:T(8,128)} %get-tuple-element.75.x_ref, f32[768,1536]{1,0:T(8,128)} %get-tuple-element.74.mid_ref.source_ref, bf16[768,1536]{1,0:T(8,128)(2,1)} %get-tuple-element.68.grad_in.base_ref, ...), custom_call_target="tpu_custom_call" | custom-call | tf_op jit(solution)/shard_map/pallas_call | solution.py:449
  183.6 44.5 %shard_map.274 = (f32[768,1536]{1,0:T(8,128)}, f32[1536,1536]{1,0:T(8,128)}, f32[1536,1536]{1,0:T(8,128)}, f32[8,1536]{1,0:T(8,128)}, f32[8,128]{1,0:T(8,128)}, /*index=5*/bf16[768,1536]{1,0:T(8,128)(2,1)}) custom-call(s32[1]{0:T(128)S(6)} %copy.31.length_ref, f32[768,384]{1,0:T(8,128)} %get-tuple-element.79.gg_ref, ...), custom_call_target="tpu_custom_call" | custom-call | flops 14000000000 | bytes 50000000 | tf_op jit(solution)/shard_map/pallas_call | solution.py:1417
  228.8 97.1 %shard_map.275 = (f32[768,1536]{1,0:T(8,128)}, f32[48,384]{1,0:T(8,128)}, f32[48,2560]{1,0:T(8,128)}, f32[16,1536]{1,0:T(8,128)}) custom-call(f32[768,1536]{1,0:T(8,128)} %get-tuple-element.91.x_ref, bf16[768,1536]{1,0:T(8,128)(2,1)} %bitcast.13, f32[192,1536]{1,0:T(8,128)} %get-tuple-element.88.own_ref.base_ref, bf16[1,1536]{1,0:T(2,128)(2,1)} %broadcast_in_dim.15.gain_ref, ...), custom_call_target="tpu_custom_call" | custom-call | tf_op jit(solution)/shard_map/pallas_call | solution.py:570
  325.9 7.0 %shard_map.276 = (f32[768,1536]{1,0:T(8,128)}, bf16[768,1536]{1,0:T(8,128)(2,1)}, f32[48,384]{1,0:T(8,128)}, f32[48,384]{1,0:T(8,128)}, f32[48,384]{1,0:T(8,128)...) custom-call(f32[768,1536]{1,0:T(8,128)} %get-tuple-element.100.grad_, ...), custom_call_target="tpu_custom_call" | custom-call | tf_op jit(solution)/shard_map/pallas_call | solution.py:1505

commit v11 on v10

--- a/solution.py
+++ b/solution.py
@@ -20,6 +20,10 @@
 HBM = pl.BlockSpec(memory_space=pl.ANY)
 VMEM = pl.BlockSpec(memory_space=pltpu.VMEM)
 STEPS = ("oR", "oL", "iR", "iL", "dR", "dL", "gRa", "gRb", "gLa", "gLb", "fR", "fL")
+
+
+def gain_row(ref):
+    return ref[...].astype(F32).reshape(1, ref.shape[0])
 
 
 def rows_of(ref, start, count):
@@ -365,7 +369,7 @@
     source = source.astype(F32)
     r = lax.rsqrt(jnp.mean(source * source, axis=1, keepdims=True) + EPSILON)
     n = source * r
-    e = value * gain.astype(F32)
+    e = value * gain
     inner = jnp.mean(e * n, axis=1, keepdims=True)
     return base.astype(F32) + r * (e - n * inner), jnp.sum(value * n, axis=0, keepdims=True)
 
@@ -407,7 +411,7 @@
     for wave in (0, 1):
         for part in (0, 1):
             at, value = ring.collect(own_s, nbr, part, wave)
-            value, more = norm_back(value, source_s[at, :], base_s[at, :], gain_ref[...])
+            value, more = norm_back(value, source_s[at, :], base_s[at, :], gain_row(gain_ref))
             grad_ref[at, :] = value
             sums = sums + more
         tall = ring.tall
@@ -503,7 +507,7 @@
     for wave in (0,):
         for part in (0, 1):
             at, value = ring.collect(own_s, nbr, part, wave)
-            value, more = norm_back(value, source_s[at, :], base_ref[at, :], gain_ref[...])
+            value, more = norm_back(value, source_s[at, :], base_ref[at, :], gain_row(gain_ref))
             mine_s[at, :] = value
             ring.spread(part, wave, mine_s, out_ref)
             sums = sums + more
@@ -687,7 +691,7 @@
     gain2_ref, cot_in, wg_in, wu_in, wd_in,
     low_out, qn_ref, kn_ref, v_ref, sig_ref, att_ref, stat_ref, decay_ref, gated_out, full_out,
     mid_out, normed_out, grad_out, gate_out, up_out, hid_out, mlp_out, sums_ref,
-    top_s, row_s, q_s, k_s, w_s, pre_s, gs, ws, wf_s, bf_s, low_ref, gated_ref, full_ref,
+    top_s, row_s, q_s, k_s, w_s, pre_s, gs, ws, mine, wf_s, bf_s, low_ref, gated_ref, full_ref,
     wg_s, wu_s, wd_s, cot_s, mid_s, normed_s, grad_s, gate_s, up_s, hid_s, mlp_s, osem, *sem,
 ):
     step = pl.program_id(0)
@@ -697,11 +701,10 @@
     me, right, left, far = (lax.rem(here.my + by, Y) for by in (0, 1, 3, 2))
     sibling, right1, left1, right2, left2 = here.peers()
     c, p1, p2, half, quarter = here.c, here.p1, here.p2, seq // 2, seq // Y
-    mine = ws.at[c, p2, p1, me]
     cross_order = (p2, here.l2, here.r2, here.o2)
 
     def plane(j):
-        return link(mine, mine, *sem[2:4], j, (here.dp, (right, far, left)[j]))
+        return link(mine, ws.at[c, p2, p1, 2 - j], *sem[2:4], j, (here.dp, (right, far, left)[j]))
 
     def torus(stage, j):
         if stage == 0:
@@ -709,7 +712,8 @@
         else:
             at, spots, to = (lambda p: ws.at[c, p]), (p2, here.l2, here.r2), (right2, left2)
         spot, part, side = ((0, 0, 0), (0, 1, 0), (0, 0, 1), (0, 1, 1), (1, 0, 0), (2, 1, 1))[j]
-        piece = at(spots[spot]).at[2 * part : 2 * part + 2]
+        cut = (slice(0, 2), slice(2, 4 if stage else 3))[part]
+        piece = at(spots[spot]).at[cut]
         return link(piece, piece, *sem[4 + 2 * stage : 6 + 2 * stage], j, to[side])
 
     def cross(j):
@@ -776,7 +780,7 @@
             at = rows_at(i, 128)
             x = x_ref[at, :].astype(F32)
             r = lax.rsqrt(jnp.mean(x * x, axis=1, keepdims=True) + EPSILON)
-            low_ref[at, :] = (x * r * gain_ref[...].astype(F32)).astype(jnp.bfloat16)
+            low_ref[at, :] = (x * r * gain_row(gain_ref)).astype(jnp.bfloat16)
             return carry
 
         lax.fori_loop(0, seq // 128, norm, 0)
@@ -786,6 +790,10 @@
         wf_s[0:heads, :] = wf_ref[...]
         bf_s[...] = jnp.zeros_like(bf_s)
         bf_s[:, 0:heads] = bf_ref[...].astype(F32)
+        for j in range(3):
+            plane(j).wait_recv()
+        for j in range(4):
+            torus(0, j).start()
         pre = mm_t(wf_s[...], low_ref[...])[0:8] + jnp.broadcast_to(bf_s[...], (PAIR, PAIR)).T[0:8, 0:1]
         fall = jnp.minimum(pre, 0.0) - jnp.log1p(jnp.exp(-jnp.abs(pre)))
         decay = running_sum(fall)
@@ -818,26 +826,11 @@
 
     lax.fori_loop(0, seq // 128, norms, 0)
 
-    @pl.when(step == 0)
-    def _():
-        for j in range(3):
-            plane(j).wait_recv()
-        for j in range(4):
-            torus(0, j).start()
-
     @pl.when(step == 1)
     def _():
-        arrived(lambda j: torus(0, j))
-        for j in range(4):
-            torus(1, j).start()
-        cross(0).start()
         for j in (3, 4, 5):
             flush(j).start()
         come(0).start()
-
-    @pl.when(step == 2)
-    def _():
-        pass_on(lambda j: torus(1, j))
 
     lines = [one_row(row_s, 2 * step + head) for head in (0, 1)]
     first = first_head((128, PAIR))
@@ -872,13 +865,20 @@
             def _():
                 hand_on(step - 1, 0, 4)
 
+            @pl.when(step == 0)
+            def _():
+                pass_on(lambda j: torus(0, j))
+
 
     gate(step, 3).start()
 
     @pl.when(step == 0)
     def _():
         gate(0, 1).start()
-        pass_on(lambda j: torus(0, j))
+        arrived(lambda j: torus(0, j))
+        for j in range(4):
+            torus(1, j).start()
+        cross(0).start()
 
     @pl.when(step > 0)
     def _():
@@ -886,35 +886,39 @@
 
     @pl.when(step == pl.num_programs(0) - 1)
     def _():
+        pairs = gs.shape[0]
+        pass_on(lambda j: torus(1, j))
         torus(1, 1).wait_recv()
         cross(1).start()
         torus(1, 2).wait_recv()
         cross(2).start()
+        hand_on(step, 0, 4)
+        for pair in range(1, pairs):
+            gate(pair, 1).start()
+        hand_on(step, 3, 5)
         torus(1, 4).wait_recv()
         torus(1, 5).wait_recv()
         cross(3).start()
-        hand_on(step, 0, 4)
-        pairs = gs.shape[0]
-        for pair in range(1, pairs):
-            gate(pair, 1).start()
-        hand_on(step, 3, 5)
         for j in range(4):
             cross(j).wait_recv()
         tall, wide, shard = ws.shape[4], ws.shape[5], w_ref.shape[0]
 
+        rows_of(full_ref, me * shard, shard)[...] = w_ref[...]
+
         def turn(k, carry):
-            y, m = k // 8, lax.rem(k, 8)
+            on, m = k // 8, lax.rem(k, 8)
             x, z = m // 2, lax.rem(m, 2) * 2
+            y = lax.rem(me + on + 1, Y)
             rows = pl.ds(pl.multiple_of(y * shard + m * 2 * tall, 16), 2 * tall)
             for h, one, two in (
-                (0, ws[0, z, x, y], ws[0, z + 1, x, y]),
-                (1, ws[1, x, z, y], ws[1, x, z + 1, y]),
+                (0, ws[0, z, x, on], ws[0, z + 1, x, on]),
+                (1, ws[1, x, z, on], ws[1, x, z + 1, on]),
             ):
                 both = jnp.concatenate([one, two], axis=0).astype(jnp.bfloat16)
                 full_ref[rows, h * wide : h * wide + wide] = both
             return carry
 
-        lax.fori_loop(0, 8 * Y, turn, 0)
+        lax.fori_loop(0, 8 * (Y - 1), turn, 0)
         flush(1).start()
         for j in (3, 4, 5):
             flush(j).wait()
@@ -964,7 +968,7 @@
                 at = rows_at(i, 128)
                 mid = mid_s[at, :]
                 r = lax.rsqrt(jnp.mean(mid * mid, axis=1, keepdims=True) + EPSILON)
-                normed_s[at, :] = (mid * r * gain2_ref[...].astype(F32)).astype(jnp.bfloat16)
+                normed_s[at, :] = (mid * r * gain_row(gain2_ref)).astype(jnp.bfloat16)
                 return carry
 
             lax.fori_loop(0, half // 128, norm, 0)
@@ -1020,8 +1024,8 @@
     return local_call(
         forward_kernel,
         heads // PAIR,
-        [whole((seq, width)), whole((1, width))] + [weights] * 4
-        + [whole(wf.shape), whole(bf.shape), whole(w_out.shape), whole((1, width))] + [HBM] * 4,
+        [whole((seq, width)), whole((width,))] + [weights] * 4
+        + [whole(wf.shape), whole(bf.shape), whole(w_out.shape), whole((width,))] + [HBM] * 4,
         [HBM] + [lanes] * 6 + [whole((2, 8, seq))] + [HBM] * 9 + [whole((2, width))],
         [
             struct(seq, width, t=low), struct(seq, heads), struct(seq, heads), struct(seq, heads, t=low),
@@ -1039,7 +1043,8 @@
             pltpu.VMEM((width, 4 * PAIR), low),
             pltpu.VMEM((seq, 4 * PAIR), F32),
             pltpu.VMEM((heads // PAIR, Y, seq, PAIR), F32),
-            pltpu.VMEM((2, 4, 4, Y, heads // 16, width // 2), F32),
+            pltpu.VMEM((2, 4, 4, Y - 1, heads // 16, width // 2), F32),
+            pltpu.VMEM((heads // 16, width // 2), F32),
             pltpu.VMEM((16, width), low),
             pltpu.VMEM((1, PAIR), F32),
             pltpu.VMEM((seq, width), low),
@@ -1523,7 +1528,7 @@
 ):
     x, cotangent = tokens[0], out_cotangent[0]
     heads = w_forget.shape[1]
-    gain_in, gain_mid = gain_attn[None], gain_mlp[None]
+    gain_in, gain_mid = gain_attn, gain_mlp
     weights = (w_query, w_key, w_value, w_outgate, w_forget.T)
     (
         low, qn, kn, value, sig, attended, stat, decay, gated, w_full,

time: 333 us -> 329 us (0.988)
    pallas_call x1, Pallas kernels: 44.5 us -> 48.3 us  [backward_attention(): local_call(backward_kernel, heads // PAIR, [lanes, HBM] + [lanes] * 6 + [...]
    pallas_call x1, Pallas kernels: 75.3 us -> 71.7 us  [forward(): local_call(forward_kernel, heads // PAIR, [whole((seq, width)), whole((wi...]
where the time goes in v11:
time: 329 us
  Pallas kernels  327 us (99%)
    pallas_call x1, Pallas kernels, reduce_input(): pl.pallas_call(functools.partial(input_kernel, pieces, len(grads)), out_s...  95.2 us
    pallas_call x1, Pallas kernels, forward(): local_call(forward_kernel, heads // PAIR, [whole((seq, width)), whole((wi...  71.7 us
    pallas_call x1, Pallas kernels, reduce_middle(): pl.pallas_call(functools.partial(middle_kernel, pieces, len(grads)), out_...  61.8 us
    pallas_call x1, Pallas kernels, backward_attention(): local_call(backward_kernel, heads // PAIR, [lanes, HBM] + [lanes] * 6 + [...  48.3 us
    pallas_call x1, Pallas kernels, mlp_backward(): pl.pallas_call(mlp_backward_kernel, in_specs=[smem] + [HBM] * 10, out_spe...  43 us
    pallas_call x1, Pallas kernels, finish(): pl.pallas_call(finish_kernel, out_shape=[struct(*grad.shape), struct(*lay...  7 us

profile of v11, /device:TPU:0, one launch (start us, length us, event | category | flops | bytes accessed | tf_op | source)
XLA Modules:
  0.0 329.2 jit_solution(234192770365718288)
XLA Ops:
  1.3 71.7 %shard_map.271 = (bf16[768,1536]{1,0:T(8,128)(2,1)}, f32[768,384]{1,0:T(8,128)}, f32[768,384]{1,0:T(8,128)}, bf16[768,384]{1,0:T(8,128)(2,1)}, f32[768,384]{1,0:...) custom-call(s32[1]{0:T(128)S(6)} %copy.31.length_ref, ...), custom_call_target="tpu_custom_call" | custom-call | flops 16999999488 | bytes 60000000 | tf_op jit(solution)/shard_map/pallas_call | solution.py:1024
  73.0 43.0 %shard_map.272 = (f32[768,1536]{1,0:T(8,128)}, f32[1536,1024]{1,0:T(8,128)}, f32[1536,1024]{1,0:T(8,128)}, f32[1536,1024]{1,0:T(8,128)}, f32[192,1536]{1,0:T(8,128)}, /*index=5*/f32[1,1536]{1,0:T(1,128)}) custom-call(s32[1]{0:T(128)S(6)} %copy.31.length_ref, bf16[768,1536]{1,0:T(8,128)(2,1)} %get-tuple-element.68.grad_in.base_ref, ...), custom_call_target="tpu_custom_call" | custom-call | tf_op jit(solution)/shard_map/pallas_call | solution.py:1224
  116.1 61.8 %shard_map.273 = (f32[192,1536]{1,0:T(8,128)}, f32[768,384]{1,0:T(8,128)}, f32[48,2048]{1,0:T(8,128)}, f32[1,1536]{1,0:T(1,128)}) custom-call(f32[768,1536]{1,0:T(8,128)} %get-tuple-element.75.x_ref, f32[768,1536]{1,0:T(8,128)} %get-tuple-element.74.mid_ref.source_ref, bf16[768,1536]{1,0:T(8,128)(2,1)} %get-tuple-element.68.grad_in.base_ref, ...), custom_call_target="tpu_custom_call" | custom-call | tf_op jit(solution)/shard_map/pallas_call | solution.py:453
  177.9 48.3 %shard_map.274 = (f32[768,1536]{1,0:T(8,128)}, f32[1536,1536]{1,0:T(8,128)}, f32[1536,1536]{1,0:T(8,128)}, f32[8,1536]{1,0:T(8,128)}, f32[8,128]{1,0:T(8,128)}, /*index=5*/bf16[768,1536]{1,0:T(8,128)(2,1)}) custom-call(s32[1]{0:T(128)S(6)} %copy.31.length_ref, f32[768,384]{1,0:T(8,128)} %get-tuple-element.79.gg_ref, ...), custom_call_target="tpu_custom_call" | custom-call | flops 14000000000 | bytes 50000000 | tf_op jit(solution)/shard_map/pallas_call | solution.py:1422
  226.9 95.2 %shard_map.275 = (f32[768,1536]{1,0:T(8,128)}, f32[48,384]{1,0:T(8,128)}, f32[48,2560]{1,0:T(8,128)}, f32[16,1536]{1,0:T(8,128)}) custom-call(f32[768,1536]{1,0:T(8,128)} %get-tuple-element.91.x_ref, bf16[768,1536]{1,0:T(8,128)(2,1)} %bitcast.13, f32[192,1536]{1,0:T(8,128)} %get-tuple-element.88.own_ref.base_ref, bf16[1536]{0:T(1024)(128)(2,1)} %gain_ref.5, ...), custom_call_target="tpu_custom_call" | custom-call | tf_op jit(solution)/shard_map/pallas_call | solution.py:574
  322.0 7.0 %shard_map.276 = (f32[768,1536]{1,0:T(8,128)}, bf16[768,1536]{1,0:T(8,128)(2,1)}, f32[48,384]{1,0:T(8,128)}, f32[48,384]{1,0:T(8,128)}, f32[48,384]{1,0:T(8,128)...) custom-call(f32[768,1536]{1,0:T(8,128)} %get-tuple-element.100.grad_, ...), custom_call_target="tpu_custom_call" | custom-call | tf_op jit(solution)/shard_map/pallas_call | solution.py:1510

commit v12 on v11

--- a/solution.py
+++ b/solution.py
@@ -899,27 +899,23 @@
         torus(1, 4).wait_recv()
         torus(1, 5).wait_recv()
         cross(3).start()
-        for j in range(4):
-            cross(j).wait_recv()
         tall, wide, shard = ws.shape[4], ws.shape[5], w_ref.shape[0]
-
         rows_of(full_ref, me * shard, shard)[...] = w_ref[...]
 
-        def turn(k, carry):
-            on, m = k // 8, lax.rem(k, 8)
-            x, z = m // 2, lax.rem(m, 2) * 2
-            y = lax.rem(me + on + 1, Y)
-            rows = pl.ds(pl.multiple_of(y * shard + m * 2 * tall, 16), 2 * tall)
-            for h, one, two in (
-                (0, ws[0, z, x, on], ws[0, z + 1, x, on]),
-                (1, ws[1, x, z, on], ws[1, x, z + 1, on]),
-            ):
-                both = jnp.concatenate([one, two], axis=0).astype(jnp.bfloat16)
+        def turn(h):
+            def piece(k, carry):
+                on, m = k // 8, lax.rem(k, 8)
+                x, z = m // 2, lax.rem(m, 2) * 2
+                rows = rows_at(lax.rem(me + on + 1, Y) * (shard // (2 * tall)) + m, 2 * tall)
+                parts = [ws[h, z + t, x, on] if h == 0 else ws[h, x, z + t, on] for t in (0, 1)]
+                both = jnp.concatenate(parts, axis=0).astype(jnp.bfloat16)
                 full_ref[rows, h * wide : h * wide + wide] = both
-            return carry
-
-        lax.fori_loop(0, 8 * (Y - 1), turn, 0)
-        flush(1).start()
+                return carry
+
+            lax.fori_loop(0, 8 * (Y - 1), piece, 0)
+
+        for h in (0, 1):
+            pl.when(c == h)(functools.partial(turn, h))
         for j in (3, 4, 5):
             flush(j).wait()
         outer, inner = full_ref.shape[1] // 2, wg_s.shape[1] // 2
@@ -951,7 +947,15 @@
             kept = lax.broadcasted_iota(jnp.int32, (half, 1), 0) + chunk * half < length
 
             def project(k):
-                at = columns(k, outer)
+                @pl.when((k == 1) & (chunk == 0))
+                def _():
+                    for j in range(4):
+                        cross(j).wait_recv()
+                    for h in (0, 1):
+                        pl.when(c != h)(functools.partial(turn, h))
+                    flush(1).start()
+
+                at = columns(lax.rem(k + c, 2), outer)
                 branch = mm(gated_ref[rows, :], full_ref[:, at])
                 x = x_ref[rows, at].astype(F32)
                 mid_s[:, at] = x + branch
@@ -1401,9 +1405,11 @@
 
         lax.fori_loop(0, width // 768, tail, 0)
         last = load(back_ref, back_out, osem.at[4])
-        for j in (1, 2, 4, 5):
-            spread(j).wait_recv()
-        out_ref[...] = lay_s[...].astype(low16)
+        for names, owners in (((1, 2), (me, left, right)), ((4, 5), (lax.rem(me + 2, Y),))):
+            for j in names:
+                spread(j).wait_recv()
+            for owner in owners:
+                out_ref[rows_at(owner, q), :] = lay_s[rows_at(owner, q), :].astype(low16)
         for at, done in ((1, 1), (0, 2)):
             for j in (0, 1):
                 flush(j, at, done).wait()

time: 329 us -> 331 us (level)
  no operation moved by 1% of the time
where the time goes in v12:
time: 331 us
  Pallas kernels  329 us (99%)
    pallas_call x1, Pallas kernels, reduce_input(): pl.pallas_call(functools.partial(input_kernel, pieces, len(grads)), out_s...  95.8 us
    pallas_call x1, Pallas kernels, forward(): local_call(forward_kernel, heads // PAIR, [whole((seq, width)), whole((wi...  72.1 us
    pallas_call x1, Pallas kernels, reduce_middle(): pl.pallas_call(functools.partial(middle_kernel, pieces, len(grads)), out_...  63.4 us
    pallas_call x1, Pallas kernels, backward_attention(): local_call(backward_kernel, heads // PAIR, [lanes, HBM] + [lanes] * 6 + [...  46.2 us
    pallas_call x1, Pallas kernels, mlp_backward(): pl.pallas_call(mlp_backward_kernel, in_specs=[smem] + [HBM] * 10, out_spe...  44.2 us
    pallas_call x1, Pallas kernels, finish(): pl.pallas_call(finish_kernel, out_shape=[struct(*grad.shape), struct(*lay...  7 us

profile of v12, /device:TPU:0, one launch (start us, length us, event | category | flops | bytes accessed | tf_op | source)
XLA Modules:
  0.0 331.0 jit_solution(6105445361398781052)
XLA Ops:
  1.3 72.1 %shard_map.271 = (bf16[768,1536]{1,0:T(8,128)(2,1)}, f32[768,384]{1,0:T(8,128)}, f32[768,384]{1,0:T(8,128)}, bf16[768,384]{1,0:T(8,128)(2,1)}, f32[768,384]{1,0:...) custom-call(s32[1]{0:T(128)S(6)} %copy.31.length_ref, ...), custom_call_target="tpu_custom_call" | custom-call | flops 16999999488 | bytes 60000000 | tf_op jit(solution)/shard_map/pallas_call | solution.py:1028
  73.4 44.2 %shard_map.272 = (f32[768,1536]{1,0:T(8,128)}, f32[1536,1024]{1,0:T(8,128)}, f32[1536,1024]{1,0:T(8,128)}, f32[1536,1024]{1,0:T(8,128)}, f32[192,1536]{1,0:T(8,128)}, /*index=5*/f32[1,1536]{1,0:T(1,128)}) custom-call(s32[1]{0:T(128)S(6)} %copy.31.length_ref, bf16[768,1536]{1,0:T(8,128)(2,1)} %get-tuple-element.68.grad_in.base_ref, ...), custom_call_target="tpu_custom_call" | custom-call | tf_op jit(solution)/shard_map/pallas_call | solution.py:1228
  117.7 63.4 %shard_map.273 = (f32[192,1536]{1,0:T(8,128)}, f32[768,384]{1,0:T(8,128)}, f32[48,2048]{1,0:T(8,128)}, f32[1,1536]{1,0:T(1,128)}) custom-call(f32[768,1536]{1,0:T(8,128)} %get-tuple-element.75.x_ref, f32[768,1536]{1,0:T(8,128)} %get-tuple-element.74.mid_ref.source_ref, bf16[768,1536]{1,0:T(8,128)(2,1)} %get-tuple-element.68.grad_in.base_ref, ...), custom_call_target="tpu_custom_call" | custom-call | tf_op jit(solution)/shard_map/pallas_call | solution.py:453
  181.1 46.2 %shard_map.274 = (f32[768,1536]{1,0:T(8,128)}, f32[1536,1536]{1,0:T(8,128)}, f32[1536,1536]{1,0:T(8,128)}, f32[8,1536]{1,0:T(8,128)}, f32[8,128]{1,0:T(8,128)}, /*index=5*/bf16[768,1536]{1,0:T(8,128)(2,1)}) custom-call(s32[1]{0:T(128)S(6)} %copy.31.length_ref, f32[768,384]{1,0:T(8,128)} %get-tuple-element.79.gg_ref, ...), custom_call_target="tpu_custom_call" | custom-call | flops 14000000000 | bytes 50000000 | tf_op jit(solution)/shard_map/pallas_call | solution.py:1428
  228.0 95.8 %shard_map.275 = (f32[768,1536]{1,0:T(8,128)}, f32[48,384]{1,0:T(8,128)}, f32[48,2560]{1,0:T(8,128)}, f32[16,1536]{1,0:T(8,128)}) custom-call(f32[768,1536]{1,0:T(8,128)} %get-tuple-element.91.x_ref, bf16[768,1536]{1,0:T(8,128)(2,1)} %bitcast.13, f32[192,1536]{1,0:T(8,128)} %get-tuple-element.88.own_ref.base_ref, bf16[1536]{0:T(1024)(128)(2,1)} %gain_ref.5, ...), custom_call_target="tpu_custom_call" | custom-call | tf_op jit(solution)/shard_map/pallas_call | solution.py:574
  323.8 7.0 %shard_map.276 = (f32[768,1536]{1,0:T(8,128)}, bf16[768,1536]{1,0:T(8,128)(2,1)}, f32[48,384]{1,0:T(8,128)}, f32[48,384]{1,0:T(8,128)}, f32[48,384]{1,0:T(8,128)...) custom-call(f32[768,1536]{1,0:T(8,128)} %get-tuple-element.100.grad_, ...), custom_call_target="tpu_custom_call" | custom-call | tf_op jit(solution)/shard_map/pallas_call | solution.py:1516
